TPU v7x, 32 devices: a whole 2x2x4 slice. The times are simulated.
32 devices in a mesh: blk: 4 (over y, x), dp: 8 (over z, core).
Axes of the slice: x: 2, y: 2, z: 4, core: 2. Of those that a mesh axis runs over, the one named last changes fastest.
Arguments:
- patches: bfloat16 [4096, 64, 256], P(('blk', 'dp')), may hold values from -6 to 6
- w_mix: bfloat16 [256, 128], replicated, may hold values from -0.375 to 0.375
- w_in: bfloat16 [2048, 512], replicated, may hold values from -0.125 to 0.125
- w_out: bfloat16 [512, 128], replicated, may hold values from -0.25 to 0.25
- partner_dev: int32 [4096], P(('blk', 'dp')), may hold values from 0 to 7, as said below
- partner_row: int32 [4096], P(('blk', 'dp')), may hold values from 0 to 127, as said below
Outputs:
- loss_rows: float32 [4096], P(('blk', 'dp'))
- grad_mix: float32 [256, 128], replicated
- grad_in: float32 [2048, 512], replicated
- grad_out: float32 [512, 128], replicated
Inputs may be any that keep to these rules, and one draw needn't show every extreme that they name: Among one device's rows every dp index appears as partner_dev exactly 128/8 times. Over the rows that share a blk index, the pairs (partner_dev, partner_row) name every pair of dp index and row of a device exactly once.
All inputs are finite; a program needn't handle non-finite values.
Results may differ from a plain program's by a relative error of at most 0.012.
The roundings to bfloat16 on the way count: a program that leaves them out, or rounds other values in their place, can miss the bound.
Values may be sent and summed in bfloat16 or wider, within the bound.
No kernel may reach another device: no remote copies, remote signals or barrier semaphores. Data moves between devices by JAX's collectives and lax.ppermute only.
A program may use at most 64 MiB of HBM per device.

v0:
```python
import math

import jax
import jax.numpy as jnp
from jax import lax
from jax.sharding import PartitionSpec as P

SCALE = 10.0


def dft_table(length, freqs):
    angle_idx = jnp.arange(length, dtype=jnp.int32)
    freq_idx = jnp.arange(freqs, dtype=jnp.int32)
    phase = jnp.mod(freq_idx[None, :] * angle_idx[:, None], length).astype(jnp.float32) * (
        2.0 * math.pi / length
    )
    return jnp.concatenate([jnp.cos(phase), -jnp.sin(phase)], axis=1).astype(jnp.bfloat16)


def encode(block, w_mix, w_in, w_out):
    count, length, lanes = block.shape
    filters = w_mix.shape[1]
    freqs = w_in.shape[0] // filters
    angle_table = dft_table(length, freqs)
    spec = jnp.einsum("pac,ak->pkc", block, angle_table, preferred_element_type=jnp.float32).astype(
        jnp.bfloat16
    )
    mixed = jnp.dot(spec.reshape(-1, lanes), w_mix, preferred_element_type=jnp.float32).reshape(
        count, 2 * freqs, filters
    )
    real_part = mixed[:, :freqs]
    imag_part = mixed[:, freqs:]
    powers = real_part * real_part + imag_part * imag_part
    features = jnp.log1p(powers).reshape(count, -1)
    mean_removed = features - jnp.mean(features, axis=1, keepdims=True)
    reciprocal_scale = lax.rsqrt(
        jnp.mean(mean_removed * mean_removed, axis=1, keepdims=True) + 1e-05
    )
    normed = (mean_removed * reciprocal_scale).astype(jnp.bfloat16)
    preact = jnp.dot(normed, w_in, preferred_element_type=jnp.float32)
    hidden = jax.nn.silu(preact).astype(jnp.bfloat16)
    raw_embed = jnp.dot(hidden, w_out, preferred_element_type=jnp.float32)
    norms = jnp.sqrt(jnp.sum(raw_embed * raw_embed, axis=1, keepdims=True) + 1e-06)
    unit32 = raw_embed / norms
    saved = (
        spec,
        real_part,
        imag_part,
        powers,
        mean_removed,
        reciprocal_scale,
        normed,
        preact,
        hidden,
        unit32,
        norms,
    )
    return (unit32.astype(jnp.bfloat16), saved)


def back_upper(grad_units, saved, w_in, w_out):
    (
        spec,
        real_part,
        imag_part,
        powers,
        mean_removed,
        reciprocal_scale,
        normed,
        preact,
        hidden,
        unit32,
        norms,
    ) = saved
    grad_raw = (
        (grad_units - unit32 * jnp.sum(unit32 * grad_units, axis=1, keepdims=True)) / norms
    ).astype(jnp.bfloat16)
    g_out = jnp.dot(hidden.T, grad_raw, preferred_element_type=jnp.float32)
    grad_hid = jnp.dot(grad_raw, w_out.T, preferred_element_type=jnp.float32)
    sigm = jax.nn.sigmoid(preact)
    grad_pre = (grad_hid * sigm * (1.0 + preact * (1.0 - sigm))).astype(jnp.bfloat16)
    g_in = jnp.dot(normed.T, grad_pre, preferred_element_type=jnp.float32)
    norm_gradient = jnp.dot(grad_pre, w_in.T, preferred_element_type=jnp.float32)
    return (g_in, g_out, norm_gradient)


def back_lower(norm_gradient, saved):
    (
        spec,
        real_part,
        imag_part,
        powers,
        mean_removed,
        reciprocal_scale,
        normed,
        preact,
        hidden,
        unit32,
        norms,
    ) = saved
    lanes = spec.shape[2]
    normalized_input = mean_removed * reciprocal_scale
    feature_gradient = reciprocal_scale * (
        norm_gradient
        - jnp.mean(norm_gradient, axis=1, keepdims=True)
        - normalized_input * jnp.mean(norm_gradient * normalized_input, axis=1, keepdims=True)
    )
    grad_pow = feature_gradient.reshape(powers.shape) / (1.0 + powers)
    grad_mixed = jnp.concatenate(
        [2.0 * real_part * grad_pow, 2.0 * imag_part * grad_pow], axis=1
    ).astype(jnp.bfloat16)
    return jnp.dot(
        spec.reshape(-1, lanes).T,
        grad_mixed.reshape(-1, grad_mixed.shape[2]),
        preferred_element_type=jnp.float32,
    )


def negative_part(units, piece, row_ids):
    scores = SCALE * jnp.dot(units, piece.T, preferred_element_type=jnp.float32)
    column = jnp.arange(piece.shape[0], dtype=jnp.int32)
    expo = jnp.where(column[None, :] == row_ids[:, None], jnp.float32(0.0), jnp.exp(scores))
    return (
        jnp.sum(expo, axis=1),
        jnp.dot(expo.astype(jnp.bfloat16), piece, preferred_element_type=jnp.float32),
    )


def key_part(units, piece, tot_piece, row_ids):
    scores = SCALE * jnp.dot(piece, units.T, preferred_element_type=jnp.float32)
    column = jnp.arange(piece.shape[0], dtype=jnp.int32)
    expo = jnp.where(column[:, None] == row_ids[None, :], jnp.float32(0.0), jnp.exp(scores))
    weights = (expo / tot_piece[:, None]).astype(jnp.bfloat16)
    return jnp.dot(weights.T, piece, preferred_element_type=jnp.float32)


def on_device(patches, w_mix, w_in, w_out, partner_dev, partner_row):
    count = patches.shape[0]
    embed = w_out.shape[1]
    units, saved = encode(patches, w_mix, w_in, w_out)
    peers = lax.axis_size("dp")
    per_peer = count // peers
    sorted_positions = jnp.argsort(partner_dev, stable=True)
    inverse = jnp.argsort(sorted_positions, stable=True)
    wanted = partner_row[sorted_positions].reshape(peers, per_peer)
    asked = lax.all_to_all(wanted, "dp", split_axis=0, concat_axis=0, tiled=True)
    picked = units[asked]
    returned_rows = lax.all_to_all(picked, "dp", split_axis=0, concat_axis=0, tiled=True)
    positive = returned_rows.reshape(count, embed)[inverse]
    spos = SCALE * jnp.sum(units.astype(jnp.float32) * positive.astype(jnp.float32), axis=1)
    row_ids = lax.axis_index("blk") * count + jnp.arange(count, dtype=jnp.int32)
    zpart, npart = negative_part(units, lax.all_gather(units, "blk", axis=0, tiled=True), row_ids)
    totals = jnp.exp(spos) + zpart
    all_totals = lax.all_gather(totals, "blk", axis=0, tiled=True)
    keyterm = key_part(units, lax.all_gather(units, "blk", axis=0, tiled=True), all_totals, row_ids)
    loss_rows = jnp.log(totals) - spos
    coef = SCALE / count
    ppos = jnp.exp(spos) / totals
    partner_grad = coef * (ppos - 1.0)[:, None] * units.astype(jnp.float32)
    outgoing = partner_grad[sorted_positions].reshape(peers, per_peer, embed)
    incoming = lax.all_to_all(outgoing, "dp", split_axis=0, concat_axis=0, tiled=True)
    from_partner = (
        jnp.zeros((count, embed), jnp.float32)
        .at[asked.reshape(-1)]
        .add(incoming.reshape(-1, embed))
    )
    grad_units = (
        coef * ((ppos - 1.0)[:, None] * positive.astype(jnp.float32) + npart / totals[:, None])
        + coef * keyterm
        + from_partner
    )
    g_in, g_out, norm_gradient = back_upper(grad_units, saved, w_in, w_out)
    g_mix = back_lower(norm_gradient, saved)
    g_mix, g_in, g_out = lax.psum((g_mix, g_in, g_out), ("blk", "dp"))
    return (loss_rows, g_mix, g_in, g_out)


def solution(mesh):
    placed = (P(("blk", "dp"), None, None), P(), P(), P(), P(("blk", "dp")), P(("blk", "dp")))
    return jax.shard_map(
        on_device,
        mesh=mesh,
        in_specs=placed,
        out_specs=(P(("blk", "dp")), P(), P(), P()),
        check_vma=False,
    )
```

profile of v0, /device:TPU:0, one launch (start us, length us, event | category | flops | bytes accessed | tf_op | source)
XLA Modules:
  0.0 252.1 jit_solution(4154058484988354202)
XLA Ops:
  7.2 3.3 %sort.31 = (s32[128]{0:T(128)}, s32[128]{0:T(128)S(1)}) sort(s32[128]{0:T(128)} %param.10, s32[128]{0:T(128)S(1)} %iota.30), dimensions={0}, to_apply=%region_3.4 | sort | flops 896 | bytes 2048 | tf_op jit(solution)/shard_map/jit(argsort)/sort | solution.py:143
  10.5 1.6 gather_fusion
  12.8 6.4 %all-to-all-start = ((s32[8,1,16]{2,1,0:T(1,128)}), s32[8,1,16]{2,1,0:T(1,128)S(1)}, u32[]{:S(2)}, u32[]{:S(2)}) async-start(s32[8,1,16]{2,1,0:T(1,128)} %bitcast.4), calls=%async_computation | async-start | bytes 8192 | tf_op jit(solution)/shard_map/all_to_all | solution.py:146
  19.3 2.5 %sort.32 = (s32[128]{0:T(128)}, s32[128]{0:T(128)S(1)}) sort(s32[128]{0:T(128)S(1)} %get-tuple-element.6, s32[128]{0:T(128)S(1)} %iota.31), dimensions={0}, to_apply=%region_4.5 | sort | flops 896 | bytes 2048 | tf_op jit(solution)/shard_map/jit(argsort)/sort | solution.py:144
  21.8 2.9 %convert_bitcast_fusion = bf16[128,32,256]{2,1,0:T(8,128)(2,1)S(1)} fusion(bf16[128,64,256]{2,1,0:T(8,128)(2,1)} %param.6, bf16[64,16]{0,1:T(8,128)(2,1)S(1)} %get-tuple-element.27, bf16[64,16]{0,1:T(8,128)(2,1)S(1)} %get-tuple-element.28), kind=kOutput, calls=%fused_computation.7 | convolution fusion | flops 135274496 | bytes 6295552 | tf_op jit(solution)/shard_map/pac,ak->pkc/dot_general | solution.py:25
  24.8 2.5 fusion
  28.9 1.6 copy.38
  30.5 1.2 multiply_convert_fusion.2
  32.0 8.5 %all_gather.7 = bf16[512,128]{0,1:T(8,128)(2,1)S(1)} all-gather(bf16[128,128]{0,1:T(8,128)(2,1)S(1)} %fusion.35), channel_id=1, replica_groups=mesh['blk'=4,'dp'=8] {'blk'}, dimensions={0}, use_global_device_ids=true | all-gather | bytes 163840 | tf_op jit(solution)/shard_map/all_gather | solution.py:152
  42.9 1.3 gather_fusion.1
  44.2 5.1 %all-to-all-start.1 = ((bf16[8,16,128]{2,1,0:T(8,128)(2,1)}), bf16[8,16,128]{2,1,0:T(8,128)(2,1)S(1)}, u32[]{:S(2)}, u32[]{:S(2)}) async-start(bf16[8,16,128]{2,1,0:T(8,128)(2,1)} %bitcast.6), calls=%async_computation.1 | async-start | bytes 65536 | tf_op jit(solution)/shard_map/all_to_all | solution.py:148
  49.9 5.2 %all-to-all-done.1 = bf16[8,16,128]{2,1,0:T(8,128)(2,1)S(1)} async-done(((bf16[8,16,128]{2,1,0:T(8,128)(2,1)}), bf16[8,16,128]{2,1,0:T(8,128)(2,1)S(1)}, u32[]{:S(2)}, u32[]{:S(2)}) %all-to-all-start.1) | async-done | bytes 32800 | tf_op jit(solution)/shard_map/all_to_all | solution.py:148
  56.4 8.5 %all-gather = f32[4,1,128]{2,1,0:T(1,128)} all-gather(f32[1,1,128]{2,1,0:T(1,128)S(1)} %bitcast.47), channel_id=1, replica_groups=mesh['blk'=4,'dp'=8] {'blk'}, dimensions={0}, use_global_device_ids=true | all-gather | bytes 2560 | tf_op jit(solution)/shard_map/all_gather | solution.py:154
  65.1 1.2 gather_fusion.3
  66.3 3.5 %all-to-all-start.2 = ((f32[8,16,128]{2,1,0:T(8,128)}), f32[8,16,128]{2,1,0:T(8,128)S(1)}, u32[]{:S(2)}, u32[]{:S(2)}) async-start(f32[8,16,128]{2,1,0:T(8,128)} %bitcast.11), calls=%async_computation.2 | async-start | bytes 131072 | tf_op jit(solution)/shard_map/all_to_all | solution.py:161
  69.9 1.2 fusion.13
  71.0 2.0 fusion.12
  73.1 0.9 copy.45
  74.0 1.7 all-to-all-done.2
  75.7 1.5 scatter_fusion
  77.3 1.8 fusion.44
  79.1 1.2 fusion.9
  80.3 0.9 fusion.40
  81.2 2.8 %fusion.36 = f32[2048,512]{1,0:T(8,128)} fusion(bf16[128,512]{1,0:T(8,128)(2,1)S(1)} %fusion.9, f32[128,2048]{1,0:T(8,128)S(1)} %copy.38, f32[128]{0:T(128)S(1)} %add_rsqrt_fusion, f32[128]{0:T(128)S(1)} %broadcast_multiply_fusion.4), kind=kOutput, calls=%fused_computation.91 | convolution fusion | flops 269221888 | bytes 5374976 | tf_op jit(solution)/shard_map/dot_general | solution.py:82
  84.1 1.4 subtract_multiply_fusion
  85.5 1.5 copy.48
  87.0 2.0 multiply_convert_fusion.1
  89.1 1.7 copy.49
  90.8 3.3 %convolution_bitcast_fusion = f32[256,128]{1,0:T(8,128)} fusion(bf16[128,32,256]{2,1,0:T(8,128)(2,1)} %copy-done.3, bf16[128,32,128]{2,1,0:T(8,128)(2,1)} %copy.49), kind=kOutput, calls=%fused_computation.19 | convolution fusion | flops 268435456 | bytes 3276800 | tf_op jit(solution)/shard_map/dot_general | solution.py:112
  95.3 143.0 %all-reduce.3.cloned.1.call-done = (f32[256,128]{1,0:T(8,128)}, f32[2048,512]{1,0:T(8,128)}, f32[512,128]{1,0:T(8,128)}) async-done(((f32[256,128]{1,0:T(8,128)}, f32[2048,512]{1,0:T(8,128)}, f32[512,128]{1,0:T(8,128)}), (f32[256,128]{1,0:T(8,128)}, f32[2048,512]{1,0:T(8,128)}, f32[512,128]{1,0:T(8,128)})) %all-reduce.3.cloned.1.call-update) | async-done | bytes 4587536 | tf_op jit(solution)/shard_map/psum | solution.py:174
  238.3 1.6 copy.60
  239.8 4.7 %copy.61 = f32[2048,512]{1,0:T(8,128)} copy(f32[2048,512]{1,0:T(8,128)} %get-tuple-element.33) | data formatting | bytes 8388608
  (71 shorter events, 9.3 us)
Async XLA Ops:
  7.2 23.3 %copy-start = (bf16[2048,512]{1,0:T(8,128)(2,1)S(1)}, bf16[2048,512]{1,0:T(8,128)(2,1)}, u32[]{:S(2)}) copy-start(bf16[2048,512]{1,0:T(8,128)(2,1)} %param.8) | copy-start | bytes 6291460
  12.8 28.7 %all-to-all-start = ((s32[8,1,16]{2,1,0:T(1,128)}), s32[8,1,16]{2,1,0:T(1,128)S(1)}, u32[]{:S(2)}, u32[]{:S(2)}) async-start(s32[8,1,16]{2,1,0:T(1,128)} %bitcast.4), calls=%async_computation | async-start | bytes 8192 | tf_op jit(solution)/shard_map/all_to_all | solution.py:146
  19.2 21.2 %copy-start.14 = (s32[128]{0:T(128)}, s32[128]{0:T(128)S(1)}, u32[]{:S(2)}) copy-start(s32[128]{0:T(128)S(1)} %iota_add_fusion) | copy-start | bytes 1540
  21.8 2.9 %copy-start.8 = (bf16[256,128]{1,0:T(8,128)(2,1)S(1)}, bf16[256,128]{1,0:T(8,128)(2,1)}, u32[]{:S(2)}) copy-start(bf16[256,128]{1,0:T(8,128)(2,1)} %param.7) | copy-start | bytes 196612
  24.7 2.5 %copy-start.3 = (bf16[128,32,256]{2,1,0:T(8,128)(2,1)}, bf16[128,32,256]{2,1,0:T(8,128)(2,1)S(1)}, u32[]{:S(2)}) copy-start(bf16[128,32,256]{2,1,0:T(8,128)(2,1)S(1)} %convert_bitcast_fusion) | copy-start | bytes 6291460
  27.3 1.3 copy-start.1
  27.8 1.2 copy-start.2
  30.5 1.2 copy-start.5
  31.7 9.7 %copy-start.6 = (bf16[128,512]{1,0:T(8,128)(2,1)}, bf16[128,512]{1,0:T(8,128)(2,1)S(1)}, u32[]{:S(2)}) copy-start(bf16[128,512]{1,0:T(8,128)(2,1)S(1)} %get-tuple-element.20) | copy-start | bytes 393220
  40.5 0.9 copy-start.7
  44.2 10.8 %all-to-all-start.1 = ((bf16[8,16,128]{2,1,0:T(8,128)(2,1)}), bf16[8,16,128]{2,1,0:T(8,128)(2,1)S(1)}, u32[]{:S(2)}, u32[]{:S(2)}) async-start(bf16[8,16,128]{2,1,0:T(8,128)(2,1)} %bitcast.6), calls=%async_computation.1 | async-start | bytes 65536 | tf_op jit(solution)/shard_map/all_to_all | solution.py:148
  55.9 9.1 %copy-start.9 = (f32[128]{0:T(128)}, f32[128]{0:T(128)S(1)}, u32[]{:S(2)}) copy-start(f32[128]{0:T(128)S(1)} %fusion.21) | copy-start | bytes 1540
  56.4 8.6 %copy-start.11 = (f32[128]{0:T(128)}, f32[128]{0:T(128)S(1)}, u32[]{:S(2)}) copy-start(f32[128]{0:T(128)S(1)} %get-tuple-element.15) | copy-start | bytes 1540
  66.3 9.3 %copy-start.13 = (s32[128]{0:T(128)S(1)}, s32[128]{0:T(128)}, u32[]{:S(2)}) copy-start(s32[128]{0:T(128)} %fusion.31) | copy-start | bytes 1540
  66.3 9.3 %all-to-all-start.2 = ((f32[8,16,128]{2,1,0:T(8,128)}), f32[8,16,128]{2,1,0:T(8,128)S(1)}, u32[]{:S(2)}, u32[]{:S(2)}) async-start(f32[8,16,128]{2,1,0:T(8,128)} %bitcast.11), calls=%async_computation.2 | async-start | bytes 131072 | tf_op jit(solution)/shard_map/all_to_all | solution.py:161
  69.8 168.4 %all-reduce.3.cloned.1.call-start = ((), (), s32[]{:S(2)}) async-start(), calls=%async_computation.3 | async-start | bytes 9175040 | tf_op jit(solution)/shard_map/psum | solution.py:174
  94.1 0.7 copy-start.10
  94.1 0.7 copy-start.12
  239.8 4.7 %copy-start.4 = (f32[512,128]{1,0:T(8,128)S(1)}, f32[512,128]{1,0:T(8,128)}, u32[]{:S(2)}) copy-start(f32[512,128]{1,0:T(8,128)} %get-tuple-element.34) | copy-start | bytes 786436
Sparse Core Ops, SparseCore 0:
  94.2 143.9 all-reduce.2
where the time goes:
time: 253 us; the launch traced here: 252 us
  waiting for transfers between devices  150 us (59%)
  matrix products  21 us (8%)
  local copies, waits for them, and re-layouts  20.9 us (8%)
  blocking collectives  17 us (7%)
  starting transfers between devices  15 us (6%)
  between operations  14.3 us (6%)
  other arithmetic  14.1 us (6%)
    psum x1, waiting for transfers between devices, on_device(): g_mix, g_in, g_out = lax.psum((g_mix, g_in, g_out), ('blk', 'dp'))  143 us
    all_gather x1, blocking collectives, on_device(): all_totals = lax.all_gather(totals, 'blk', axis=0, tiled=True)  8.55 us
    unnamed x33, local copies, waits for them, and re-layouts  8.52 us
    all_gather x1, blocking collectives, on_device(): lax.all_gather(units, 'blk', axis=0, tiled=True)  8.46 us
    all_to_all x1, starting transfers between devices, on_device(): lax.all_to_all(wanted, 'dp', split_axis=0, concat_axis=0, tiled=True)  6.35 us
    all_to_all x1, waiting for transfers between devices, on_device(): lax.all_to_all(picked, 'dp', split_axis=0, concat_axis=0, tiled=True)  5.16 us
    all_to_all x1, starting transfers between devices, on_device(): lax.all_to_all(picked, 'dp', split_axis=0, concat_axis=0, tiled=True)  5.09 us
  transfers between devices with their start and end apart: 4, of which 3 were waited for; matrix products, arithmetic and copies ran while one was open for 7% of the time, Pallas kernels for 0%

commit v1 on v0

--- a/solution.py
+++ b/solution.py
@@ -132,6 +132,71 @@
     expo = jnp.where(column[:, None] == row_ids[None, :], jnp.float32(0.0), jnp.exp(scores))
     weights = (expo / tot_piece[:, None]).astype(jnp.bfloat16)
     return jnp.dot(weights.T, piece, preferred_element_type=jnp.float32)
+
+
+def hop_bits(axis):
+    size = lax.axis_size(axis)
+    steps = size.bit_length() - 1
+    assert size == 1 << steps
+    return [1 << step for step in range(steps)]
+
+
+def swap(block, axis, bit):
+    size = lax.axis_size(axis)
+    return lax.ppermute(block, axis, [(src, src ^ bit) for src in range(size)])
+
+
+def side(axis, bit):
+    return (lax.axis_index(axis) & bit) != 0
+
+
+def scatter_sum(part, route):
+    for axis, bit in route:
+        half = part.shape[0] // 2
+        upper = side(axis, bit)
+        low, high = part[:half], part[half:]
+        away = jnp.where(upper, low, high).astype(jnp.bfloat16)
+        kept = jnp.where(upper, high, low)
+        part = kept + swap(away, axis, bit).astype(jnp.float32)
+    return part
+
+
+def gather_back(part, route):
+    for axis, bit in reversed(route):
+        other = swap(part, axis, bit)
+        upper = side(axis, bit)
+        part = jnp.concatenate(
+            [jnp.where(upper, other, part), jnp.where(upper, part, other)], axis=0
+        )
+    return part
+
+
+def reduce_all(g_mix, g_in, g_out):
+    width = g_in.shape[1]
+    pieces = [g_mix.reshape(-1, width), g_out.reshape(-1, width)]
+    small = jnp.concatenate(pieces, axis=0)
+    devices = lax.axis_size("blk") * lax.axis_size("dp")
+    unit = 8 * devices
+    total = -(-(g_in.shape[0] + small.shape[0]) // (2 * unit)) * 2 * unit
+    pad = total - g_in.shape[0] - small.shape[0]
+    whole = jnp.concatenate([g_in, small, jnp.zeros((pad, width), jnp.float32)], axis=0)
+    across = [("blk", bit) for bit in hop_bits("blk")]
+    along = [("dp", bit) for bit in hop_bits("dp")]
+    routes = [along[:1] + across + along[1:], along[:1] + across[::-1] + along[1:]]
+    half = total // 2
+    done = [
+        gather_back(scatter_sum(whole[k * half : (k + 1) * half], route).astype(jnp.bfloat16), route)
+        for k, route in enumerate(routes)
+    ]
+    whole = jnp.concatenate(done, axis=0).astype(jnp.float32)
+    rows = g_in.shape[0]
+    mix_rows = pieces[0].shape[0]
+    out_rows = pieces[1].shape[0]
+    return (
+        whole[rows : rows + mix_rows].reshape(g_mix.shape),
+        whole[:rows],
+        whole[rows + mix_rows : rows + mix_rows + out_rows].reshape(g_out.shape),
+    )
 
 
 def on_device(patches, w_mix, w_in, w_out, partner_dev, partner_row):
@@ -171,7 +236,7 @@
     )
     g_in, g_out, norm_gradient = back_upper(grad_units, saved, w_in, w_out)
     g_mix = back_lower(norm_gradient, saved)
-    g_mix, g_in, g_out = lax.psum((g_mix, g_in, g_out), ("blk", "dp"))
+    g_mix, g_in, g_out = reduce_all(g_mix, g_in, g_out)
     return (loss_rows, g_mix, g_in, g_out)
 
 

time: 253 us -> 169 us (0.67)
  waiting for transfers between devices: 150 us -> 45.2 us
  starting transfers between devices: 15 us -> 31.6 us
  other arithmetic: 14.1 us -> 29.2 us
  between operations: 14.3 us -> 1.26 us
    psum x1 -> x0, waiting for transfers between devices: 143 us -> none  [on_device(): g_mix, g_in, g_out = lax.psum((g_mix, g_in, g_out), ('blk', 'dp'))]
    ppermute x0 -> x20, waiting for transfers between devices: none -> 38.4 us  [swap(): return lax.ppermute(block, axis, [(src, src ^ bit) for src in range(size)])]
    ppermute x0 -> x20, starting transfers between devices: none -> 16.7 us  [swap(): return lax.ppermute(block, axis, [(src, src ^ bit) for src in range(size)])]
    convert_element_type x0 -> x12, other arithmetic: none -> 7.47 us  [the longest x9 4.86 us: scatter_sum(): away = jnp.where(upper, low, high).astype(jnp.bfloat16)]
    unnamed x33 -> x38, local copies, waits for them, and re-layouts: 8.52 us -> 2.84 us
    add x0 -> x7, other arithmetic: none -> 5.14 us  [scatter_sum(): part = kept + swap(away, axis, bit).astype(jnp.float32)]
    slice x0 -> x2, local copies, waits for them, and re-layouts: none -> 4.72 us  [the longest x1 4.64 us: reduce_all(): whole[:rows]]
  transfers between devices with their start and end apart: 4 -> 23, of which waited for: 3 -> 18; matrix products, arithmetic and copies ran while one was open for 7% -> 13% of each run, Pallas kernels for 0% -> 0%
where the time goes in v1:
time: 169 us; the launch traced here: 168 us
  waiting for transfers between devices  45.2 us (27%)
  starting transfers between devices  31.6 us (19%)
  other arithmetic  29.2 us (17%)
  local copies, waits for them, and re-layouts  22.3 us (13%)
  matrix products  21.2 us (13%)
  blocking collectives  17 us (10%)
    ppermute x20, waiting for transfers between devices, swap(): return lax.ppermute(block, axis, [(src, src ^ bit) for src in range(size)])  38.4 us
    ppermute x20, starting transfers between devices, swap(): return lax.ppermute(block, axis, [(src, src ^ bit) for src in range(size)])  16.7 us
    all_gather x1, blocking collectives, on_device(): all_totals = lax.all_gather(totals, 'blk', axis=0, tiled=True)  8.54 us
    all_gather x1, blocking collectives, on_device(): lax.all_gather(units, 'blk', axis=0, tiled=True)  8.46 us
    all_to_all x1, starting transfers between devices, on_device(): lax.all_to_all(wanted, 'dp', split_axis=0, concat_axis=0, tiled=True)  6.35 us
    all_to_all x1, waiting for transfers between devices, on_device(): lax.all_to_all(picked, 'dp', split_axis=0, concat_axis=0, tiled=True)  5.15 us
    add x7, other arithmetic, scatter_sum(): part = kept + swap(away, axis, bit).astype(jnp.float32)  5.14 us
    all_to_all x1, starting transfers between devices, on_device(): lax.all_to_all(picked, 'dp', split_axis=0, concat_axis=0, tiled=True)  5.1 us
  transfers between devices with their start and end apart: 23, of which 18 were waited for; matrix products, arithmetic and copies ran while one was open for 13% of the time, Pallas kernels for 0%

profile of v1, /device:TPU:0, one launch (start us, length us, event | category | flops | bytes accessed | tf_op | source)
XLA Modules:
  0.0 167.8 jit_solution(6626681958586853782)
XLA Ops:
  0.7 3.3 %sort.31 = (s32[128]{0:T(128)}, s32[128]{0:T(128)S(1)}) sort(s32[128]{0:T(128)} %param.10, s32[128]{0:T(128)S(1)} %iota.30), dimensions={0}, to_apply=%region_3.4 | sort | flops 896 | bytes 2048 | tf_op jit(solution)/shard_map/jit(argsort)/sort | solution.py:208
  6.3 6.4 %all-to-all-start = ((s32[8,1,16]{2,1,0:T(1,128)}), s32[8,1,16]{2,1,0:T(1,128)S(1)}, u32[]{:S(2)}, u32[]{:S(2)}) async-start(s32[8,1,16]{2,1,0:T(1,128)} %bitcast.4), calls=%async_computation | async-start | bytes 8192 | tf_op jit(solution)/shard_map/all_to_all | solution.py:211
  12.7 2.5 %sort.32 = (s32[128]{0:T(128)}, s32[128]{0:T(128)S(1)}) sort(s32[128]{0:T(128)S(1)} %get-tuple-element.6, s32[128]{0:T(128)S(1)} %iota.31), dimensions={0}, to_apply=%region_4.5 | sort | flops 896 | bytes 2048 | tf_op jit(solution)/shard_map/jit(argsort)/sort | solution.py:209
  15.3 2.9 %convert_bitcast_fusion = bf16[128,32,256]{2,1,0:T(8,128)(2,1)S(1)} fusion(bf16[128,64,256]{2,1,0:T(8,128)(2,1)} %param.6, bf16[64,16]{0,1:T(8,128)(2,1)S(1)} %get-tuple-element.49, bf16[64,16]{0,1:T(8,128)(2,1)S(1)} %get-tuple-element.50), kind=kOutput, calls=%fused_computation.8 | convolution fusion | flops 135274496 | bytes 6295552 | tf_op jit(solution)/shard_map/pac,ak->pkc/dot_general | solution.py:25
  18.3 2.5 %fusion = f32[128,32,128]{0,2,1:T(8,128)S(1)} fusion(bf16[128,32,256]{2,1,0:T(8,128)(2,1)S(1)} %convert_bitcast_fusion, bf16[256,128]{1,0:T(8,128)(2,1)S(1)} %copy-done.10), kind=kOutput, calls=%fused_computation.6 | convolution fusion | flops 268435456 | bytes 4259840 | tf_op jit(solution)/shard_map/dot_general | solution.py:28
  25.6 8.5 %all_gather.7 = bf16[512,128]{0,1:T(8,128)(2,1)S(1)} all-gather(bf16[128,128]{0,1:T(8,128)(2,1)S(1)} %fusion.36), channel_id=1, replica_groups=mesh['blk'=4,'dp'=8] {'blk'}, dimensions={0}, use_global_device_ids=true | all-gather | bytes 163840 | tf_op jit(solution)/shard_map/all_gather | solution.py:217
  37.7 5.1 %all-to-all-start.1 = ((bf16[8,16,128]{2,1,0:T(8,128)(2,1)}), bf16[8,16,128]{2,1,0:T(8,128)(2,1)S(1)}, u32[]{:S(2)}, u32[]{:S(2)}) async-start(bf16[8,16,128]{2,1,0:T(8,128)(2,1)} %bitcast.6), calls=%async_computation.1 | async-start | bytes 65536 | tf_op jit(solution)/shard_map/all_to_all | solution.py:213
  43.4 5.2 %all-to-all-done.1 = bf16[8,16,128]{2,1,0:T(8,128)(2,1)S(1)} async-done(((bf16[8,16,128]{2,1,0:T(8,128)(2,1)}), bf16[8,16,128]{2,1,0:T(8,128)(2,1)S(1)}, u32[]{:S(2)}, u32[]{:S(2)}) %all-to-all-start.1) | async-done | bytes 32800 | tf_op jit(solution)/shard_map/all_to_all | solution.py:213
  50.0 8.5 %all-gather = f32[4,1,128]{2,1,0:T(1,128)} all-gather(f32[1,1,128]{2,1,0:T(1,128)S(1)} %bitcast.47), channel_id=1, replica_groups=mesh['blk'=4,'dp'=8] {'blk'}, dimensions={0}, use_global_device_ids=true | all-gather | bytes 2560 | tf_op jit(solution)/shard_map/all_gather | solution.py:219
  59.9 3.5 %all-to-all-start.2 = ((f32[8,16,128]{2,1,0:T(8,128)}), f32[8,16,128]{2,1,0:T(8,128)S(1)}, u32[]{:S(2)}, u32[]{:S(2)}) async-start(f32[8,16,128]{2,1,0:T(8,128)} %bitcast.11), calls=%async_computation.2 | async-start | bytes 131072 | tf_op jit(solution)/shard_map/all_to_all | solution.py:226
  64.6 2.0 %fusion.13 = f32[128,128]{0,1:T(8,128)} fusion(f32[128,128]{0,1:T(8,128)S(1)} %fusion.14, bf16[512,128]{0,1:T(8,128)(2,1)} %copy-done.9, bf16[128,128]{0,1:T(8,128)(2,1)S(1)} %fusion.36, f32[512]{0:T(512)} %bitcast.48, s32[128]{0:T(128)} %copy-done.18), kind=kOutput, calls=%fused_computation.30 | convolution fusion | flops 33914880 | bytes 297472 | tf_op jit(solution)/shard_map/dot_general | solution.py:134
  70.9 1.8 %fusion.46 = f32[512,128]{1,0:T(8,128)} fusion(bf16[128,512]{1,0:T(8,128)(2,1)} %copy-done.8, f32[128,128]{0,1:T(8,128)S(1)} %copy.47, f32[128]{0:T(128)S(1)} %multiply_reduce_fusion.2, f32[128]{0:T(128)S(1)} %add_sqrt_fusion, f32[128,128]{0,1:T(8,128)S(1)} %get-tuple-element.45), kind=kOutput, calls=%fused_computation.151 | convolution fusion | flops 16859136 | bytes 525312 | tf_op jit(solution)/shard_map/dot_general | solution.py:78
  73.9 1.8 %fusion.41 = (f32[128]{0:T(128)S(1)}, f32[128]{0:T(128)S(1)}, f32[128,2048]{1,0:T(8,128)}) fusion(f32[128]{0:T(128)S(1)} %copy-done.12, f32[128,2048]{1,0:T(8,128)S(1)} %copy.38, f32[128]{0:T(128)S(1)} %broadcast_multiply_fusion.4, bf16[128,512]{1,0:T(8,128)(2,1)S(1)} %fusion.10, bf16[2048,512]{1,0:T(8,128)(2,1)S(1)} %copy-done), kind=kOutput, calls=%fused_computation.148 | convolution fusion | flops 269745920 | bytes 4327424 | tf_op jit(solution)/shard_map/dot_general | solution.py:83
  75.7 2.8 %fusion.37 = f32[2048,512]{1,0:T(8,128)} fusion(bf16[128,512]{1,0:T(8,128)(2,1)S(1)} %fusion.10, f32[128,2048]{1,0:T(8,128)S(1)} %copy.38, f32[128]{0:T(128)S(1)} %copy-done.12, f32[128]{0:T(128)S(1)} %broadcast_multiply_fusion.4), kind=kOutput, calls=%fused_computation.146 | convolution fusion | flops 269221888 | bytes 5374976 | tf_op jit(solution)/shard_map/dot_general | solution.py:82
  79.6 2.7 %subtract_multiply_fusion = f32[128,2048]{1,0:T(8,128)} fusion(f32[128,2048]{1,0:T(8,128)} %get-tuple-element.48, f32[128,2048]{1,0:T(8,128)S(1)} %copy.38, f32[128]{0:T(128)S(1)} %broadcast_multiply_fusion.2, f32[128]{0:T(128)S(1)} %broadcast_multiply_fusion.3, f32[128]{0:T(128)S(1)} %copy-done.12, f32[128]{0:T(128)S(1)} %broadcast_multiply_fusion.4), kind=kLoop, calls=%fused_computation.37 | loop fusion | flops 1572864 | bytes 3147776 | tf_op jit(solution)/shard_map/mul | solution.py:103
  83.8 2.0 %multiply_convert_fusion.1 = (bf16[128,16,128]{0,2,1:T(8,128)(2,1)S(1)}, bf16[128,16,128]{0,2,1:T(8,128)(2,1)S(1)}) fusion(f32[128,32,128]{0,2,1:T(8,128)} %copy-done.1, f32[128,16,128]{0,2,1:T(8,128)S(1)} %bitcast.43), kind=kLoop, calls=%fused_computation.35 | loop fusion | flops 2883584 | bytes 4194304 | tf_op jit(solution)/shard_map/convert
  87.6 2.6 %convolution_bitcast_fusion = f32[256,128]{1,0:T(8,128)S(1)} fusion(bf16[128,32,256]{2,1,0:T(8,128)(2,1)} %copy-done.3, bf16[128,32,128]{2,1,0:T(8,128)(2,1)} %copy.49), kind=kOutput, calls=%fused_computation.27 | convolution fusion | flops 268435456 | bytes 3276800 | tf_op jit(solution)/shard_map/dot_general | solution.py:112
  90.3 3.9 %select_convert_fusion = (bf16[640,512]{1,0:T(8,128)(2,1)}, f32[640,512]{1,0:T(8,128)}, bf16[640,512]{1,0:T(8,128)(2,1)}) fusion(f32[2048,512]{1,0:T(8,128)} %fusion.37, pred[]{:T(512)S(6)} %ne.21, f32[640]{0:T(1024)S(1)} %pad_slice_fusion, f32[128,512]{1,0:T(8,128)S(1)} %reshape.172, f32[64,512]{1,0:T(8,128)S(1)} %reshape.171), kind=kLoop, calls=%fused_computation.13 | loop fusion | flops 1638400 | bytes 9177601 | tf_op jit(solution)/shard_map/convert_element_type | solution.py:158
  98.2 3.3 %convert_add_fusion.1 = (f32[640,512]{1,0:T(8,128)S(1)}, f32[640,512]{1,0:T(8,128)S(1)}) fusion(bf16[640,512]{1,0:T(8,128)(2,1)} %copy-done.6, f32[2048,512]{1,0:T(8,128)} %fusion.37, pred[]{:T(512)S(6)} %ne.21, bf16[640,512]{1,0:T(8,128)(2,1)} %copy-done.5, f32[640,512]{1,0:T(8,128)} %get-tuple-element.11), kind=kLoop, calls=%fused_computation.14 | loop fusion | flops 1966080 | bytes 9175041 | tf_op jit(solution)/shard_map/add | solution.py:160
  103.6 1.8 %collective-permute-start.1 = (bf16[320,512]{1,0:T(8,128)(2,1)S(1)}, bf16[320,512]{1,0:T(8,128)(2,1)S(1)}, u32[]{:S(2)}, u32[]{:S(2)}) collective-permute-start(bf16[320,512]{1,0:T(8,128)(2,1)S(1)} %select_convert_fusion.3), channel_id=1, source_target_pairs={{0,8},{8,0},{16,24},{24,16},{1,9},{9,1},{17,25},{25,17},{2,10},{10... | collective-permute-start | bytes 983048 | tf_op jit(solution)/shard_map/ppermute | solution.py:146
  105.5 8.3 %collective-permute-done.11 = bf16[320,512]{1,0:T(8,128)(2,1)} collective-permute-done((bf16[320,512]{1,0:T(8,128)(2,1)}, bf16[320,512]{1,0:T(8,128)(2,1)}, u32[]{:S(2)}, u32[]{:S(2)}) %collective-permute-start.11) | collective-permute-done | bytes 327712 | tf_op jit(solution)/shard_map/ppermute | solution.py:146
  117.8 3.5 %collective-permute-done.12 = bf16[160,512]{1,0:T(8,128)(2,1)S(1)} collective-permute-done((bf16[160,512]{1,0:T(8,128)(2,1)S(1)}, bf16[160,512]{1,0:T(8,128)(2,1)S(1)}, u32[]{:S(2)}, u32[]{:S(2)}) %collective-permute-start.12) | collective-permute-done | bytes 163872 | tf_op jit(solution)/shard_map/ppermute | solution.py:146
  123.7 2.2 %collective-permute-done.13 = bf16[80,512]{1,0:T(8,128)(2,1)S(1)} collective-permute-done((bf16[80,512]{1,0:T(8,128)(2,1)S(1)}, bf16[80,512]{1,0:T(8,128)(2,1)S(1)}, u32[]{:S(2)}, u32[]{:S(2)}) %collective-permute-start.13) | collective-permute-done | bytes 81952 | tf_op jit(solution)/shard_map/ppermute | solution.py:146
  127.3 1.9 %collective-permute-start.4 = (bf16[40,512]{1,0:T(8,128)(2,1)S(1)}, bf16[40,512]{1,0:T(8,128)(2,1)S(1)}, u32[]{:S(2)}, u32[]{:S(2)}) collective-permute-start(bf16[40,512]{1,0:T(8,128)(2,1)S(1)} %select_convert_fusion.9), channel_id=1, source_target_pairs={{0,4},{1,5},{2,6},{3,7},{4,0},{5,1},{6,2},{7,3},{8,12},{9,13},{10,... | collective-permute-start | bytes 122888 | tf_op jit(solution)/shard_map/ppermute | solution.py:146
  129.3 2.2 %collective-permute-done.14 = bf16[40,512]{1,0:T(8,128)(2,1)S(1)} collective-permute-done((bf16[40,512]{1,0:T(8,128)(2,1)S(1)}, bf16[40,512]{1,0:T(8,128)(2,1)S(1)}, u32[]{:S(2)}, u32[]{:S(2)}) %collective-permute-start.14) | collective-permute-done | bytes 40992 | tf_op jit(solution)/shard_map/ppermute | solution.py:146
  134.5 2.1 %collective-permute-done.15 = bf16[40,512]{1,0:T(8,128)(2,1)S(1)} collective-permute-done((bf16[40,512]{1,0:T(8,128)(2,1)S(1)}, bf16[40,512]{1,0:T(8,128)(2,1)S(1)}, u32[]{:S(2)}, u32[]{:S(2)}) %collective-permute-start.15) | collective-permute-done | bytes 40992 | tf_op jit(solution)/shard_map/ppermute | solution.py:146
  136.9 1.9 %collective-permute-done.5 = bf16[40,512]{1,0:T(8,128)(2,1)S(1)} collective-permute-done((bf16[40,512]{1,0:T(8,128)(2,1)S(1)}, bf16[40,512]{1,0:T(8,128)(2,1)S(1)}, u32[]{:S(2)}, u32[]{:S(2)}) %collective-permute-start.5) | collective-permute-done | bytes 40992 | tf_op jit(solution)/shard_map/ppermute | solution.py:146
  139.3 1.9 %collective-permute-done.16 = bf16[80,512]{1,0:T(8,128)(2,1)S(1)} collective-permute-done((bf16[80,512]{1,0:T(8,128)(2,1)S(1)}, bf16[80,512]{1,0:T(8,128)(2,1)S(1)}, u32[]{:S(2)}, u32[]{:S(2)}) %collective-permute-start.16) | collective-permute-done | bytes 81952 | tf_op jit(solution)/shard_map/ppermute | solution.py:146
  144.1 4.3 %collective-permute-done.17 = bf16[160,512]{1,0:T(8,128)(2,1)S(1)} collective-permute-done((bf16[160,512]{1,0:T(8,128)(2,1)S(1)}, bf16[160,512]{1,0:T(8,128)(2,1)S(1)}, u32[]{:S(2)}, u32[]{:S(2)}) %collective-permute-start.17) | collective-permute-done | bytes 163872 | tf_op jit(solution)/shard_map/ppermute | solution.py:146
  150.7 4.9 %collective-permute-done.18 = bf16[320,512]{1,0:T(8,128)(2,1)S(1)} collective-permute-done((bf16[320,512]{1,0:T(8,128)(2,1)S(1)}, bf16[320,512]{1,0:T(8,128)(2,1)S(1)}, u32[]{:S(2)}, u32[]{:S(2)}) %collective-permute-start.18) | collective-permute-done | bytes 327712 | tf_op jit(solution)/shard_map/ppermute | solution.py:146
  159.2 2.6 %maximum_convert_fusion = f32[2560,512]{1,0:T(8,128)} fusion(bf16[640,512]{1,0:T(8,128)(2,1)S(1)} %get-tuple-element.25, bf16[640,512]{1,0:T(8,128)(2,1)S(1)} %get-tuple-element.24, bf16[640,512]{1,0:T(8,128)(2,1)S(1)} %get-tuple-element.23, bf16[640,512]{1,0:T(8,128)(2,1)S(1)} %get-tuple-element.22), kind=kLoop, calls=%fused_computation.5 | loop fusion | flops 10485760 | bytes 7864320 | tf_op jit(solution)/shard_map/convert_element_type | solution.py:191
  163.2 4.6 %slice.137 = f32[2048,512]{1,0:T(8,128)} slice(f32[2560,512]{1,0:T(8,128)} %maximum_convert_fusion), slice={[0:2048], [0:512]} | slice | bytes 8388608 | tf_op jit(solution)/shard_map/slice | solution.py:197
  (159 shorter events, 52.9 us)
Async XLA Ops:
  0.6 23.4 %copy-start = (bf16[2048,512]{1,0:T(8,128)(2,1)S(1)}, bf16[2048,512]{1,0:T(8,128)(2,1)}, u32[]{:S(2)}) copy-start(bf16[2048,512]{1,0:T(8,128)(2,1)} %param.8) | copy-start | bytes 6291460
  6.3 28.8 %all-to-all-start = ((s32[8,1,16]{2,1,0:T(1,128)}), s32[8,1,16]{2,1,0:T(1,128)S(1)}, u32[]{:S(2)}, u32[]{:S(2)}) async-start(s32[8,1,16]{2,1,0:T(1,128)} %bitcast.4), calls=%async_computation | async-start | bytes 8192 | tf_op jit(solution)/shard_map/all_to_all | solution.py:211
  12.7 21.3 %copy-start.18 = (s32[128]{0:T(128)}, s32[128]{0:T(128)S(1)}, u32[]{:S(2)}) copy-start(s32[128]{0:T(128)S(1)} %iota_add_fusion) | copy-start | bytes 1540
  15.3 2.9 %copy-start.10 = (bf16[256,128]{1,0:T(8,128)(2,1)S(1)}, bf16[256,128]{1,0:T(8,128)(2,1)}, u32[]{:S(2)}) copy-start(bf16[256,128]{1,0:T(8,128)(2,1)} %param.7) | copy-start | bytes 196612
  22.5 2.8 %copy-start.11 = (f32[128]{0:T(128)}, f32[128]{0:T(128)S(1)}, u32[]{:S(2)}) copy-start(f32[128]{0:T(128)S(1)} %add_rsqrt_fusion) | copy-start | bytes 1540
  25.3 9.7 %copy-start.8 = (bf16[128,512]{1,0:T(8,128)(2,1)}, bf16[128,512]{1,0:T(8,128)(2,1)S(1)}, u32[]{:S(2)}) copy-start(bf16[128,512]{1,0:T(8,128)(2,1)S(1)} %get-tuple-element.42) | copy-start | bytes 393220
  37.7 10.8 %all-to-all-start.1 = ((bf16[8,16,128]{2,1,0:T(8,128)(2,1)}), bf16[8,16,128]{2,1,0:T(8,128)(2,1)S(1)}, u32[]{:S(2)}, u32[]{:S(2)}) async-start(bf16[8,16,128]{2,1,0:T(8,128)(2,1)} %bitcast.6), calls=%async_computation.1 | async-start | bytes 65536 | tf_op jit(solution)/shard_map/all_to_all | solution.py:213
  49.5 9.1 %copy-start.13 = (f32[128]{0:T(128)}, f32[128]{0:T(128)S(1)}, u32[]{:S(2)}) copy-start(f32[128]{0:T(128)S(1)} %fusion.22) | copy-start | bytes 1540
  50.0 8.5 %copy-start.15 = (f32[128]{0:T(128)}, f32[128]{0:T(128)S(1)}, u32[]{:S(2)}) copy-start(f32[128]{0:T(128)S(1)} %get-tuple-element.14) | copy-start | bytes 1540
  59.9 9.3 %copy-start.17 = (s32[128]{0:T(128)S(1)}, s32[128]{0:T(128)}, u32[]{:S(2)}) copy-start(s32[128]{0:T(128)} %fusion.32) | copy-start | bytes 1540
  59.9 9.3 %all-to-all-start.2 = ((f32[8,16,128]{2,1,0:T(8,128)}), f32[8,16,128]{2,1,0:T(8,128)S(1)}, u32[]{:S(2)}, u32[]{:S(2)}) async-start(f32[8,16,128]{2,1,0:T(8,128)} %bitcast.11), calls=%async_computation.2 | async-start | bytes 131072 | tf_op jit(solution)/shard_map/all_to_all | solution.py:226
  66.6 7.3 %copy-start.12 = (f32[128]{0:T(128)S(1)}, f32[128]{0:T(128)}, u32[]{:S(2)}) copy-start(f32[128]{0:T(128)} %copy-done.11) | copy-start | bytes 1540
  94.1 2.3 %collective-permute-start.10 = (bf16[640,512]{1,0:T(8,128)(2,1)}, bf16[640,512]{1,0:T(8,128)(2,1)S(1)}, u32[]{:S(2)}, u32[]{:S(2)}) collective-permute-start(bf16[640,512]{1,0:T(8,128)(2,1)} %get-tuple-element.10), channel_id=1, source_target_pairs={{0,1},{1,0},{2,3},{3,2},{4,5},{5,4},{6,7},{7,6},{8,9},{9,8},{10,11... | collective-permute-start | bytes 1966088 | tf_op jit(solution)/shard_map/ppermute | solution.py:146
  94.1 3.2 %collective-permute-start = (bf16[640,512]{1,0:T(8,128)(2,1)}, bf16[640,512]{1,0:T(8,128)(2,1)S(1)}, u32[]{:S(2)}, u32[]{:S(2)}) collective-permute-start(bf16[640,512]{1,0:T(8,128)(2,1)} %get-tuple-element.19), channel_id=1, source_target_pairs={{0,1},{1,0},{2,3},{3,2},{4,5},{5,4},{6,7},{7,6},{8,9},{9,8},{10,11... | collective-permute-start | bytes 1966088 | tf_op jit(solution)/shard_map/ppermute | solution.py:146
  103.3 10.5 %collective-permute-start.11 = (bf16[320,512]{1,0:T(8,128)(2,1)}, bf16[320,512]{1,0:T(8,128)(2,1)}, u32[]{:S(2)}, u32[]{:S(2)}) collective-permute-start(bf16[320,512]{1,0:T(8,128)(2,1)} %select_convert_fusion.2), channel_id=1, source_target_pairs={{0,16},{8,24},{16,0},{24,8},{1,17},{9,25},{17,1},{25,9},{2,18},{10... | collective-permute-start | bytes 983048 | tf_op jit(solution)/shard_map/ppermute | solution.py:146
  103.6 12.1 %collective-permute-start.1 = (bf16[320,512]{1,0:T(8,128)(2,1)S(1)}, bf16[320,512]{1,0:T(8,128)(2,1)S(1)}, u32[]{:S(2)}, u32[]{:S(2)}) collective-permute-start(bf16[320,512]{1,0:T(8,128)(2,1)S(1)} %select_convert_fusion.3), channel_id=1, source_target_pairs={{0,8},{8,0},{16,24},{24,16},{1,9},{9,1},{17,25},{25,17},{2,10},{10... | collective-permute-start | bytes 983048 | tf_op jit(solution)/shard_map/ppermute | solution.py:146
  115.4 5.9 %collective-permute-start.12 = (bf16[160,512]{1,0:T(8,128)(2,1)S(1)}, bf16[160,512]{1,0:T(8,128)(2,1)S(1)}, u32[]{:S(2)}, u32[]{:S(2)}) collective-permute-start(bf16[160,512]{1,0:T(8,128)(2,1)S(1)} %select_convert_fusion.4), channel_id=1, source_target_pairs={{0,8},{8,0},{16,24},{24,16},{1,9},{9,1},{17,25},{25,17},{2,10},{10... | collective-permute-start | bytes 491528 | tf_op jit(solution)/shard_map/ppermute | solution.py:146
  116.0 6.2 %collective-permute-start.2 = (bf16[160,512]{1,0:T(8,128)(2,1)S(1)}, bf16[160,512]{1,0:T(8,128)(2,1)S(1)}, u32[]{:S(2)}, u32[]{:S(2)}) collective-permute-start(bf16[160,512]{1,0:T(8,128)(2,1)S(1)} %select_convert_fusion.5), channel_id=1, source_target_pairs={{0,16},{8,24},{16,0},{24,8},{1,17},{9,25},{17,1},{25,9},{2,18},{10... | collective-permute-start | bytes 491528 | tf_op jit(solution)/shard_map/ppermute | solution.py:146
  121.4 4.5 %collective-permute-start.13 = (bf16[80,512]{1,0:T(8,128)(2,1)S(1)}, bf16[80,512]{1,0:T(8,128)(2,1)S(1)}, u32[]{:S(2)}, u32[]{:S(2)}) collective-permute-start(bf16[80,512]{1,0:T(8,128)(2,1)S(1)} %select_convert_fusion.6), channel_id=1, source_target_pairs={{0,2},{1,3},{2,0},{3,1},{4,6},{5,7},{6,4},{7,5},{8,10},{9,11},{10,... | collective-permute-start | bytes 245768 | tf_op jit(solution)/shard_map/ppermute | solution.py:146
  122.3 5.0 %collective-permute-start.3 = (bf16[80,512]{1,0:T(8,128)(2,1)S(1)}, bf16[80,512]{1,0:T(8,128)(2,1)S(1)}, u32[]{:S(2)}, u32[]{:S(2)}) collective-permute-start(bf16[80,512]{1,0:T(8,128)(2,1)S(1)} %select_convert_fusion.7), channel_id=1, source_target_pairs={{0,2},{1,3},{2,0},{3,1},{4,6},{5,7},{6,4},{7,5},{8,10},{9,11},{10,... | collective-permute-start | bytes 245768 | tf_op jit(solution)/shard_map/ppermute | solution.py:146
  126.0 5.4 %collective-permute-start.14 = (bf16[40,512]{1,0:T(8,128)(2,1)S(1)}, bf16[40,512]{1,0:T(8,128)(2,1)S(1)}, u32[]{:S(2)}, u32[]{:S(2)}) collective-permute-start(bf16[40,512]{1,0:T(8,128)(2,1)S(1)} %select_convert_fusion.8), channel_id=1, source_target_pairs={{0,4},{1,5},{2,6},{3,7},{4,0},{5,1},{6,2},{7,3},{8,12},{9,13},{10,... | collective-permute-start | bytes 122888 | tf_op jit(solution)/shard_map/ppermute | solution.py:146
  127.3 6.0 %collective-permute-start.4 = (bf16[40,512]{1,0:T(8,128)(2,1)S(1)}, bf16[40,512]{1,0:T(8,128)(2,1)S(1)}, u32[]{:S(2)}, u32[]{:S(2)}) collective-permute-start(bf16[40,512]{1,0:T(8,128)(2,1)S(1)} %select_convert_fusion.9), channel_id=1, source_target_pairs={{0,4},{1,5},{2,6},{3,7},{4,0},{5,1},{6,2},{7,3},{8,12},{9,13},{10,... | collective-permute-start | bytes 122888 | tf_op jit(solution)/shard_map/ppermute | solution.py:146
  131.4 5.2 %collective-permute-start.15 = (bf16[40,512]{1,0:T(8,128)(2,1)S(1)}, bf16[40,512]{1,0:T(8,128)(2,1)S(1)}, u32[]{:S(2)}, u32[]{:S(2)}) collective-permute-start(bf16[40,512]{1,0:T(8,128)(2,1)S(1)} %add_convert_fusion), channel_id=1, source_target_pairs={{0,4},{1,5},{2,6},{3,7},{4,0},{5,1},{6,2},{7,3},{8,12},{9,13},{10,... | collective-permute-start | bytes 122888 | tf_op jit(solution)/shard_map/ppermute | solution.py:146
  133.4 5.4 %collective-permute-start.5 = (bf16[40,512]{1,0:T(8,128)(2,1)S(1)}, bf16[40,512]{1,0:T(8,128)(2,1)S(1)}, u32[]{:S(2)}, u32[]{:S(2)}) collective-permute-start(bf16[40,512]{1,0:T(8,128)(2,1)S(1)} %add_convert_fusion.1), channel_id=1, source_target_pairs={{0,4},{1,5},{2,6},{3,7},{4,0},{5,1},{6,2},{7,3},{8,12},{9,13},{10,... | collective-permute-start | bytes 122888 | tf_op jit(solution)/shard_map/ppermute | solution.py:146
  136.7 4.5 %collective-permute-start.16 = (bf16[80,512]{1,0:T(8,128)(2,1)S(1)}, bf16[80,512]{1,0:T(8,128)(2,1)S(1)}, u32[]{:S(2)}, u32[]{:S(2)}) collective-permute-start(bf16[80,512]{1,0:T(8,128)(2,1)S(1)} %pad_maximum_fusion.10), channel_id=1, source_target_pairs={{0,2},{1,3},{2,0},{3,1},{4,6},{5,7},{6,4},{7,5},{8,10},{9,11},{10,... | collective-permute-start | bytes 245768 | tf_op jit(solution)/shard_map/ppermute | solution.py:146
  138.8 4.5 %collective-permute-start.6 = (bf16[80,512]{1,0:T(8,128)(2,1)S(1)}, bf16[80,512]{1,0:T(8,128)(2,1)S(1)}, u32[]{:S(2)}, u32[]{:S(2)}) collective-permute-start(bf16[80,512]{1,0:T(8,128)(2,1)S(1)} %pad_maximum_fusion.9), channel_id=1, source_target_pairs={{0,2},{1,3},{2,0},{3,1},{4,6},{5,7},{6,4},{7,5},{8,10},{9,11},{10,... | collective-permute-start | bytes 245768 | tf_op jit(solution)/shard_map/ppermute | solution.py:146
  141.2 7.1 %collective-permute-start.17 = (bf16[160,512]{1,0:T(8,128)(2,1)S(1)}, bf16[160,512]{1,0:T(8,128)(2,1)S(1)}, u32[]{:S(2)}, u32[]{:S(2)}) collective-permute-start(bf16[160,512]{1,0:T(8,128)(2,1)S(1)} %pad_maximum_fusion.8), channel_id=1, source_target_pairs={{0,8},{8,0},{16,24},{24,16},{1,9},{9,1},{17,25},{25,17},{2,10},{10... | collective-permute-start | bytes 491528 | tf_op jit(solution)/shard_map/ppermute | solution.py:146
  143.4 5.8 %collective-permute-start.7 = (bf16[160,512]{1,0:T(8,128)(2,1)S(1)}, bf16[160,512]{1,0:T(8,128)(2,1)S(1)}, u32[]{:S(2)}, u32[]{:S(2)}) collective-permute-start(bf16[160,512]{1,0:T(8,128)(2,1)S(1)} %pad_maximum_fusion.7), channel_id=1, source_target_pairs={{0,16},{8,24},{16,0},{24,8},{1,17},{9,25},{17,1},{25,9},{2,18},{10... | collective-permute-start | bytes 491528 | tf_op jit(solution)/shard_map/ppermute | solution.py:146
  148.5 7.1 %collective-permute-start.18 = (bf16[320,512]{1,0:T(8,128)(2,1)S(1)}, bf16[320,512]{1,0:T(8,128)(2,1)S(1)}, u32[]{:S(2)}, u32[]{:S(2)}) collective-permute-start(bf16[320,512]{1,0:T(8,128)(2,1)S(1)} %pad_maximum_fusion.6), channel_id=1, source_target_pairs={{0,16},{8,24},{16,0},{24,8},{1,17},{9,25},{17,1},{25,9},{2,18},{10... | collective-permute-start | bytes 983048 | tf_op jit(solution)/shard_map/ppermute | solution.py:146
  149.3 7.1 %collective-permute-start.8 = (bf16[320,512]{1,0:T(8,128)(2,1)S(1)}, bf16[320,512]{1,0:T(8,128)(2,1)S(1)}, u32[]{:S(2)}, u32[]{:S(2)}) collective-permute-start(bf16[320,512]{1,0:T(8,128)(2,1)S(1)} %pad_maximum_fusion.5), channel_id=1, source_target_pairs={{0,8},{8,0},{16,24},{24,16},{1,9},{9,1},{17,25},{25,17},{2,10},{10... | collective-permute-start | bytes 983048 | tf_op jit(solution)/shard_map/ppermute | solution.py:146
  155.8 2.2 %collective-permute-start.19 = (bf16[640,512]{1,0:T(8,128)(2,1)S(1)}, bf16[640,512]{1,0:T(8,128)(2,1)S(1)}, u32[]{:S(2)}, u32[]{:S(2)}) collective-permute-start(bf16[640,512]{1,0:T(8,128)(2,1)S(1)} %pad_maximum_fusion.4), channel_id=1, source_target_pairs={{0,1},{1,0},{2,3},{3,2},{4,5},{5,4},{6,7},{7,6},{8,9},{9,8},{10,11... | collective-permute-start | bytes 1966088 | tf_op jit(solution)/shard_map/ppermute | solution.py:146
  156.6 2.3 %collective-permute-start.9 = (bf16[640,512]{1,0:T(8,128)(2,1)S(1)}, bf16[640,512]{1,0:T(8,128)(2,1)S(1)}, u32[]{:S(2)}, u32[]{:S(2)}) collective-permute-start(bf16[640,512]{1,0:T(8,128)(2,1)S(1)} %pad_maximum_fusion.3), channel_id=1, source_target_pairs={{0,1},{1,0},{2,3},{3,2},{4,5},{5,4},{6,7},{7,6},{8,9},{9,8},{10,11... | collective-permute-start | bytes 1966088 | tf_op jit(solution)/shard_map/ppermute | solution.py:146
  (10 other events, 11.9 us)

commit v2 on v1

v2 whole, which is shorter than its diff:
```python
import functools
import math

import jax
import jax.numpy as jnp
import numpy as np
from jax import lax
from jax.experimental import pallas as pl
from jax.experimental.pallas import tpu as pltpu
from jax.sharding import PartitionSpec as P

SCALE = 10.0
SUB = 8
BF16 = jnp.bfloat16
F32 = jnp.float32
VMEM = pl.BlockSpec(memory_space=pltpu.VMEM)
ANY = pl.BlockSpec(memory_space=pl.ANY)


def shape(dims, dtype):
    return jax.ShapeDtypeStruct(tuple(dims), dtype)


def mm(left, right):
    return jnp.dot(left, right, preferred_element_type=F32)


def mm_nt(left, right):
    return lax.dot_general(left, right, (((1,), (1,)), ((), ())), preferred_element_type=F32)


def mm_tn(left, right):
    return lax.dot_general(left, right, (((0,), (0,)), ((), ())), preferred_element_type=F32)


def params(mib):
    return pltpu.CompilerParams(vmem_limit_bytes=mib << 20)


def cost(flops, nbytes):
    return pl.CostEstimate(flops=int(flops), bytes_accessed=int(nbytes), transcendentals=0)


def angle_basis(length, freqs):
    phase = np.mod(np.outer(np.arange(freqs), np.arange(length)), length).astype(np.float32)
    phase = phase * np.float32(2.0 * math.pi / length)
    table = np.concatenate([np.cos(phase), -np.sin(phase)], axis=0).astype(np.float32)
    basis = np.einsum("ka,pq->kpqa", table, np.eye(SUB, dtype=np.float32))
    return jnp.asarray(basis.reshape(2 * freqs * SUB, SUB * length), BF16)


def encode_kernel(
    freqs,
    patch_ref,
    basis_ref,
    mix_ref,
    out_w_ref,
    in_hbm,
    spec_ref,
    mixed_ref,
    units_ref,
    unit32_ref,
    norm_ref,
    rscale_ref,
    normed_ref,
    preact_ref,
    hidden_ref,
    feat,
    in_w,
    sem,
):
    step = pl.program_id(0)
    load = pltpu.make_async_copy(in_hbm, in_w, sem)

    @pl.when(step == 0)
    def _():
        load.start()

    per, length, lanes = patch_ref.shape
    groups = per // SUB
    filters = mix_ref.shape[1]
    half = freqs * SUB
    for s in range(groups):
        block = patch_ref[s * SUB : (s + 1) * SUB].reshape(SUB * length, lanes)
        spec = mm(basis_ref[...], block).astype(BF16)
        spec_ref[s] = spec
        mixed = mm(spec, mix_ref[...])
        mixed_ref[s] = mixed
        real_part, imag_part = mixed[:half], mixed[half:]
        piece = jnp.log1p(real_part * real_part + imag_part * imag_part)
        base = pl.multiple_of((step * groups + s) * SUB, SUB)
        for k in range(freqs):
            feat[pl.ds(base, SUB), k * filters : (k + 1) * filters] = piece[
                k * SUB : (k + 1) * SUB
            ]

    @pl.when(step == pl.num_programs(0) - 1)
    def _():
        load.wait()
        features = feat[...]
        removed = features - jnp.mean(features, axis=1, keepdims=True)
        rscale = lax.rsqrt(jnp.mean(removed * removed, axis=1, keepdims=True) + 1e-05)
        normed = (removed * rscale).astype(BF16)
        normed_ref[...] = normed
        rscale_ref[...] = jnp.broadcast_to(rscale, rscale_ref.shape)
        preact = mm(normed, in_w[...])
        preact_ref[...] = preact
        hidden = (preact * jax.nn.sigmoid(preact)).astype(BF16)
        hidden_ref[...] = hidden
        raw = mm(hidden, out_w_ref[...])
        norms = jnp.sqrt(jnp.sum(raw * raw, axis=1, keepdims=True) + 1e-06)
        norm_ref[...] = jnp.broadcast_to(norms, norm_ref.shape)
        unit32 = raw / norms
        unit32_ref[...] = unit32
        units_ref[...] = unit32.astype(BF16)


def encode(patches, w_mix, w_in, w_out):
    count, length, lanes = patches.shape
    filters = w_mix.shape[1]
    feats, width = w_in.shape
    embed = w_out.shape[1]
    freqs = feats // filters
    per = 2 * SUB
    groups = count // SUB
    rows = 2 * freqs * SUB

    def whole(*dims):
        return pl.BlockSpec(dims, lambda i: (0,) * len(dims))

    outs = [
        (shape((groups, rows, lanes), BF16), pl.BlockSpec((per // SUB, rows, lanes), lambda i: (i, 0, 0))),
        (shape((groups, rows, filters), F32), pl.BlockSpec((per // SUB, rows, filters), lambda i: (i, 0, 0))),
        (shape((count, embed), BF16), whole(count, embed)),
        (shape((count, embed), F32), whole(count, embed)),
        (shape((count, 128), F32), whole(count, 128)),
        (shape((count, 128), F32), whole(count, 128)),
        (shape((count, feats), BF16), whole(count, feats)),
        (shape((count, width), F32), whole(count, width)),
        (shape((count, width), BF16), whole(count, width)),
    ]
    return pl.pallas_call(
        functools.partial(encode_kernel, freqs),
        grid=(count // per,),
        in_specs=[
            pl.BlockSpec((per, length, lanes), lambda i: (i, 0, 0)),
            whole(rows, SUB * length),
            whole(lanes, filters),
            whole(width, embed),
            ANY,
        ],
        out_shape=[each for each, _ in outs],
        out_specs=[spec for _, spec in outs],
        scratch_shapes=[
            pltpu.VMEM((count, feats), F32),
            pltpu.VMEM((feats, width), BF16),
            pltpu.SemaphoreType.DMA,
        ],
        compiler_params=params(24),
        cost_estimate=cost(3e9, 14e6),
    )(patches, angle_basis(length, freqs), w_mix, w_out, w_in)


def negative_kernel(size, *refs):
    pieces, (expo_ref, zneg_ref, numer_ref) = refs[:size], refs[size:]
    units = pieces[0][...]
    count = units.shape[0]
    zneg = numer = None
    for i, piece in enumerate(pieces):
        keys = piece[...]
        expo = jnp.exp(SCALE * mm_nt(units, keys))
        if i == 0:
            row = lax.broadcasted_iota(jnp.int32, expo.shape, 0)
            col = lax.broadcasted_iota(jnp.int32, expo.shape, 1)
            expo = jnp.where(row == col, 0.0, expo)
        expo_ref[:, i * count : (i + 1) * count] = expo
        total = jnp.sum(expo, axis=1, keepdims=True)
        term = mm(expo.astype(BF16), keys)
        zneg = total if zneg is None else zneg + total
        numer = term if numer is None else numer + term
    zneg_ref[...] = jnp.broadcast_to(zneg, zneg_ref.shape)
    numer_ref[...] = numer


def negatives(pieces):
    count, embed = pieces[0].shape
    size = len(pieces)
    return pl.pallas_call(
        functools.partial(negative_kernel, size),
        in_specs=[VMEM] * size,
        out_shape=[
            shape((count, size * count), F32),
            shape((count, 128), F32),
            shape((count, embed), F32),
        ],
        out_specs=[VMEM] * 3,
        compiler_params=params(8),
        cost_estimate=cost(4e8, 1e6),
    )(*pieces)


def as_rows(column, count):
    return jnp.broadcast_to(column, (column.shape[0], count)).T


def positive_kernel(
    dev_ref, row_ref, even_ref, odd_ref, zneg_ref, numer_ref, local_ref, stats_ref, loss_ref
):
    count = dev_ref.shape[1]
    me = lax.axis_index("dp")
    step = dev_ref[...] ^ me
    place = ((step & 1) * even_ref.shape[0] + (step >> 1) * count + row_ref[...]).astype(F32)
    place = jnp.broadcast_to(place, (count, count)).T
    lane = lax.broadcasted_iota(jnp.int32, (count, count), 1).astype(F32)
    positive = None
    blocks = even_ref.shape[0] // count
    for i in range(2 * blocks):
        source = even_ref if i < blocks else odd_ref
        at = (i % blocks) * count
        hit = jnp.where(place - float(i * count) == lane, 1.0, 0.0).astype(BF16)
        term = mm(hit, source[at : at + count, :])
        positive = term if positive is None else positive + term
    units = even_ref[:count, :].astype(F32)
    spos = SCALE * jnp.sum(units * positive, axis=1, keepdims=True)
    top = jnp.exp(spos)
    totals = top + zneg_ref[:, :1]
    less = top / totals - 1.0
    coef = SCALE / count
    local_ref[...] = coef * (less * positive + numer_ref[...] / totals)
    loss_ref[...] = as_rows(jnp.log(totals) - spos, count)[:1]
    stats_ref[...] = jnp.zeros(stats_ref.shape, F32)
    stats_ref[0:1, :] = as_rows(totals, count)[:1]
    stats_ref[1:2, :] = as_rows(coef * less, count)[:1]
    stats_ref[2:3, :] = (dev_ref[...] * count + row_ref[...]).astype(F32)


def positives(partner_dev, partner_row, even, odd, zneg, numer):
    count, embed = numer.shape
    return pl.pallas_call(
        positive_kernel,
        in_specs=[VMEM] * 6,
        out_shape=[shape((count, embed), F32), shape((SUB, count), F32), shape((1, count), F32)],
        out_specs=[VMEM] * 3,
        compiler_params=params(8),
        cost_estimate=cost(4e8, 1e6),
    )(partner_dev.reshape(1, count), partner_row.reshape(1, count), even, odd, zneg, numer)


def upper_kernel(size, *refs):
    pieces, rest = refs[:size], refs[size:]
    stats, rest = rest[:size], rest[size:]
    (
        expo_ref,
        even_ref,
        odd_ref,
        even_stats,
        odd_stats,
        local_ref,
        unit32_ref,
        norm_ref,
        out_w_ref,
        preact_ref,
        pay_ref,
    ) = rest
    count, embed = local_ref.shape
    coef = SCALE / count
    keyterm = None
    for i in range(size):
        expo = expo_ref[:, i * count : (i + 1) * count]
        weights = (expo / stats[i][0:1, :]).astype(BF16)
        term = mm(weights, pieces[i][...])
        keyterm = term if keyterm is None else keyterm + term
    mine = lax.axis_index("dp") * count + lax.broadcasted_iota(jnp.int32, (count, count), 0)
    mine = mine.astype(F32)
    blocks = even_ref.shape[0] // count
    chosen = amount = None
    for i in range(2 * blocks):
        source, table = (even_ref, even_stats) if i < blocks else (odd_ref, odd_stats)
        j = i % blocks
        hit = table[j * SUB + 2 : j * SUB + 3, :] == mine
        share = jnp.where(hit, table[j * SUB + 1 : j * SUB + 2, :], 0.0)
        term = mm(jnp.where(hit, 1.0, 0.0).astype(BF16), source[j * count : (j + 1) * count, :])
        chosen = term if chosen is None else chosen + term
        amount = share if amount is None else amount + share
    back = jnp.sum(amount, axis=1, keepdims=True) * chosen
    grad_units = local_ref[...] + coef * keyterm + back
    unit32 = unit32_ref[...]
    along = jnp.sum(unit32 * grad_units, axis=1, keepdims=True)
    grad_raw = ((grad_units - unit32 * along) / norm_ref[:, :1]).astype(BF16)
    grad_hid = mm_nt(grad_raw, out_w_ref[...])
    preact = preact_ref[...]
    sigm = jax.nn.sigmoid(preact)
    width = preact.shape[1]
    pay_ref[:, :width] = (grad_hid * sigm * (1.0 + preact * (1.0 - sigm))).astype(BF16)
    pay_ref[:, width:] = grad_raw


def upper(pieces, stats, expo, even, odd, even_stats, odd_stats, local, unit32, norms, w_out, preact):
    count, embed = local.shape
    size = len(pieces)
    args = [*pieces, *stats, expo, even, odd, even_stats, odd_stats, local, unit32, norms, w_out, preact]
    return pl.pallas_call(
        functools.partial(upper_kernel, size),
        in_specs=[VMEM] * len(args),
        out_shape=shape((count, preact.shape[1] + embed), BF16),
        out_specs=VMEM,
        compiler_params=params(8),
        cost_estimate=cost(4e8, 2e6),
    )(*args)


def lower_kernel(
    freqs,
    pay_ref,
    normed_ref,
    rscale_ref,
    in_hbm,
    mixed_hbm,
    spec_hbm,
    g_mix_ref,
    in_w,
    mixed,
    spec,
    grad_feat,
    sems,
):
    loads = [
        pltpu.make_async_copy(source, target, sems.at[i])
        for i, (source, target) in enumerate([(in_hbm, in_w), (mixed_hbm, mixed), (spec_hbm, spec)])
    ]
    for each in loads:
        each.start()
    width = in_w.shape[1]
    loads[0].wait()
    grad_norm = mm_nt(pay_ref[:, :width], in_w[...])
    xhat = normed_ref[...].astype(F32)
    mean = jnp.mean(grad_norm, axis=1, keepdims=True)
    slope = jnp.mean(grad_norm * xhat, axis=1, keepdims=True)
    grad_feat[...] = rscale_ref[:, :1] * (grad_norm - mean - xhat * slope)
    loads[1].wait()
    loads[2].wait()
    groups, rows, filters = mixed.shape
    half = freqs * SUB

    def one(g, total):
        real_part, imag_part = mixed[g, :half], mixed[g, half:]
        powers = real_part * real_part + imag_part * imag_part
        base = pl.multiple_of(g * SUB, SUB)
        grads = jnp.concatenate(
            [grad_feat[pl.ds(base, SUB), k * filters : (k + 1) * filters] for k in range(freqs)],
            axis=0,
        )
        share = 2.0 * grads / (1.0 + powers)
        grad_mixed = jnp.concatenate([real_part * share, imag_part * share], axis=0).astype(BF16)
        return total + mm_tn(grad_mixed, spec[g])

    total = lax.fori_loop(0, groups, one, jnp.zeros((filters, spec.shape[2]), F32), unroll=4)
    g_mix_ref[...] = total.T


def lower(pay, normed, rscale, w_in, mixed, spec, freqs):
    count, feats = normed.shape
    groups, rows, filters = mixed.shape
    lanes = spec.shape[2]
    return pl.pallas_call(
        functools.partial(lower_kernel, freqs),
        in_specs=[VMEM] * 3 + [ANY] * 3,
        out_shape=shape((lanes, filters), F32),
        out_specs=VMEM,
        scratch_shapes=[
            pltpu.VMEM(w_in.shape, BF16),
            pltpu.VMEM(mixed.shape, F32),
            pltpu.VMEM(spec.shape, BF16),
            pltpu.VMEM((count, feats), F32),
            pltpu.SemaphoreType.DMA((3,)),
        ],
        compiler_params=params(24),
        cost_estimate=cost(1e9, 7e6),
    )(pay, normed, rscale, w_in, mixed, spec)


def weights_kernel(width, normed_ref, hidden_ref, pay_ref, g_in_ref, g_out_ref):
    grad_pre = pay_ref[:, :width]
    g_in_ref[...] = mm_tn(normed_ref[...], grad_pre)
    g_out_ref[...] = mm_tn(hidden_ref[...], pay_ref[:, width:])


def weight_grads(normed, hidden, pay):
    count, feats = normed.shape
    width = hidden.shape[1]
    embed = pay.shape[1] - width
    return pl.pallas_call(
        functools.partial(weights_kernel, width),
        in_specs=[VMEM] * 3,
        out_shape=[shape((feats, width), F32), shape((width, embed), F32)],
        out_specs=[VMEM] * 2,
        compiler_params=params(24),
        cost_estimate=cost(3e8, 6e6),
    )(normed, hidden, pay)


def hop_bits(axis):
    size = lax.axis_size(axis)
    steps = size.bit_length() - 1
    assert size == 1 << steps
    return [1 << step for step in range(steps)]


def swap(block, axis, bit):
    size = lax.axis_size(axis)
    return lax.ppermute(block, axis, [(src, src ^ bit) for src in range(size)])


def side(axis, bit):
    return (lax.axis_index(axis) & bit) != 0


def scatter_sum(part, route):
    for axis, bit in route:
        half = part.shape[0] // 2
        upper_side = side(axis, bit)
        low, high = part[:half], part[half:]
        away = jnp.where(upper_side, low, high).astype(BF16)
        kept = jnp.where(upper_side, high, low)
        part = kept + swap(away, axis, bit).astype(F32)
    return part


def gather_back(part, route):
    for axis, bit in reversed(route):
        other = swap(part, axis, bit)
        upper_side = side(axis, bit)
        part = jnp.concatenate(
            [jnp.where(upper_side, other, part), jnp.where(upper_side, part, other)], axis=0
        )
    return part


def reduce_all(g_mix, g_in, g_out):
    width = g_in.shape[1]
    pieces = [g_mix.reshape(-1, width), g_out.reshape(-1, width)]
    small = jnp.concatenate(pieces, axis=0)
    devices = lax.axis_size("blk") * lax.axis_size("dp")
    unit = 8 * devices
    total = -(-(g_in.shape[0] + small.shape[0]) // (2 * unit)) * 2 * unit
    pad = total - g_in.shape[0] - small.shape[0]
    whole = jnp.concatenate([g_in, small, jnp.zeros((pad, width), F32)], axis=0)
    across = [("blk", bit) for bit in hop_bits("blk")]
    along = [("dp", bit) for bit in hop_bits("dp")]
    routes = [along[:1] + across + along[1:], along[:1] + across[::-1] + along[1:]]
    half = total // 2
    done = [
        gather_back(scatter_sum(whole[k * half : (k + 1) * half], route).astype(BF16), route)
        for k, route in enumerate(routes)
    ]
    whole = jnp.concatenate(done, axis=0).astype(F32)
    rows = g_in.shape[0]
    mix_rows = pieces[0].shape[0]
    out_rows = pieces[1].shape[0]
    return (
        whole[rows : rows + mix_rows].reshape(g_mix.shape),
        whole[:rows],
        whole[rows + mix_rows : rows + mix_rows + out_rows].reshape(g_out.shape),
    )


def spread(block, axis, hops):
    return [block] + [swap(block, axis, hop) for hop in hops]


def on_device(patches, w_mix, w_in, w_out, partner_dev, partner_row):
    count = patches.shape[0]
    filters = w_mix.shape[1]
    freqs = w_in.shape[0] // filters
    blocks, peers = lax.axis_size("blk"), lax.axis_size("dp")
    assert peers % 2 == 0
    spec, mixed, units, unit32, norms, rscale, normed, preact, hidden = encode(
        patches, w_mix, w_in, w_out
    )
    across, along = range(1, blocks), range(2, peers, 2)
    pieces = spread(units, "blk", across)
    even = jnp.concatenate(spread(units, "dp", along), axis=0)
    odd = swap(even, "dp", 1)
    expo, zneg, numer = negatives(pieces)
    local, stats, loss = positives(partner_dev, partner_row, even, odd, zneg, numer)
    group_stats = spread(stats, "blk", across)
    even_stats = jnp.concatenate(spread(stats, "dp", along), axis=0)
    odd_stats = swap(even_stats, "dp", 1)
    pay = upper(
        pieces, group_stats, expo, even, odd, even_stats, odd_stats, local, unit32, norms, w_out, preact
    )
    g_in, g_out = weight_grads(normed, hidden, pay)
    g_mix = lower(pay, normed, rscale, w_in, mixed, spec, freqs)
    g_mix, g_in, g_out = reduce_all(g_mix, g_in, g_out)
    return (loss.reshape(count), g_mix, g_in, g_out)


def solution(mesh):
    placed = (P(("blk", "dp"), None, None), P(), P(), P(), P(("blk", "dp")), P(("blk", "dp")))
    return jax.shard_map(
        on_device,
        mesh=mesh,
        in_specs=placed,
        out_specs=(P(("blk", "dp")), P(), P(), P()),
        check_vma=False,
    )
```

time: 169 us -> 131 us (0.78)
  matrix products: 21.2 us -> 0 us
  other arithmetic: 29.2 us -> 11.1 us
  blocking collectives: 17 us -> 0 us
  Pallas kernels: 0 us -> 12 us
  starting transfers between devices: 31.6 us -> 43.3 us
  waiting for transfers between devices: 45.2 us -> 37.9 us
  local copies, waits for them, and re-layouts: 22.3 us -> 25.3 us
    ppermute x20 -> x34, starting transfers between devices: 16.7 us -> 43.3 us  [swap(): return lax.ppermute(block, axis, [(src, src ^ bit) for src in range(size)])]
    dot_general x12 -> x0, matrix products: 21.2 us -> none  [the longest x1 2.93 us: encode(): jnp.einsum('pac,ak->pkc', block, angle_table, preferred_element_type=jnp....]
    all_gather x2 -> x0, blocking collectives: 17 us -> none  [the longest x1 8.54 us: on_device(): all_totals = lax.all_gather(totals, 'blk', axis=0, tiled=True)]
    unnamed x38 -> x54, local copies, waits for them, and re-layouts: 2.84 us -> 18.6 us
    all_to_all x3 -> x0, starting transfers between devices: 14.9 us -> none  [the longest x1 6.35 us: on_device(): lax.all_to_all(wanted, 'dp', split_axis=0, concat_axis=0, tiled=True)]
    pallas_call x0 -> x6, Pallas kernels: none -> 12 us  [the longest x1 6.51 us: encode(): pl.pallas_call(functools.partial(encode_kernel, freqs), grid=(count // pe...]
    all_to_all x3 -> x0, waiting for transfers between devices: 6.88 us -> none  [the longest x1 5.15 us: on_device(): lax.all_to_all(picked, 'dp', split_axis=0, concat_axis=0, tiled=True)]
    sort x2 -> x0, other arithmetic: 5.87 us -> none  [the longest x1 3.33 us: on_device(): sorted_positions = jnp.argsort(partner_dev, stable=True)]
  transfers between devices with their start and end apart: 23 -> 34, of which waited for: 18 -> 24; matrix products, arithmetic and copies ran while one was open for 13% -> 2% of each run, Pallas kernels for 0% -> 0%
where the time goes in v2:
time: 131 us
  starting transfers between devices  43.3 us (33%)
  waiting for transfers between devices  37.9 us (29%)
  local copies, waits for them, and re-layouts  25.3 us (19%)
  Pallas kernels  12 us (9%)
  other arithmetic  11.1 us (8%)
    ppermute x34, starting transfers between devices, swap(): return lax.ppermute(block, axis, [(src, src ^ bit) for src in range(size)])  43.3 us
    ppermute x34, waiting for transfers between devices, swap(): return lax.ppermute(block, axis, [(src, src ^ bit) for src in range(size)])  37.9 us
    unnamed x54, local copies, waits for them, and re-layouts  18.6 us
    pallas_call x1, Pallas kernels, encode(): pl.pallas_call(functools.partial(encode_kernel, freqs), grid=(count // pe...  6.51 us
    slice x1, local copies, waits for them, and re-layouts, reduce_all(): whole[:rows]  4.64 us
    convert_element_type x9, other arithmetic, scatter_sum(): away = jnp.where(upper_side, low, high).astype(BF16)  3.73 us
    add x7, other arithmetic, scatter_sum(): part = kept + swap(away, axis, bit).astype(F32)  3.52 us
    pallas_call x1, Pallas kernels, lower(): pl.pallas_call(functools.partial(lower_kernel, freqs), in_specs=[VMEM] *...  2.73 us
  transfers between devices with their start and end apart: 34, of which 24 were waited for; matrix products, arithmetic and copies ran while one was open for 2% of the time, Pallas kernels for 0%

profile of v2, /device:TPU:0, one launch (start us, length us, event | category | flops | bytes accessed | tf_op | source)
XLA Modules:
  0.0 130.8 jit_solution(3131898783934706762)
XLA Ops:
  0.6 1.6 %copy-done.1 = bf16[2048,512]{1,0:T(8,128)(2,1)S(1)} copy-done((bf16[2048,512]{1,0:T(8,128)(2,1)S(1)}, bf16[2048,512]{1,0:T(8,128)(2,1)}, u32[]{:S(2)}) %copy-start.1) | copy-done | bytes 2097176
  2.2 2.2 %copy-done.7 = bf16[128,64,256]{2,1,0:T(8,128)(2,1)S(1)} copy-done((bf16[128,64,256]{2,1,0:T(8,128)(2,1)S(1)}, bf16[128,64,256]{2,1,0:T(8,128)(2,1)}, u32[]{:S(2)}) %copy-start.7) | copy-done | bytes 4194328
  7.1 6.5 %shard_map.102 = (bf16[16,256,256]{2,1,0:T(8,128)(2,1)S(1)}, f32[16,256,128]{2,1,0:T(8,128)S(1)}, bf16[128,128]{1,0:T(8,128)(2,1)S(1)}, f32[128,128]{1,0:T(8,128...) custom-call(bf16[128,64,256]{2,1,0:T(8,128)(2,1)S(1)} %copy-done.7, ...), custom_call_target="tpu_custom_call" | custom-call | flops 3000000000 | bytes 14000000 | tf_op jit(solution)/shard_map/pallas_call | solution.py:142
  15.6 5.1 %collective-permute-start.2 = (bf16[128,128]{1,0:T(8,128)(2,1)S(1)}, bf16[128,128]{1,0:T(8,128)(2,1)S(1)}, u32[]{:S(2)}, u32[]{:S(2)}) collective-permute-start(bf16[128,128]{1,0:T(8,128)(2,1)S(1)} %get-tuple-element.21.refs_0_), channel_id=1, source_target_pairs={{0,6},{1,7},{2,4},{3,5},{4,2},{5,3},{6,0},{7,1},{8,14},{9,15},{10,... | collective-permute-start | bytes 98312 | tf_op jit(solution)/shard_map/ppermute | solution.py:411
  21.4 3.3 %collective-permute-done = bf16[128,128]{1,0:T(8,128)(2,1)S(1)} collective-permute-done((bf16[128,128]{1,0:T(8,128)(2,1)S(1)}, bf16[128,128]{1,0:T(8,128)(2,1)S(1)}, u32[]{:S(2)}, u32[]{:S(2)}) %collective-permute-start) | collective-permute-done | bytes 32800 | tf_op jit(solution)/shard_map/ppermute | solution.py:411
  25.7 2.5 %collective-permute-start.6 = (bf16[128,128]{1,0:T(8,128)(2,1)S(1)}, bf16[128,128]{1,0:T(8,128)(2,1)S(1)}, u32[]{:S(2)}, u32[]{:S(2)}) collective-permute-start(bf16[128,128]{1,0:T(8,128)(2,1)S(1)} %get-tuple-element.21.refs_0_), channel_id=1, source_target_pairs={{0,24},{8,16},{16,8},{24,0},{1,25},{9,17},{17,9},{25,1},{2,26},{10... | collective-permute-start | bytes 98312 | tf_op jit(solution)/shard_map/ppermute | solution.py:411
  30.6 1.5 %collective-permute-done.5.refs_2_ = bf16[128,128]{1,0:T(8,128)(2,1)S(1)} collective-permute-done((bf16[128,128]{1,0:T(8,128)(2,1)S(1)}, bf16[128,128]{1,0:T(8,128)(2,1)S(1)}, u32[]{:S(2)}, u32[]{:S(2)}) %collective-permute-start.5) | collective-permute-done | bytes 32800 | tf_op jit(solution)/shard_map/ppermute | solution.py:411
  37.5 2.3 %collective-permute-start.10 = (f32[8,128]{1,0:T(8,128)S(1)}, f32[8,128]{1,0:T(8,128)S(1)}, u32[]{:S(2)}, u32[]{:S(2)}) collective-permute-start(f32[8,128]{1,0:T(8,128)S(1)} %get-tuple-element.27.refs_4_), channel_id=1, source_target_pairs={{0,2},{1,3},{2,0},{3,1},{4,6},{5,7},{6,4},{7,5},{8,10},{9,11},{10,... | collective-permute-start | bytes 12296 | tf_op jit(solution)/shard_map/ppermute | solution.py:411
  48.8 1.6 %copy-done.4 = bf16[16,256,256]{2,1,0:T(8,128)(2,1)S(1)} copy-done((bf16[16,256,256]{2,1,0:T(8,128)(2,1)S(1)}, bf16[16,256,256]{2,1,0:T(8,128)(2,1)}, u32[]{:S(2)}) %copy-start.4) | copy-done | bytes 2097176
  50.4 1.6 %copy-done.6 = f32[16,256,128]{2,1,0:T(8,128)S(1)} copy-done((f32[16,256,128]{2,1,0:T(8,128)S(1)}, f32[16,256,128]{2,1,0:T(8,128)}, u32[]{:S(2)}) %copy-start.6) | copy-done | bytes 2097176
  52.0 2.7 %shard_map.107 = f32[256,128]{1,0:T(8,128)S(1)} custom-call(bf16[128,640]{1,0:T(8,128)(2,1)S(1)} %shard_map.105.pay_ref, bf16[128,2048]{1,0:T(8,128)(2,1)S(1)} %get-tuple-element.25.normed_ref, f32[128,128]{1,0:T(8,128)S(1)} %get-tuple-element.34.rscale_ref, bf16[2048,512]{1,0:T(8,128)(2,1)S(1)} %copy-done.2, f32[16,256,128]{2,1,0:T(8,128)S(1)} %copy-done.6, ...), custom_call_target="tpu_custom_call" | custom-call | flops 1000000000 | bytes 7000000 | tf_op jit(solution)/shard_map/pallas_call | solution.py:365
  55.5 2.0 %copy-done = f32[2048,512]{1,0:T(8,128)} copy-done((f32[2048,512]{1,0:T(8,128)}, f32[2048,512]{1,0:T(8,128)S(1)}, u32[]{:S(2)}) %copy-start) | copy-done | bytes 4194328
  57.6 3.5 %select_convert_fusion = (bf16[640,512]{1,0:T(8,128)(2,1)S(1)}, f32[640,512]{1,0:T(8,128)}, bf16[640,512]{1,0:T(8,128)(2,1)S(1)}) fusion(f32[2048,512]{1,0:T(8,128)} %copy-done, pred[]{:T(512)S(6)} %ne.10, f32[640]{0:T(1024)S(1)} %copy-done.23, f32[128,512]{1,0:T(8,128)S(1)} %reshape.33, f32[64,512]{1,0:T(8,128)S(1)} %reshape.32), kind=kLoop, calls=%fused_computation.5 | loop fusion | flops 1638400 | bytes 9177601 | tf_op jit(solution)/shard_map/convert_element_type | solution.py:423
  61.6 1.6 %collective-permute-done.24 = bf16[640,512]{1,0:T(8,128)(2,1)S(1)} collective-permute-done((bf16[640,512]{1,0:T(8,128)(2,1)S(1)}, bf16[640,512]{1,0:T(8,128)(2,1)S(1)}, u32[]{:S(2)}, u32[]{:S(2)}) %collective-permute-start.24) | collective-permute-done | bytes 655392 | tf_op jit(solution)/shard_map/ppermute | solution.py:411
  64.9 3.0 %convert_add_fusion.1 = (f32[640,512]{1,0:T(8,128)S(1)}, f32[640,512]{1,0:T(8,128)S(1)}) fusion(bf16[640,512]{1,0:T(8,128)(2,1)} %copy-done.22, f32[2048,512]{1,0:T(8,128)} %copy-done, pred[]{:T(512)S(6)} %ne.10, bf16[640,512]{1,0:T(8,128)(2,1)S(1)} %collective-permute-done.24, f32[640,512]{1,0:T(8,128)} %get-tuple-element.39), kind=kLoop, calls=%fused_computation.6 | loop fusion | flops 1966080 | bytes 9175041 | tf_op jit(solution)/shard_map/add | solution.py:425
  68.0 1.6 %collective-permute-start.25 = (bf16[320,512]{1,0:T(8,128)(2,1)S(1)}, bf16[320,512]{1,0:T(8,128)(2,1)S(1)}, u32[]{:S(2)}, u32[]{:S(2)}) collective-permute-start(bf16[320,512]{1,0:T(8,128)(2,1)S(1)} %select_convert_fusion.2), channel_id=1, source_target_pairs={{0,16},{8,24},{16,0},{24,8},{1,17},{9,25},{17,1},{25,9},{2,18},{10... | collective-permute-start | bytes 983048 | tf_op jit(solution)/shard_map/ppermute | solution.py:411
  69.7 1.5 %collective-permute-start.15 = (bf16[320,512]{1,0:T(8,128)(2,1)S(1)}, bf16[320,512]{1,0:T(8,128)(2,1)S(1)}, u32[]{:S(2)}, u32[]{:S(2)}) collective-permute-start(bf16[320,512]{1,0:T(8,128)(2,1)S(1)} %select_convert_fusion.3), channel_id=1, source_target_pairs={{0,8},{8,0},{16,24},{24,16},{1,9},{9,1},{17,25},{25,17},{2,10},{10... | collective-permute-start | bytes 983048 | tf_op jit(solution)/shard_map/ppermute | solution.py:411
  71.2 7.0 %collective-permute-done.25 = bf16[320,512]{1,0:T(8,128)(2,1)S(1)} collective-permute-done((bf16[320,512]{1,0:T(8,128)(2,1)S(1)}, bf16[320,512]{1,0:T(8,128)(2,1)S(1)}, u32[]{:S(2)}, u32[]{:S(2)}) %collective-permute-start.25) | collective-permute-done | bytes 327712 | tf_op jit(solution)/shard_map/ppermute | solution.py:411
  80.2 1.6 %collective-permute-start.16 = (bf16[160,512]{1,0:T(8,128)(2,1)S(1)}, bf16[160,512]{1,0:T(8,128)(2,1)S(1)}, u32[]{:S(2)}, u32[]{:S(2)}) collective-permute-start(bf16[160,512]{1,0:T(8,128)(2,1)S(1)} %select_convert_fusion.5), channel_id=1, source_target_pairs={{0,16},{8,24},{16,0},{24,8},{1,17},{9,25},{17,1},{25,9},{2,18},{10... | collective-permute-start | bytes 491528 | tf_op jit(solution)/shard_map/ppermute | solution.py:411
  81.8 2.5 %collective-permute-done.26 = bf16[160,512]{1,0:T(8,128)(2,1)S(1)} collective-permute-done((bf16[160,512]{1,0:T(8,128)(2,1)S(1)}, bf16[160,512]{1,0:T(8,128)(2,1)S(1)}, u32[]{:S(2)}, u32[]{:S(2)}) %collective-permute-start.26) | collective-permute-done | bytes 163872 | tf_op jit(solution)/shard_map/ppermute | solution.py:411
  84.4 1.7 %collective-permute-start.27 = (bf16[80,512]{1,0:T(8,128)(2,1)S(1)}, bf16[80,512]{1,0:T(8,128)(2,1)S(1)}, u32[]{:S(2)}, u32[]{:S(2)}) collective-permute-start(bf16[80,512]{1,0:T(8,128)(2,1)S(1)} %select_convert_fusion.6), channel_id=1, source_target_pairs={{0,2},{1,3},{2,0},{3,1},{4,6},{5,7},{6,4},{7,5},{8,10},{9,11},{10,... | collective-permute-start | bytes 245768 | tf_op jit(solution)/shard_map/ppermute | solution.py:411
  87.2 2.0 %collective-permute-done.27 = bf16[80,512]{1,0:T(8,128)(2,1)S(1)} collective-permute-done((bf16[80,512]{1,0:T(8,128)(2,1)S(1)}, bf16[80,512]{1,0:T(8,128)(2,1)S(1)}, u32[]{:S(2)}, u32[]{:S(2)}) %collective-permute-start.27) | collective-permute-done | bytes 81952 | tf_op jit(solution)/shard_map/ppermute | solution.py:411
  92.3 1.9 %collective-permute-done.28 = bf16[40,512]{1,0:T(8,128)(2,1)S(1)} collective-permute-done((bf16[40,512]{1,0:T(8,128)(2,1)S(1)}, bf16[40,512]{1,0:T(8,128)(2,1)S(1)}, u32[]{:S(2)}, u32[]{:S(2)}) %collective-permute-start.28) | collective-permute-done | bytes 40992 | tf_op jit(solution)/shard_map/ppermute | solution.py:411
  94.2 1.6 %collective-permute-start.29 = (bf16[40,512]{1,0:T(8,128)(2,1)S(1)}, bf16[40,512]{1,0:T(8,128)(2,1)S(1)}, u32[]{:S(2)}, u32[]{:S(2)}) collective-permute-start(bf16[40,512]{1,0:T(8,128)(2,1)S(1)} %add_convert_fusion), channel_id=1, source_target_pairs={{0,4},{1,5},{2,6},{3,7},{4,0},{5,1},{6,2},{7,3},{8,12},{9,13},{10,... | collective-permute-start | bytes 122888 | tf_op jit(solution)/shard_map/ppermute | solution.py:411
  103.8 2.2 %collective-permute-start.31 = (bf16[160,512]{1,0:T(8,128)(2,1)S(1)}, bf16[160,512]{1,0:T(8,128)(2,1)S(1)}, u32[]{:S(2)}, u32[]{:S(2)}) collective-permute-start(bf16[160,512]{1,0:T(8,128)(2,1)S(1)} %pad_maximum_fusion.7), channel_id=1, source_target_pairs={{0,8},{8,0},{16,24},{24,16},{1,9},{9,1},{17,25},{25,17},{2,10},{10... | collective-permute-start | bytes 491528 | tf_op jit(solution)/shard_map/ppermute | solution.py:411
  106.0 2.5 %collective-permute-start.21 = (bf16[160,512]{1,0:T(8,128)(2,1)S(1)}, bf16[160,512]{1,0:T(8,128)(2,1)S(1)}, u32[]{:S(2)}, u32[]{:S(2)}) collective-permute-start(bf16[160,512]{1,0:T(8,128)(2,1)S(1)} %pad_maximum_fusion.6), channel_id=1, source_target_pairs={{0,16},{8,24},{16,0},{24,8},{1,17},{9,25},{17,1},{25,9},{2,18},{10... | collective-permute-start | bytes 491528 | tf_op jit(solution)/shard_map/ppermute | solution.py:411
  112.3 1.8 %collective-permute-start.22 = (bf16[320,512]{1,0:T(8,128)(2,1)S(1)}, bf16[320,512]{1,0:T(8,128)(2,1)S(1)}, u32[]{:S(2)}, u32[]{:S(2)}) collective-permute-start(bf16[320,512]{1,0:T(8,128)(2,1)S(1)} %pad_maximum_fusion.4), channel_id=1, source_target_pairs={{0,8},{8,0},{16,24},{24,16},{1,9},{9,1},{17,25},{25,17},{2,10},{10... | collective-permute-start | bytes 983048 | tf_op jit(solution)/shard_map/ppermute | solution.py:411
  114.1 2.9 %collective-permute-done.32 = bf16[320,512]{1,0:T(8,128)(2,1)S(1)} collective-permute-done((bf16[320,512]{1,0:T(8,128)(2,1)S(1)}, bf16[320,512]{1,0:T(8,128)(2,1)S(1)}, u32[]{:S(2)}, u32[]{:S(2)}) %collective-permute-start.32) | collective-permute-done | bytes 327712 | tf_op jit(solution)/shard_map/ppermute | solution.py:411
  117.3 2.1 %collective-permute-done.22 = bf16[320,512]{1,0:T(8,128)(2,1)S(1)} collective-permute-done((bf16[320,512]{1,0:T(8,128)(2,1)S(1)}, bf16[320,512]{1,0:T(8,128)(2,1)S(1)}, u32[]{:S(2)}, u32[]{:S(2)}) %collective-permute-start.22) | collective-permute-done | bytes 327712 | tf_op jit(solution)/shard_map/ppermute | solution.py:411
  120.0 1.8 %collective-permute-done.23 = bf16[640,512]{1,0:T(8,128)(2,1)S(1)} collective-permute-done((bf16[640,512]{1,0:T(8,128)(2,1)S(1)}, bf16[640,512]{1,0:T(8,128)(2,1)S(1)}, u32[]{:S(2)}, u32[]{:S(2)}) %collective-permute-start.23) | collective-permute-done | bytes 655392 | tf_op jit(solution)/shard_map/ppermute | solution.py:411
  122.1 2.6 %maximum_convert_fusion = f32[2560,512]{1,0:T(8,128)} fusion(bf16[640,512]{1,0:T(8,128)(2,1)S(1)} %get-tuple-element.46, bf16[640,512]{1,0:T(8,128)(2,1)S(1)} %get-tuple-element.45, bf16[640,512]{1,0:T(8,128)(2,1)S(1)} %get-tuple-element.44, bf16[640,512]{1,0:T(8,128)(2,1)S(1)} %get-tuple-element.43), kind=kLoop, calls=%fused_computation | loop fusion | flops 10485760 | bytes 7864320 | tf_op jit(solution)/shard_map/convert_element_type | solution.py:456
  126.1 4.6 %slice.116 = f32[2048,512]{1,0:T(8,128)} slice(f32[2560,512]{1,0:T(8,128)} %maximum_convert_fusion), slice={[0:2048], [0:512]} | slice | bytes 8388608 | tf_op jit(solution)/shard_map/slice | solution.py:462
  (144 shorter events, 46.7 us)
Async XLA Ops:
  15.6 10.0 %collective-permute-start.2 = (bf16[128,128]{1,0:T(8,128)(2,1)S(1)}, bf16[128,128]{1,0:T(8,128)(2,1)S(1)}, u32[]{:S(2)}, u32[]{:S(2)}) collective-permute-start(bf16[128,128]{1,0:T(8,128)(2,1)S(1)} %get-tuple-element.21.refs_0_), channel_id=1, source_target_pairs={{0,6},{1,7},{2,4},{3,5},{4,2},{5,3},{6,0},{7,1},{8,14},{9,15},{10,... | collective-permute-start | bytes 98312 | tf_op jit(solution)/shard_map/ppermute | solution.py:411
  20.8 4.8 %collective-permute-start.1 = (bf16[128,128]{1,0:T(8,128)(2,1)S(1)}, bf16[128,128]{1,0:T(8,128)(2,1)S(1)}, u32[]{:S(2)}, u32[]{:S(2)}) collective-permute-start(bf16[128,128]{1,0:T(8,128)(2,1)S(1)} %get-tuple-element.21.refs_0_), channel_id=1, source_target_pairs={{0,4},{1,5},{2,6},{3,7},{4,0},{5,1},{6,2},{7,3},{8,12},{9,13},{10,... | collective-permute-start | bytes 98312 | tf_op jit(solution)/shard_map/ppermute | solution.py:411
  20.8 3.9 %collective-permute-start = (bf16[128,128]{1,0:T(8,128)(2,1)S(1)}, bf16[128,128]{1,0:T(8,128)(2,1)S(1)}, u32[]{:S(2)}, u32[]{:S(2)}) collective-permute-start(bf16[128,128]{1,0:T(8,128)(2,1)S(1)} %get-tuple-element.21.refs_0_), channel_id=1, source_target_pairs={{0,2},{1,3},{2,0},{3,1},{4,6},{5,7},{6,4},{7,5},{8,10},{9,11},{10,... | collective-permute-start | bytes 98312 | tf_op jit(solution)/shard_map/ppermute | solution.py:411
  25.6 8.1 %collective-permute-start.3 = (bf16[512,128]{1,0:T(8,128)(2,1)S(1)}, bf16[512,128]{1,0:T(8,128)(2,1)S(1)}, u32[]{:S(2)}, u32[]{:S(2)}) collective-permute-start(bf16[512,128]{1,0:T(8,128)(2,1)S(1)} %constant_dynamic-update-slice_fusion.even_ref.refs_9_), channel_id=1, source_target_pairs={{0,1},{1,0},{2,3},{3,2},{4,5},{5,4},{6,7},{7,6},{8,9},{9,8},{10,11... | collective-permute-start | bytes 393224 | tf_op jit(solution)/shard_map/ppermute | solution.py:411
  25.7 4.9 %collective-permute-start.6 = (bf16[128,128]{1,0:T(8,128)(2,1)S(1)}, bf16[128,128]{1,0:T(8,128)(2,1)S(1)}, u32[]{:S(2)}, u32[]{:S(2)}) collective-permute-start(bf16[128,128]{1,0:T(8,128)(2,1)S(1)} %get-tuple-element.21.refs_0_), channel_id=1, source_target_pairs={{0,24},{8,16},{16,8},{24,0},{1,25},{9,17},{17,9},{25,1},{2,26},{10... | collective-permute-start | bytes 98312 | tf_op jit(solution)/shard_map/ppermute | solution.py:411
  28.2 3.9 %collective-permute-start.5 = (bf16[128,128]{1,0:T(8,128)(2,1)S(1)}, bf16[128,128]{1,0:T(8,128)(2,1)S(1)}, u32[]{:S(2)}, u32[]{:S(2)}) collective-permute-start(bf16[128,128]{1,0:T(8,128)(2,1)S(1)} %get-tuple-element.21.refs_0_), channel_id=1, source_target_pairs={{0,16},{8,24},{16,0},{24,8},{1,17},{9,25},{17,1},{25,9},{2,18},{10... | collective-permute-start | bytes 98312 | tf_op jit(solution)/shard_map/ppermute | solution.py:411
  28.7 3.9 %collective-permute-start.4 = (bf16[128,128]{1,0:T(8,128)(2,1)S(1)}, bf16[128,128]{1,0:T(8,128)(2,1)S(1)}, u32[]{:S(2)}, u32[]{:S(2)}) collective-permute-start(bf16[128,128]{1,0:T(8,128)(2,1)S(1)} %get-tuple-element.21.refs_0_), channel_id=1, source_target_pairs={{0,8},{8,0},{16,24},{24,16},{1,9},{9,1},{17,25},{25,17},{2,10},{10... | collective-permute-start | bytes 98312 | tf_op jit(solution)/shard_map/ppermute | solution.py:411
  35.5 7.9 %collective-permute-start.12 = (f32[8,128]{1,0:T(8,128)S(1)}, f32[8,128]{1,0:T(8,128)S(1)}, u32[]{:S(2)}, u32[]{:S(2)}) collective-permute-start(f32[8,128]{1,0:T(8,128)S(1)} %get-tuple-element.27.refs_4_), channel_id=1, source_target_pairs={{0,6},{1,7},{2,4},{3,5},{4,2},{5,3},{6,0},{7,1},{8,14},{9,15},{10,... | collective-permute-start | bytes 12296 | tf_op jit(solution)/shard_map/ppermute | solution.py:411
  36.9 6.4 %collective-permute-start.11 = (f32[8,128]{1,0:T(8,128)S(1)}, f32[8,128]{1,0:T(8,128)S(1)}, u32[]{:S(2)}, u32[]{:S(2)}) collective-permute-start(f32[8,128]{1,0:T(8,128)S(1)} %get-tuple-element.27.refs_4_), channel_id=1, source_target_pairs={{0,4},{1,5},{2,6},{3,7},{4,0},{5,1},{6,2},{7,3},{8,12},{9,13},{10,... | collective-permute-start | bytes 12296 | tf_op jit(solution)/shard_map/ppermute | solution.py:411
  37.5 4.3 %collective-permute-start.10 = (f32[8,128]{1,0:T(8,128)S(1)}, f32[8,128]{1,0:T(8,128)S(1)}, u32[]{:S(2)}, u32[]{:S(2)}) collective-permute-start(f32[8,128]{1,0:T(8,128)S(1)} %get-tuple-element.27.refs_4_), channel_id=1, source_target_pairs={{0,2},{1,3},{2,0},{3,1},{4,6},{5,7},{6,4},{7,5},{8,10},{9,11},{10,... | collective-permute-start | bytes 12296 | tf_op jit(solution)/shard_map/ppermute | solution.py:411
  39.8 4.5 %collective-permute-start.9 = (f32[8,128]{1,0:T(8,128)S(1)}, f32[8,128]{1,0:T(8,128)S(1)}, u32[]{:S(2)}, u32[]{:S(2)}) collective-permute-start(f32[8,128]{1,0:T(8,128)S(1)} %get-tuple-element.27.refs_4_), channel_id=1, source_target_pairs={{0,24},{8,16},{16,8},{24,0},{1,25},{9,17},{17,9},{25,1},{2,26},{10... | collective-permute-start | bytes 12296 | tf_op jit(solution)/shard_map/ppermute | solution.py:411
  41.3 3.6 %collective-permute-start.8 = (f32[8,128]{1,0:T(8,128)S(1)}, f32[8,128]{1,0:T(8,128)S(1)}, u32[]{:S(2)}, u32[]{:S(2)}) collective-permute-start(f32[8,128]{1,0:T(8,128)S(1)} %get-tuple-element.27.refs_4_), channel_id=1, source_target_pairs={{0,16},{8,24},{16,0},{24,8},{1,17},{9,25},{17,1},{25,9},{2,18},{10... | collective-permute-start | bytes 12296 | tf_op jit(solution)/shard_map/ppermute | solution.py:411
  41.8 3.6 %collective-permute-start.7 = (f32[8,128]{1,0:T(8,128)S(1)}, f32[8,128]{1,0:T(8,128)S(1)}, u32[]{:S(2)}, u32[]{:S(2)}) collective-permute-start(f32[8,128]{1,0:T(8,128)S(1)} %get-tuple-element.27.refs_4_), channel_id=1, source_target_pairs={{0,8},{8,0},{16,24},{24,16},{1,9},{9,1},{17,25},{25,17},{2,10},{10... | collective-permute-start | bytes 12296 | tf_op jit(solution)/shard_map/ppermute | solution.py:411
  61.1 3.0 %collective-permute-start.14 = (bf16[640,512]{1,0:T(8,128)(2,1)S(1)}, bf16[640,512]{1,0:T(8,128)(2,1)S(1)}, u32[]{:S(2)}, u32[]{:S(2)}) collective-permute-start(bf16[640,512]{1,0:T(8,128)(2,1)S(1)} %get-tuple-element.42), channel_id=1, source_target_pairs={{0,1},{1,0},{2,3},{3,2},{4,5},{5,4},{6,7},{7,6},{8,9},{9,8},{10,11... | collective-permute-start | bytes 1966088 | tf_op jit(solution)/shard_map/ppermute | solution.py:411
  68.0 10.2 %collective-permute-start.25 = (bf16[320,512]{1,0:T(8,128)(2,1)S(1)}, bf16[320,512]{1,0:T(8,128)(2,1)S(1)}, u32[]{:S(2)}, u32[]{:S(2)}) collective-permute-start(bf16[320,512]{1,0:T(8,128)(2,1)S(1)} %select_convert_fusion.2), channel_id=1, source_target_pairs={{0,16},{8,24},{16,0},{24,8},{1,17},{9,25},{17,1},{25,9},{2,18},{10... | collective-permute-start | bytes 983048 | tf_op jit(solution)/shard_map/ppermute | solution.py:411
  69.7 10.3 %collective-permute-start.15 = (bf16[320,512]{1,0:T(8,128)(2,1)S(1)}, bf16[320,512]{1,0:T(8,128)(2,1)S(1)}, u32[]{:S(2)}, u32[]{:S(2)}) collective-permute-start(bf16[320,512]{1,0:T(8,128)(2,1)S(1)} %select_convert_fusion.3), channel_id=1, source_target_pairs={{0,8},{8,0},{16,24},{24,16},{1,9},{9,1},{17,25},{25,17},{2,10},{10... | collective-permute-start | bytes 983048 | tf_op jit(solution)/shard_map/ppermute | solution.py:411
  78.5 5.8 %collective-permute-start.26 = (bf16[160,512]{1,0:T(8,128)(2,1)S(1)}, bf16[160,512]{1,0:T(8,128)(2,1)S(1)}, u32[]{:S(2)}, u32[]{:S(2)}) collective-permute-start(bf16[160,512]{1,0:T(8,128)(2,1)S(1)} %select_convert_fusion.4), channel_id=1, source_target_pairs={{0,8},{8,0},{16,24},{24,16},{1,9},{9,1},{17,25},{25,17},{2,10},{10... | collective-permute-start | bytes 491528 | tf_op jit(solution)/shard_map/ppermute | solution.py:411
  80.2 5.9 %collective-permute-start.16 = (bf16[160,512]{1,0:T(8,128)(2,1)S(1)}, bf16[160,512]{1,0:T(8,128)(2,1)S(1)}, u32[]{:S(2)}, u32[]{:S(2)}) collective-permute-start(bf16[160,512]{1,0:T(8,128)(2,1)S(1)} %select_convert_fusion.5), channel_id=1, source_target_pairs={{0,16},{8,24},{16,0},{24,8},{1,17},{9,25},{17,1},{25,9},{2,18},{10... | collective-permute-start | bytes 491528 | tf_op jit(solution)/shard_map/ppermute | solution.py:411
  84.4 4.7 %collective-permute-start.27 = (bf16[80,512]{1,0:T(8,128)(2,1)S(1)}, bf16[80,512]{1,0:T(8,128)(2,1)S(1)}, u32[]{:S(2)}, u32[]{:S(2)}) collective-permute-start(bf16[80,512]{1,0:T(8,128)(2,1)S(1)} %select_convert_fusion.6), channel_id=1, source_target_pairs={{0,2},{1,3},{2,0},{3,1},{4,6},{5,7},{6,4},{7,5},{8,10},{9,11},{10,... | collective-permute-start | bytes 245768 | tf_op jit(solution)/shard_map/ppermute | solution.py:411
  86.2 4.9 %collective-permute-start.17 = (bf16[80,512]{1,0:T(8,128)(2,1)S(1)}, bf16[80,512]{1,0:T(8,128)(2,1)S(1)}, u32[]{:S(2)}, u32[]{:S(2)}) collective-permute-start(bf16[80,512]{1,0:T(8,128)(2,1)S(1)} %select_convert_fusion.7), channel_id=1, source_target_pairs={{0,2},{1,3},{2,0},{3,1},{4,6},{5,7},{6,4},{7,5},{8,10},{9,11},{10,... | collective-permute-start | bytes 245768 | tf_op jit(solution)/shard_map/ppermute | solution.py:411
  89.2 5.0 %collective-permute-start.28 = (bf16[40,512]{1,0:T(8,128)(2,1)S(1)}, bf16[40,512]{1,0:T(8,128)(2,1)S(1)}, u32[]{:S(2)}, u32[]{:S(2)}) collective-permute-start(bf16[40,512]{1,0:T(8,128)(2,1)S(1)} %select_convert_fusion.8), channel_id=1, source_target_pairs={{0,4},{1,5},{2,6},{3,7},{4,0},{5,1},{6,2},{7,3},{8,12},{9,13},{10,... | collective-permute-start | bytes 122888 | tf_op jit(solution)/shard_map/ppermute | solution.py:411
  91.2 5.0 %collective-permute-start.18 = (bf16[40,512]{1,0:T(8,128)(2,1)S(1)}, bf16[40,512]{1,0:T(8,128)(2,1)S(1)}, u32[]{:S(2)}, u32[]{:S(2)}) collective-permute-start(bf16[40,512]{1,0:T(8,128)(2,1)S(1)} %select_convert_fusion.9), channel_id=1, source_target_pairs={{0,4},{1,5},{2,6},{3,7},{4,0},{5,1},{6,2},{7,3},{8,12},{9,13},{10,... | collective-permute-start | bytes 122888 | tf_op jit(solution)/shard_map/ppermute | solution.py:411
  94.2 5.0 %collective-permute-start.29 = (bf16[40,512]{1,0:T(8,128)(2,1)S(1)}, bf16[40,512]{1,0:T(8,128)(2,1)S(1)}, u32[]{:S(2)}, u32[]{:S(2)}) collective-permute-start(bf16[40,512]{1,0:T(8,128)(2,1)S(1)} %add_convert_fusion), channel_id=1, source_target_pairs={{0,4},{1,5},{2,6},{3,7},{4,0},{5,1},{6,2},{7,3},{8,12},{9,13},{10,... | collective-permute-start | bytes 122888 | tf_op jit(solution)/shard_map/ppermute | solution.py:411
  96.2 5.1 %collective-permute-start.19 = (bf16[40,512]{1,0:T(8,128)(2,1)S(1)}, bf16[40,512]{1,0:T(8,128)(2,1)S(1)}, u32[]{:S(2)}, u32[]{:S(2)}) collective-permute-start(bf16[40,512]{1,0:T(8,128)(2,1)S(1)} %add_convert_fusion.1), channel_id=1, source_target_pairs={{0,4},{1,5},{2,6},{3,7},{4,0},{5,1},{6,2},{7,3},{8,12},{9,13},{10,... | collective-permute-start | bytes 122888 | tf_op jit(solution)/shard_map/ppermute | solution.py:411
  99.2 4.5 %collective-permute-start.30 = (bf16[80,512]{1,0:T(8,128)(2,1)S(1)}, bf16[80,512]{1,0:T(8,128)(2,1)S(1)}, u32[]{:S(2)}, u32[]{:S(2)}) collective-permute-start(bf16[80,512]{1,0:T(8,128)(2,1)S(1)} %pad_maximum_fusion.9), channel_id=1, source_target_pairs={{0,2},{1,3},{2,0},{3,1},{4,6},{5,7},{6,4},{7,5},{8,10},{9,11},{10,... | collective-permute-start | bytes 245768 | tf_op jit(solution)/shard_map/ppermute | solution.py:411
  101.3 4.7 %collective-permute-start.20 = (bf16[80,512]{1,0:T(8,128)(2,1)S(1)}, bf16[80,512]{1,0:T(8,128)(2,1)S(1)}, u32[]{:S(2)}, u32[]{:S(2)}) collective-permute-start(bf16[80,512]{1,0:T(8,128)(2,1)S(1)} %pad_maximum_fusion.8), channel_id=1, source_target_pairs={{0,2},{1,3},{2,0},{3,1},{4,6},{5,7},{6,4},{7,5},{8,10},{9,11},{10,... | collective-permute-start | bytes 245768 | tf_op jit(solution)/shard_map/ppermute | solution.py:411
  103.8 6.1 %collective-permute-start.31 = (bf16[160,512]{1,0:T(8,128)(2,1)S(1)}, bf16[160,512]{1,0:T(8,128)(2,1)S(1)}, u32[]{:S(2)}, u32[]{:S(2)}) collective-permute-start(bf16[160,512]{1,0:T(8,128)(2,1)S(1)} %pad_maximum_fusion.7), channel_id=1, source_target_pairs={{0,8},{8,0},{16,24},{24,16},{1,9},{9,1},{17,25},{25,17},{2,10},{10... | collective-permute-start | bytes 491528 | tf_op jit(solution)/shard_map/ppermute | solution.py:411
  106.0 6.3 %collective-permute-start.21 = (bf16[160,512]{1,0:T(8,128)(2,1)S(1)}, bf16[160,512]{1,0:T(8,128)(2,1)S(1)}, u32[]{:S(2)}, u32[]{:S(2)}) collective-permute-start(bf16[160,512]{1,0:T(8,128)(2,1)S(1)} %pad_maximum_fusion.6), channel_id=1, source_target_pairs={{0,16},{8,24},{16,0},{24,8},{1,17},{9,25},{17,1},{25,9},{2,18},{10... | collective-permute-start | bytes 491528 | tf_op jit(solution)/shard_map/ppermute | solution.py:411
  109.9 7.1 %collective-permute-start.32 = (bf16[320,512]{1,0:T(8,128)(2,1)S(1)}, bf16[320,512]{1,0:T(8,128)(2,1)S(1)}, u32[]{:S(2)}, u32[]{:S(2)}) collective-permute-start(bf16[320,512]{1,0:T(8,128)(2,1)S(1)} %pad_maximum_fusion.5), channel_id=1, source_target_pairs={{0,16},{8,24},{16,0},{24,8},{1,17},{9,25},{17,1},{25,9},{2,18},{10... | collective-permute-start | bytes 983048 | tf_op jit(solution)/shard_map/ppermute | solution.py:411
  112.3 7.1 %collective-permute-start.22 = (bf16[320,512]{1,0:T(8,128)(2,1)S(1)}, bf16[320,512]{1,0:T(8,128)(2,1)S(1)}, u32[]{:S(2)}, u32[]{:S(2)}) collective-permute-start(bf16[320,512]{1,0:T(8,128)(2,1)S(1)} %pad_maximum_fusion.4), channel_id=1, source_target_pairs={{0,8},{8,0},{16,24},{24,16},{1,9},{9,1},{17,25},{25,17},{2,10},{10... | collective-permute-start | bytes 983048 | tf_op jit(solution)/shard_map/ppermute | solution.py:411
  117.3 2.5 %collective-permute-start.33 = (bf16[640,512]{1,0:T(8,128)(2,1)S(1)}, bf16[640,512]{1,0:T(8,128)(2,1)S(1)}, u32[]{:S(2)}, u32[]{:S(2)}) collective-permute-start(bf16[640,512]{1,0:T(8,128)(2,1)S(1)} %pad_maximum_fusion.3), channel_id=1, source_target_pairs={{0,1},{1,0},{2,3},{3,2},{4,5},{5,4},{6,7},{7,6},{8,9},{9,8},{10,11... | collective-permute-start | bytes 1966088 | tf_op jit(solution)/shard_map/ppermute | solution.py:411
  119.7 2.2 %collective-permute-start.23 = (bf16[640,512]{1,0:T(8,128)(2,1)S(1)}, bf16[640,512]{1,0:T(8,128)(2,1)S(1)}, u32[]{:S(2)}, u32[]{:S(2)}) collective-permute-start(bf16[640,512]{1,0:T(8,128)(2,1)S(1)} %pad_maximum_fusion.2), channel_id=1, source_target_pairs={{0,1},{1,0},{2,3},{3,2},{4,5},{5,4},{6,7},{7,6},{8,9},{9,8},{10,11... | collective-permute-start | bytes 1966088 | tf_op jit(solution)/shard_map/ppermute | solution.py:411
  (26 other events, 138.0 us)

commit v3 on v2

--- a/solution.py
+++ b/solution.py
@@ -51,6 +51,7 @@
 
 def encode_kernel(
     freqs,
+    size,
     patch_ref,
     basis_ref,
     mix_ref,
@@ -63,12 +64,9 @@
     norm_ref,
     rscale_ref,
     normed_ref,
-    preact_ref,
-    hidden_ref,
-    feat,
-    in_w,
-    sem,
+    *rest,
 ):
+    pieces, (feat, hidden_ref, in_w, sem) = rest[:size], rest[size:]
     step = pl.program_id(0)
     load = pltpu.make_async_copy(in_hbm, in_w, sem)
 
@@ -104,8 +102,8 @@
         normed_ref[...] = normed
         rscale_ref[...] = jnp.broadcast_to(rscale, rscale_ref.shape)
         preact = mm(normed, in_w[...])
-        preact_ref[...] = preact
-        hidden = (preact * jax.nn.sigmoid(preact)).astype(BF16)
+        sigm = jax.nn.sigmoid(preact)
+        hidden = (preact * sigm).astype(BF16)
         hidden_ref[...] = hidden
         raw = mm(hidden, out_w_ref[...])
         norms = jnp.sqrt(jnp.sum(raw * raw, axis=1, keepdims=True) + 1e-06)
@@ -113,9 +111,27 @@
         unit32 = raw / norms
         unit32_ref[...] = unit32
         units_ref[...] = unit32.astype(BF16)
-
-
-def encode(patches, w_mix, w_in, w_out):
+        slope = (sigm * (1.0 + preact * (1.0 - sigm))).astype(BF16)
+        deep, wide = normed_ref.shape[1] // size, hidden_ref.shape[1] // size
+        me = lax.axis_index("blk")
+        for i, piece_ref in enumerate(pieces):
+            owner = me ^ i
+            piece_ref[:, :deep] = normed_ref[:, pl.ds(pl.multiple_of(owner * deep, 128), deep)]
+            piece_ref[:, deep : deep + slope.shape[1]] = slope
+            if wide % 128 == 0:
+                piece_ref[:, deep + slope.shape[1] :] = hidden_ref[
+                    :, pl.ds(pl.multiple_of(owner * wide, 128), wide)
+                ]
+            else:
+                piece_ref[:, deep + slope.shape[1] :] = hidden_ref[...]
+
+
+def piece_columns(feats, width, size):
+    wide = width // size
+    return feats // size, width, wide if wide % 128 == 0 else width
+
+
+def encode(patches, w_mix, w_in, w_out, size):
     count, length, lanes = patches.shape
     filters = w_mix.shape[1]
     feats, width = w_in.shape
@@ -124,6 +140,7 @@
     per = 2 * SUB
     groups = count // SUB
     rows = 2 * freqs * SUB
+    piece = (count, sum(piece_columns(feats, width, size)))
 
     def whole(*dims):
         return pl.BlockSpec(dims, lambda i: (0,) * len(dims))
@@ -136,11 +153,9 @@
         (shape((count, 128), F32), whole(count, 128)),
         (shape((count, 128), F32), whole(count, 128)),
         (shape((count, feats), BF16), whole(count, feats)),
-        (shape((count, width), F32), whole(count, width)),
-        (shape((count, width), BF16), whole(count, width)),
-    ]
-    return pl.pallas_call(
-        functools.partial(encode_kernel, freqs),
+    ] + [(shape(piece, BF16), whole(*piece))] * size
+    return pl.pallas_call(
+        functools.partial(encode_kernel, freqs, size),
         grid=(count // per,),
         in_specs=[
             pl.BlockSpec((per, length, lanes), lambda i: (i, 0, 0)),
@@ -153,27 +168,35 @@
         out_specs=[spec for _, spec in outs],
         scratch_shapes=[
             pltpu.VMEM((count, feats), F32),
+            pltpu.VMEM((count, width), BF16),
             pltpu.VMEM((feats, width), BF16),
             pltpu.SemaphoreType.DMA,
         ],
-        compiler_params=params(24),
+        compiler_params=params(60),
         cost_estimate=cost(3e9, 14e6),
     )(patches, angle_basis(length, freqs), w_mix, w_out, w_in)
 
 
+def exponentials(units, keys, own):
+    expo = jnp.exp(SCALE * mm_nt(units, keys))
+    if own:
+        row = lax.broadcasted_iota(jnp.int32, expo.shape, 0)
+        col = lax.broadcasted_iota(jnp.int32, expo.shape, 1)
+        expo = jnp.where(row == col, 0.0, expo)
+    return expo
+
+
 def negative_kernel(size, *refs):
-    pieces, (expo_ref, zneg_ref, numer_ref) = refs[:size], refs[size:]
+    pieces, stacked, (zneg_ref, numer_ref, even_ref) = refs[:size], refs[size:-3], refs[-3:]
     units = pieces[0][...]
     count = units.shape[0]
+    even_ref[:count, :] = units
+    for i, each in enumerate(stacked):
+        even_ref[(i + 1) * count : (i + 2) * count, :] = each[...]
     zneg = numer = None
     for i, piece in enumerate(pieces):
         keys = piece[...]
-        expo = jnp.exp(SCALE * mm_nt(units, keys))
-        if i == 0:
-            row = lax.broadcasted_iota(jnp.int32, expo.shape, 0)
-            col = lax.broadcasted_iota(jnp.int32, expo.shape, 1)
-            expo = jnp.where(row == col, 0.0, expo)
-        expo_ref[:, i * count : (i + 1) * count] = expo
+        expo = exponentials(units, keys, i == 0)
         total = jnp.sum(expo, axis=1, keepdims=True)
         term = mm(expo.astype(BF16), keys)
         zneg = total if zneg is None else zneg + total
@@ -182,21 +205,21 @@
     numer_ref[...] = numer
 
 
-def negatives(pieces):
+def negatives(pieces, stacked):
     count, embed = pieces[0].shape
     size = len(pieces)
     return pl.pallas_call(
         functools.partial(negative_kernel, size),
-        in_specs=[VMEM] * size,
+        in_specs=[VMEM] * (size + len(stacked)),
         out_shape=[
-            shape((count, size * count), F32),
             shape((count, 128), F32),
             shape((count, embed), F32),
+            shape(((len(stacked) + 1) * count, embed), BF16),
         ],
         out_specs=[VMEM] * 3,
         compiler_params=params(8),
         cost_estimate=cost(4e8, 1e6),
-    )(*pieces)
+    )(*pieces, *stacked)
 
 
 def as_rows(column, count):
@@ -249,26 +272,16 @@
 def upper_kernel(size, *refs):
     pieces, rest = refs[:size], refs[size:]
     stats, rest = rest[:size], rest[size:]
-    (
-        expo_ref,
-        even_ref,
-        odd_ref,
-        even_stats,
-        odd_stats,
-        local_ref,
-        unit32_ref,
-        norm_ref,
-        out_w_ref,
-        preact_ref,
-        pay_ref,
-    ) = rest
+    (even_ref, odd_ref, even_stats, odd_stats, local_ref, unit32_ref, norm_ref, out_ref) = rest
     count, embed = local_ref.shape
     coef = SCALE / count
+    units = pieces[0][...]
     keyterm = None
     for i in range(size):
-        expo = expo_ref[:, i * count : (i + 1) * count]
+        keys = pieces[i][...]
+        expo = exponentials(units, keys, i == 0)
         weights = (expo / stats[i][0:1, :]).astype(BF16)
-        term = mm(weights, pieces[i][...])
+        term = mm(weights, keys)
         keyterm = term if keyterm is None else keyterm + term
     mine = lax.axis_index("dp") * count + lax.broadcasted_iota(jnp.int32, (count, count), 0)
     mine = mine.astype(F32)
@@ -286,32 +299,33 @@
     grad_units = local_ref[...] + coef * keyterm + back
     unit32 = unit32_ref[...]
     along = jnp.sum(unit32 * grad_units, axis=1, keepdims=True)
-    grad_raw = ((grad_units - unit32 * along) / norm_ref[:, :1]).astype(BF16)
-    grad_hid = mm_nt(grad_raw, out_w_ref[...])
-    preact = preact_ref[...]
-    sigm = jax.nn.sigmoid(preact)
-    width = preact.shape[1]
-    pay_ref[:, :width] = (grad_hid * sigm * (1.0 + preact * (1.0 - sigm))).astype(BF16)
-    pay_ref[:, width:] = grad_raw
-
-
-def upper(pieces, stats, expo, even, odd, even_stats, odd_stats, local, unit32, norms, w_out, preact):
+    out_ref[...] = ((grad_units - unit32 * along) / norm_ref[:, :1]).astype(BF16)
+
+
+def upper(pieces, stats, even, odd, even_stats, odd_stats, local, unit32, norms):
     count, embed = local.shape
     size = len(pieces)
-    args = [*pieces, *stats, expo, even, odd, even_stats, odd_stats, local, unit32, norms, w_out, preact]
+    args = [*pieces, *stats, even, odd, even_stats, odd_stats, local, unit32, norms]
     return pl.pallas_call(
         functools.partial(upper_kernel, size),
         in_specs=[VMEM] * len(args),
-        out_shape=shape((count, preact.shape[1] + embed), BF16),
+        out_shape=shape((count, embed), BF16),
         out_specs=VMEM,
         compiler_params=params(8),
         cost_estimate=cost(4e8, 2e6),
     )(*args)
 
 
+def pre_grads(grad_raw, out_w, slope):
+    return (mm_nt(grad_raw, out_w) * slope.astype(F32)).astype(BF16)
+
+
 def lower_kernel(
     freqs,
-    pay_ref,
+    columns,
+    raw_ref,
+    out_w_ref,
+    piece_ref,
     normed_ref,
     rscale_ref,
     in_hbm,
@@ -330,9 +344,10 @@
     ]
     for each in loads:
         each.start()
-    width = in_w.shape[1]
+    deep, width, _ = columns
+    grad_pre = pre_grads(raw_ref[...], out_w_ref[...], piece_ref[:, deep : deep + width])
     loads[0].wait()
-    grad_norm = mm_nt(pay_ref[:, :width], in_w[...])
+    grad_norm = mm_nt(grad_pre, in_w[...])
     xhat = normed_ref[...].astype(F32)
     mean = jnp.mean(grad_norm, axis=1, keepdims=True)
     slope = jnp.mean(grad_norm * xhat, axis=1, keepdims=True)
@@ -358,13 +373,13 @@
     g_mix_ref[...] = total.T
 
 
-def lower(pay, normed, rscale, w_in, mixed, spec, freqs):
+def lower(grad_raw, w_out, piece, normed, rscale, w_in, mixed, spec, freqs, columns):
     count, feats = normed.shape
     groups, rows, filters = mixed.shape
     lanes = spec.shape[2]
     return pl.pallas_call(
-        functools.partial(lower_kernel, freqs),
-        in_specs=[VMEM] * 3 + [ANY] * 3,
+        functools.partial(lower_kernel, freqs, columns),
+        in_specs=[VMEM] * 5 + [ANY] * 3,
         out_shape=shape((lanes, filters), F32),
         out_specs=VMEM,
         scratch_shapes=[
@@ -374,36 +389,172 @@
             pltpu.VMEM((count, feats), F32),
             pltpu.SemaphoreType.DMA((3,)),
         ],
+        compiler_params=params(60),
+        cost_estimate=cost(1e9, 7e6),
+    )(grad_raw, w_out, piece, normed, rscale, w_in, mixed, spec)
+
+
+def up_to(rows, unit):
+    return -(-rows // unit) * unit
+
+
+class Layout:
+    def __init__(self, lanes, filters, feats, width, embed, size, peers):
+        self.size, self.peers = size, peers
+        self.in_rows = feats // size // peers
+        self.out_rows = width // size // peers
+        self.mix_rows = lanes // peers
+        self.top = up_to(self.in_rows, 16)
+        self.strip = max(16, up_to(self.out_rows, 16))
+        self.mix_blocks = -(-self.mix_rows // self.strip)
+        self.rows = self.top + self.strip
+        self.width = width
+        assert embed == 128 and filters == 128 and (1 + self.mix_blocks) * 128 <= width
+
+    def mix_parts(self):
+        for block in range(self.mix_blocks):
+            start = block * self.strip
+            yield start, min(self.strip, self.mix_rows - start), slice(128 * (block + 1), 128 * (block + 2))
+
+
+def weights_kernel(lay, columns, *refs):
+    size, peers = lay.size, lay.peers
+    pieces, raws, rest = refs[:size], refs[size : 2 * size], refs[2 * size :]
+    out_w_ref, mix_ref, keep_ref, away_ref, g_in, g_out = rest
+    deep, width, wide = columns
+    share = width // size
+    for i in range(size):
+        raw = raws[i][...]
+        grad_pre = pre_grads(raw, out_w_ref[...], pieces[i][:, deep : deep + width])
+        term_in = mm_tn(pieces[i][:, :deep], grad_pre)
+        term_out = mm_tn(pieces[i][:, deep + width :], raw)
+        if i == 0:
+            g_in[...] = term_in
+            g_out[...] = term_out
+        else:
+            g_in[...] += term_in
+            g_out[...] += term_out
+    me = lax.axis_index("dp")
+    first = 0 if wide == share else lax.axis_index("blk") * share
+    keep_ref[...] = jnp.zeros(keep_ref.shape, F32)
+    away_ref[...] = jnp.zeros(away_ref.shape, BF16)
+    for slot in range(peers):
+        owner = me ^ slot
+        target = away_ref if slot & 1 else keep_ref
+        at = slot >> 1
+        target[at, : lay.in_rows, :] = g_in[pl.ds(owner * lay.in_rows, lay.in_rows), :].astype(target.dtype)
+        target[at, lay.top : lay.top + lay.out_rows, :128] = g_out[
+            pl.ds(first + owner * lay.out_rows, lay.out_rows), :
+        ].astype(target.dtype)
+        for start, rows, cols in lay.mix_parts():
+            target[at, lay.top : lay.top + rows, cols] = mix_ref[
+                pl.ds(owner * lay.mix_rows + start, rows), :
+            ].astype(target.dtype)
+
+
+def weight_grads(lay, columns, pieces, raws, w_out, g_mix):
+    deep, width, wide = columns
+    block = (lay.peers // 2, lay.rows, lay.width)
+    args = [*pieces, *raws, w_out, g_mix]
+    return pl.pallas_call(
+        functools.partial(weights_kernel, lay, columns),
+        in_specs=[VMEM] * len(args),
+        out_shape=[shape(block, F32), shape(block, BF16)],
+        out_specs=[VMEM] * 2,
+        scratch_shapes=[pltpu.VMEM((deep, width), F32), pltpu.VMEM((wide, 128), F32)],
+        compiler_params=params(16),
+        cost_estimate=cost(6e8, 4e6),
+    )(*args)
+
+
+def pair_kernel(keep_ref, got_ref, own_ref, *out_refs):
+    own_ref[...] = keep_ref[0] + got_ref[0].astype(F32)
+    for i, out_ref in enumerate(out_refs):
+        out_ref[...] = (keep_ref[i + 1] + got_ref[i + 1].astype(F32)).astype(BF16)
+
+
+def pair_sum(keep, got):
+    slots, rows, width = keep.shape
+    return pl.pallas_call(
+        pair_kernel,
+        in_specs=[VMEM] * 2,
+        out_shape=[shape((rows, width), F32)] + [shape((rows, width), BF16)] * (slots - 1),
+        out_specs=[VMEM] * slots,
+        compiler_params=params(8),
+        cost_estimate=cost(1e6, 2e6),
+    )(keep, got)
+
+
+def total_kernel(own_ref, *refs):
+    total = own_ref[...]
+    for each in refs[:-1]:
+        total = total + each[...].astype(F32)
+    refs[-1][...] = total.astype(BF16)
+
+
+def total_sum(own, got):
+    return pl.pallas_call(
+        total_kernel,
+        in_specs=[VMEM] * (1 + len(got)),
+        out_shape=shape(own.shape, BF16),
+        out_specs=VMEM,
+        compiler_params=params(8),
+        cost_estimate=cost(1e6, 1e6),
+    )(own, *got)
+
+
+def finish_kernel(lay, *refs):
+    size, slots = lay.size, lay.peers // 2
+    evens, odds = refs[:size], refs[size : 2 * size]
+    g_mix_ref, g_in_hbm, g_out_ref, stage, sems = refs[2 * size :]
+    me_blk, me_dp = lax.axis_index("blk"), lax.axis_index("dp")
+    copies = []
+    for i in range(size):
+        for core, source in enumerate((evens[i], odds[i])):
+            for z in range(slots):
+                at = z * lay.rows
+                owner = me_dp ^ (2 * z + core)
+                slot = (i * 2 + core) * slots + z
+                stage[slot] = source[at : at + lay.in_rows, :].astype(F32)
+                row = ((me_blk ^ i) * lay.peers + owner) * lay.in_rows
+                copy = pltpu.make_async_copy(
+                    stage.at[slot], g_in_hbm.at[pl.ds(row, lay.in_rows), :], sems.at[slot]
+                )
+                copy.start()
+                copies.append(copy)
+                row = ((me_blk ^ i) * lay.peers + owner) * lay.out_rows
+                strip = at + lay.top
+                g_out_ref[pl.ds(row, lay.out_rows), :] = source[
+                    strip : strip + lay.out_rows, :128
+                ].astype(F32)
+    for core in range(2):
+        for z in range(slots):
+            strip = z * lay.rows + lay.top
+            owner = me_dp ^ (2 * z + core)
+            for start, rows, cols in lay.mix_parts():
+                blocks = {0: evens, 1: odds}[core]
+                terms = [blocks[i][strip : strip + rows, cols].astype(F32) for i in range(size)]
+                while len(terms) > 1:
+                    terms = [terms[t] + terms[t + 1] for t in range(0, len(terms), 2)]
+                g_mix_ref[pl.ds(owner * lay.mix_rows + start, rows), :] = terms[0]
+    for copy in copies:
+        copy.wait()
+
+
+def finish(lay, evens, odds, lanes, feats, width):
+    slots = lay.size * lay.peers
+    return pl.pallas_call(
+        functools.partial(finish_kernel, lay),
+        in_specs=[VMEM] * (2 * lay.size),
+        out_shape=[shape((lanes, 128), F32), shape((feats, width), F32), shape((width, 128), F32)],
+        out_specs=[VMEM, ANY, VMEM],
+        scratch_shapes=[
+            pltpu.VMEM((slots, lay.in_rows, lay.width), F32),
+            pltpu.SemaphoreType.DMA((slots,)),
+        ],
         compiler_params=params(24),
-        cost_estimate=cost(1e9, 7e6),
-    )(pay, normed, rscale, w_in, mixed, spec)
-
-
-def weights_kernel(width, normed_ref, hidden_ref, pay_ref, g_in_ref, g_out_ref):
-    grad_pre = pay_ref[:, :width]
-    g_in_ref[...] = mm_tn(normed_ref[...], grad_pre)
-    g_out_ref[...] = mm_tn(hidden_ref[...], pay_ref[:, width:])
-
-
-def weight_grads(normed, hidden, pay):
-    count, feats = normed.shape
-    width = hidden.shape[1]
-    embed = pay.shape[1] - width
-    return pl.pallas_call(
-        functools.partial(weights_kernel, width),
-        in_specs=[VMEM] * 3,
-        out_shape=[shape((feats, width), F32), shape((width, embed), F32)],
-        out_specs=[VMEM] * 2,
-        compiler_params=params(24),
-        cost_estimate=cost(3e8, 6e6),
-    )(normed, hidden, pay)
-
-
-def hop_bits(axis):
-    size = lax.axis_size(axis)
-    steps = size.bit_length() - 1
-    assert size == 1 << steps
-    return [1 << step for step in range(steps)]
+        cost_estimate=cost(1e6, 8e6),
+    )(*evens, *odds)
 
 
 def swap(block, axis, bit):
@@ -411,87 +562,48 @@
     return lax.ppermute(block, axis, [(src, src ^ bit) for src in range(size)])
 
 
-def side(axis, bit):
-    return (lax.axis_index(axis) & bit) != 0
-
-
-def scatter_sum(part, route):
-    for axis, bit in route:
-        half = part.shape[0] // 2
-        upper_side = side(axis, bit)
-        low, high = part[:half], part[half:]
-        away = jnp.where(upper_side, low, high).astype(BF16)
-        kept = jnp.where(upper_side, high, low)
-        part = kept + swap(away, axis, bit).astype(F32)
-    return part
-
-
-def gather_back(part, route):
-    for axis, bit in reversed(route):
-        other = swap(part, axis, bit)
-        upper_side = side(axis, bit)
-        part = jnp.concatenate(
-            [jnp.where(upper_side, other, part), jnp.where(upper_side, part, other)], axis=0
-        )
-    return part
-
-
-def reduce_all(g_mix, g_in, g_out):
-    width = g_in.shape[1]
-    pieces = [g_mix.reshape(-1, width), g_out.reshape(-1, width)]
-    small = jnp.concatenate(pieces, axis=0)
-    devices = lax.axis_size("blk") * lax.axis_size("dp")
-    unit = 8 * devices
-    total = -(-(g_in.shape[0] + small.shape[0]) // (2 * unit)) * 2 * unit
-    pad = total - g_in.shape[0] - small.shape[0]
-    whole = jnp.concatenate([g_in, small, jnp.zeros((pad, width), F32)], axis=0)
-    across = [("blk", bit) for bit in hop_bits("blk")]
-    along = [("dp", bit) for bit in hop_bits("dp")]
-    routes = [along[:1] + across + along[1:], along[:1] + across[::-1] + along[1:]]
-    half = total // 2
-    done = [
-        gather_back(scatter_sum(whole[k * half : (k + 1) * half], route).astype(BF16), route)
-        for k, route in enumerate(routes)
-    ]
-    whole = jnp.concatenate(done, axis=0).astype(F32)
-    rows = g_in.shape[0]
-    mix_rows = pieces[0].shape[0]
-    out_rows = pieces[1].shape[0]
-    return (
-        whole[rows : rows + mix_rows].reshape(g_mix.shape),
-        whole[:rows],
-        whole[rows + mix_rows : rows + mix_rows + out_rows].reshape(g_out.shape),
-    )
-
-
 def spread(block, axis, hops):
     return [block] + [swap(block, axis, hop) for hop in hops]
 
 
 def on_device(patches, w_mix, w_in, w_out, partner_dev, partner_row):
-    count = patches.shape[0]
+    count, _, lanes = patches.shape
     filters = w_mix.shape[1]
-    freqs = w_in.shape[0] // filters
-    blocks, peers = lax.axis_size("blk"), lax.axis_size("dp")
-    assert peers % 2 == 0
-    spec, mixed, units, unit32, norms, rscale, normed, preact, hidden = encode(
-        patches, w_mix, w_in, w_out
+    feats, width = w_in.shape
+    embed = w_out.shape[1]
+    freqs = feats // filters
+    size, peers = lax.axis_size("blk"), lax.axis_size("dp")
+    assert size & (size - 1) == 0 and peers & (peers - 1) == 0 and peers > 1
+    across, along = range(1, size), range(2, peers, 2)
+    columns = piece_columns(feats, width, size)
+    lay = Layout(lanes, filters, feats, width, embed, size, peers)
+
+    spec, mixed, units, unit32, norms, rscale, normed, *early = encode(
+        patches, w_mix, w_in, w_out, size
     )
-    across, along = range(1, blocks), range(2, peers, 2)
     pieces = spread(units, "blk", across)
-    even = jnp.concatenate(spread(units, "dp", along), axis=0)
+    stacked = spread(units, "dp", along)
+    pieces[1:], stacked[1:] = lax.optimization_barrier((pieces[1:], stacked[1:]))
+    early = lax.optimization_barrier((early, pieces[1:]))[0]
+    zneg, numer, even = negatives(pieces, stacked[1:])
     odd = swap(even, "dp", 1)
-    expo, zneg, numer = negatives(pieces)
+    factors = [early[0]] + [swap(early[hop], "blk", hop) for hop in across]
     local, stats, loss = positives(partner_dev, partner_row, even, odd, zneg, numer)
     group_stats = spread(stats, "blk", across)
     even_stats = jnp.concatenate(spread(stats, "dp", along), axis=0)
     odd_stats = swap(even_stats, "dp", 1)
-    pay = upper(
-        pieces, group_stats, expo, even, odd, even_stats, odd_stats, local, unit32, norms, w_out, preact
-    )
-    g_in, g_out = weight_grads(normed, hidden, pay)
-    g_mix = lower(pay, normed, rscale, w_in, mixed, spec, freqs)
-    g_mix, g_in, g_out = reduce_all(g_mix, g_in, g_out)
+    grad_raw = upper(pieces, group_stats, even, odd, even_stats, odd_stats, local, unit32, norms)
+    raws = spread(grad_raw, "blk", across)
+    g_mix = lower(grad_raw, w_out, early[0], normed, rscale, w_in, mixed, spec, freqs, columns)
+
+    keep, away = weight_grads(lay, columns, factors, raws, w_out, g_mix)
+    own, *sends = pair_sum(keep, swap(away, "dp", 1))
+    got = [swap(block, "dp", hop) for block, hop in zip(sends, along)]
+    share = total_sum(own, got)
+    plane = jnp.concatenate(spread(share, "dp", along), axis=0)
+    evens = spread(plane, "blk", across)
+    odds = [swap(block, "dp", 1) for block in evens]
+    g_mix, g_in, g_out = finish(lay, evens, odds, lanes, feats, width)
     return (loss.reshape(count), g_mix, g_in, g_out)
 
 

time: 131 us -> 112 us (0.85)
  local copies, waits for them, and re-layouts: 25.3 us -> 2.45 us
  Pallas kernels: 12 us -> 23.9 us
  other arithmetic: 11.1 us -> 0.02 us
  waiting for transfers between devices: 37.9 us -> 48.6 us
  starting transfers between devices: 43.3 us -> 35.9 us
    unnamed x54 -> x25, local copies, waits for them, and re-layouts: 18.6 us -> 2.45 us
    pallas_call x3 -> x6, Pallas kernels: 10 us -> 21.7 us  [the longest x1 11 us: encode(): pl.pallas_call(functools.partial(encode_kernel, freqs, size), grid=(count...]
    ppermute x34, waiting for transfers between devices: 37.9 us -> 48.6 us  [swap(): return lax.ppermute(block, axis, [(src, src ^ bit) for src in range(size)])]
    ppermute x34, starting transfers between devices: 43.3 us -> 35.9 us  [swap(): return lax.ppermute(block, axis, [(src, src ^ bit) for src in range(size)])]
    convert_element_type x12 -> x0, other arithmetic: 6.35 us -> none  [the longest x9 3.73 us: scatter_sum(): away = jnp.where(upper_side, low, high).astype(BF16)]
    slice x2 -> x0, local copies, waits for them, and re-layouts: 5.31 us -> none  [the longest x1 4.64 us: reduce_all(): whole[:rows]]
    add x7 -> x0, other arithmetic: 3.52 us -> none  [scatter_sum(): part = kept + swap(away, axis, bit).astype(F32)]
    reshape x4 -> x0, local copies, waits for them, and re-layouts: 1.44 us -> none  [the longest x1 0.72 us: reduce_all(): whole[rows + mix_rows:rows + mix_rows + out_rows].reshape(g_out.shape)]
  transfers between devices with their start and end apart: 34 -> 34, of which waited for: 24 -> 19; matrix products, arithmetic and copies ran while one was open for 2% -> 0% of each run, Pallas kernels for 0% -> 7%
where the time goes in v3:
time: 112 us
  waiting for transfers between devices  48.6 us (43%)
  starting transfers between devices  35.9 us (32%)
  Pallas kernels  23.9 us (21%)
  local copies, waits for them, and re-layouts  2.45 us (2%)
    ppermute x34, waiting for transfers between devices, swap(): return lax.ppermute(block, axis, [(src, src ^ bit) for src in range(size)])  48.6 us
    ppermute x34, starting transfers between devices, swap(): return lax.ppermute(block, axis, [(src, src ^ bit) for src in range(size)])  35.9 us
    pallas_call x1, Pallas kernels, encode(): pl.pallas_call(functools.partial(encode_kernel, freqs, size), grid=(count...  11 us
    pallas_call x1, Pallas kernels, lower(): pl.pallas_call(functools.partial(lower_kernel, freqs, columns), in_specs=...  6.04 us
    pallas_call x1, Pallas kernels, finish(): pl.pallas_call(functools.partial(finish_kernel, lay), in_specs=[VMEM] * (...  3.02 us
    unnamed x25, local copies, waits for them, and re-layouts  2.45 us
  transfers between devices with their start and end apart: 34, of which 19 were waited for; matrix products, arithmetic and copies ran while one was open for 0% of the time, Pallas kernels for 7%

profile of v3, /device:TPU:0, one launch (start us, length us, event | category | flops | bytes accessed | tf_op | source)
XLA Modules:
  0.0 111.7 jit_solution(1875634777481588498)
XLA Ops:
  0.7 11.0 %shard_map.102 = (bf16[16,256,256]{2,1,0:T(8,128)(2,1)}, f32[16,256,128]{2,1,0:T(8,128)}, bf16[128,128]{1,0:T(8,128)(2,1)}, f32[128,128]{1,0:T(8,128)}, f32[128,...) custom-call(bf16[128,64,256]{2,1,0:T(8,128)(2,1)} %patch_ref.1, ...), custom_call_target="tpu_custom_call" | custom-call | flops 3000000000 | bytes 14000000 | tf_op jit(solution)/shard_map/pallas_call | solution.py:157
  11.7 5.1 %collective-permute-start.5 = (bf16[128,128]{1,0:T(8,128)(2,1)}, bf16[128,128]{1,0:T(8,128)(2,1)S(1)}, u32[]{:S(2)}, u32[]{:S(2)}) collective-permute-start(bf16[128,128]{1,0:T(8,128)(2,1)} %get-tuple-element.40.refs_0_), channel_id=1, source_target_pairs={{0,6},{1,7},{2,4},{3,5},{4,2},{5,3},{6,0},{7,1},{8,14},{9,15},{10,... | collective-permute-start | bytes 98312 | tf_op jit(solution)/shard_map/ppermute | solution.py:562
  17.5 2.6 %collective-permute-start.2 = (bf16[128,128]{1,0:T(8,128)(2,1)}, bf16[128,128]{1,0:T(8,128)(2,1)S(1)}, u32[]{:S(2)}, u32[]{:S(2)}) collective-permute-start(bf16[128,128]{1,0:T(8,128)(2,1)} %get-tuple-element.40.refs_0_), channel_id=1, source_target_pairs={{0,24},{8,16},{16,8},{24,0},{1,25},{9,17},{17,9},{25,1},{2,26},{10... | collective-permute-start | bytes 98312 | tf_op jit(solution)/shard_map/ppermute | solution.py:562
  22.5 1.7 %collective-permute-done.1.refs_2_ = bf16[128,128]{1,0:T(8,128)(2,1)S(1)} collective-permute-done((bf16[128,128]{1,0:T(8,128)(2,1)}, bf16[128,128]{1,0:T(8,128)(2,1)S(1)}, u32[]{:S(2)}, u32[]{:S(2)}) %collective-permute-start.1) | collective-permute-done | bytes 32800 | tf_op jit(solution)/shard_map/ppermute | solution.py:562
  26.4 1.7 %collective-permute-start.8 = (bf16[128,1152]{1,0:T(8,128)(2,1)}, bf16[128,1152]{1,0:T(8,128)(2,1)S(1)}, u32[]{:S(2)}, u32[]{:S(2)}) collective-permute-start(bf16[128,1152]{1,0:T(8,128)(2,1)} %get-tuple-element.57), channel_id=1, source_target_pairs={{0,16},{8,24},{16,0},{24,8},{1,17},{9,25},{17,1},{25,9},{2,18},{10... | collective-permute-start | bytes 884744 | tf_op jit(solution)/shard_map/ppermute | solution.py:562
  28.1 1.4 %collective-permute-start.9 = (bf16[128,1152]{1,0:T(8,128)(2,1)}, bf16[128,1152]{1,0:T(8,128)(2,1)S(1)}, u32[]{:S(2)}, u32[]{:S(2)}) collective-permute-start(bf16[128,1152]{1,0:T(8,128)(2,1)} %get-tuple-element.58), channel_id=1, source_target_pairs={{0,24},{8,16},{16,8},{24,0},{1,25},{9,17},{17,9},{25,1},{2,26},{10... | collective-permute-start | bytes 884744 | tf_op jit(solution)/shard_map/ppermute | solution.py:562
  30.6 3.6 %collective-permute-start.15 = (f32[8,128]{1,0:T(8,128)S(1)}, f32[8,128]{1,0:T(8,128)S(1)}, u32[]{:S(2)}, u32[]{:S(2)}) collective-permute-start(f32[8,128]{1,0:T(8,128)S(1)} %get-tuple-element.59.refs_4_), channel_id=1, source_target_pairs={{0,6},{1,7},{2,4},{3,5},{4,2},{5,3},{6,0},{7,1},{8,14},{9,15},{10,... | collective-permute-start | bytes 12296 | tf_op jit(solution)/shard_map/ppermute | solution.py:562
  34.2 3.6 %collective-permute-done.13 = f32[8,128]{1,0:T(8,128)S(1)} collective-permute-done((f32[8,128]{1,0:T(8,128)S(1)}, f32[8,128]{1,0:T(8,128)S(1)}, u32[]{:S(2)}, u32[]{:S(2)}) %collective-permute-start.13) | collective-permute-done | bytes 4128 | tf_op jit(solution)/shard_map/ppermute | solution.py:562
  37.8 4.5 %collective-permute-done.14 = f32[8,128]{1,0:T(8,128)S(1)} collective-permute-done((f32[8,128]{1,0:T(8,128)S(1)}, f32[8,128]{1,0:T(8,128)S(1)}, u32[]{:S(2)}, u32[]{:S(2)}) %collective-permute-start.14) | collective-permute-done | bytes 4128 | tf_op jit(solution)/shard_map/ppermute | solution.py:562
  42.4 1.6 %collective-permute-start.12 = (f32[8,128]{1,0:T(8,128)S(1)}, f32[8,128]{1,0:T(8,128)S(1)}, u32[]{:S(2)}, u32[]{:S(2)}) collective-permute-start(f32[8,128]{1,0:T(8,128)S(1)} %get-tuple-element.59.refs_4_), channel_id=1, source_target_pairs={{0,24},{8,16},{16,8},{24,0},{1,25},{9,17},{17,9},{25,1},{2,26},{10... | collective-permute-start | bytes 12296 | tf_op jit(solution)/shard_map/ppermute | solution.py:562
  44.0 3.0 %collective-permute-done.12.refs_7_ = f32[8,128]{1,0:T(8,128)S(1)} collective-permute-done((f32[8,128]{1,0:T(8,128)S(1)}, f32[8,128]{1,0:T(8,128)S(1)}, u32[]{:S(2)}, u32[]{:S(2)}) %collective-permute-start.12) | collective-permute-done | bytes 4128 | tf_op jit(solution)/shard_map/ppermute | solution.py:562
  47.0 1.5 %collective-permute-start.11 = (f32[8,128]{1,0:T(8,128)S(1)}, f32[8,128]{1,0:T(8,128)S(1)}, u32[]{:S(2)}, u32[]{:S(2)}) collective-permute-start(f32[8,128]{1,0:T(8,128)S(1)} %get-tuple-element.59.refs_4_), channel_id=1, source_target_pairs={{0,16},{8,24},{16,0},{24,8},{1,17},{9,25},{17,1},{25,9},{2,18},{10... | collective-permute-start | bytes 12296 | tf_op jit(solution)/shard_map/ppermute | solution.py:562
  48.5 2.1 %collective-permute-done.11.refs_6_ = f32[8,128]{1,0:T(8,128)S(1)} collective-permute-done((f32[8,128]{1,0:T(8,128)S(1)}, f32[8,128]{1,0:T(8,128)S(1)}, u32[]{:S(2)}, u32[]{:S(2)}) %collective-permute-start.11) | collective-permute-done | bytes 4128 | tf_op jit(solution)/shard_map/ppermute | solution.py:562
  51.1 3.1 %collective-permute-done.10.refs_5_ = f32[8,128]{1,0:T(8,128)S(1)} collective-permute-done((f32[8,128]{1,0:T(8,128)S(1)}, f32[8,128]{1,0:T(8,128)S(1)}, u32[]{:S(2)}, u32[]{:S(2)}) %collective-permute-start.10) | collective-permute-done | bytes 4128 | tf_op jit(solution)/shard_map/ppermute | solution.py:562
  55.0 1.6 %collective-permute-start.19 = (bf16[128,128]{1,0:T(8,128)(2,1)S(1)}, bf16[128,128]{1,0:T(8,128)(2,1)S(1)}, u32[]{:S(2)}, u32[]{:S(2)}) collective-permute-start(bf16[128,128]{1,0:T(8,128)(2,1)S(1)} %shard_map.105.raw_ref.refs_4_), channel_id=1, source_target_pairs={{0,24},{8,16},{16,8},{24,0},{1,25},{9,17},{17,9},{25,1},{2,26},{10... | collective-permute-start | bytes 98312 | tf_op jit(solution)/shard_map/ppermute | solution.py:562
  57.1 2.9 %collective-permute-done.19.refs_7_ = bf16[128,128]{1,0:T(8,128)(2,1)S(1)} collective-permute-done((bf16[128,128]{1,0:T(8,128)(2,1)S(1)}, bf16[128,128]{1,0:T(8,128)(2,1)S(1)}, u32[]{:S(2)}, u32[]{:S(2)}) %collective-permute-start.19) | collective-permute-done | bytes 32800 | tf_op jit(solution)/shard_map/ppermute | solution.py:562
  60.5 6.0 %shard_map.106.refs_9_ = f32[256,128]{1,0:T(8,128)} custom-call(bf16[128,128]{1,0:T(8,128)(2,1)} %copy-done.3, bf16[512,128]{1,0:T(8,128)(2,1)} %refs_8_.1, bf16[128,1152]{1,0:T(8,128)(2,1)} %get-tuple-element.55.piece_ref.refs_0_, bf16[128,2048]{1,0:T(8,128)(2,1)} %get-tuple-element.63.normed_ref, f32[128,128]{1,0:T(8,128)} %get-tuple-element.64.rscale_ref, ...), custom_call_target="tpu_custom_call" | custom-call | flops 1000000000 | bytes 7000000 | tf_op jit(solution)/shard_map/pallas_call | solution.py:380
  68.3 1.5 %shard_map.107 = (f32[4,80,512]{2,1,0:T(8,128)S(1)}, bf16[4,80,512]{2,1,0:T(8,128)(2,1)S(1)}) custom-call(bf16[128,1152]{1,0:T(8,128)(2,1)S(1)} %copy-done, bf16[128,1152]{1,0:T(8,128)(2,1)S(1)} %collective-permute-done.7.refs_1_, bf16[128,1152]{1,0:T(8,128)(2,1)S(1)} %collective-permute-done.8.refs_2_, ...), custom_call_target="tpu_custom_call" | custom-call | flops 600000000 | bytes 4000000 | tf_op jit(solution)/shard_map/pallas_call | solution.py:459
  69.9 1.6 %collective-permute-done.20.got_ref = bf16[4,80,512]{2,1,0:T(8,128)(2,1)S(1)} collective-permute-done((bf16[4,80,512]{2,1,0:T(8,128)(2,1)S(1)}, bf16[4,80,512]{2,1,0:T(8,128)(2,1)S(1)}, u32[]{:S(2)}, u32[]{:S(2)}) %collective-permute-start.20) | collective-permute-done | bytes 327712 | tf_op jit(solution)/shard_map/ppermute | solution.py:562
  72.5 3.5 %collective-permute-start.23 = (bf16[80,512]{1,0:T(8,128)(2,1)S(1)}, bf16[80,512]{1,0:T(8,128)(2,1)S(1)}, u32[]{:S(2)}, u32[]{:S(2)}) collective-permute-start(bf16[80,512]{1,0:T(8,128)(2,1)S(1)} %get-tuple-element.72), channel_id=1, source_target_pairs={{0,6},{1,7},{2,4},{3,5},{4,2},{5,3},{6,0},{7,1},{8,14},{9,15},{10,... | collective-permute-start | bytes 245768 | tf_op jit(solution)/shard_map/ppermute | solution.py:562
  76.0 1.2 %collective-permute-done.21.refs_0_ = bf16[80,512]{1,0:T(8,128)(2,1)S(1)} collective-permute-done((bf16[80,512]{1,0:T(8,128)(2,1)S(1)}, bf16[80,512]{1,0:T(8,128)(2,1)S(1)}, u32[]{:S(2)}, u32[]{:S(2)}) %collective-permute-start.21) | collective-permute-done | bytes 81952 | tf_op jit(solution)/shard_map/ppermute | solution.py:562
  77.2 4.3 %collective-permute-done.22.refs_1_ = bf16[80,512]{1,0:T(8,128)(2,1)S(1)} collective-permute-done((bf16[80,512]{1,0:T(8,128)(2,1)S(1)}, bf16[80,512]{1,0:T(8,128)(2,1)S(1)}, u32[]{:S(2)}, u32[]{:S(2)}) %collective-permute-start.22) | collective-permute-done | bytes 81952 | tf_op jit(solution)/shard_map/ppermute | solution.py:562
  81.5 1.3 %collective-permute-start.26 = (bf16[80,512]{1,0:T(8,128)(2,1)S(1)}, bf16[80,512]{1,0:T(8,128)(2,1)S(1)}, u32[]{:S(2)}, u32[]{:S(2)}) collective-permute-start(bf16[80,512]{1,0:T(8,128)(2,1)S(1)} %shard_map.109), channel_id=1, source_target_pairs={{0,6},{1,7},{2,4},{3,5},{4,2},{5,3},{6,0},{7,1},{8,14},{9,15},{10,... | collective-permute-start | bytes 245768 | tf_op jit(solution)/shard_map/ppermute | solution.py:562
  82.8 1.7 %collective-permute-start.25 = (bf16[80,512]{1,0:T(8,128)(2,1)S(1)}, bf16[80,512]{1,0:T(8,128)(2,1)S(1)}, u32[]{:S(2)}, u32[]{:S(2)}) collective-permute-start(bf16[80,512]{1,0:T(8,128)(2,1)S(1)} %shard_map.109), channel_id=1, source_target_pairs={{0,4},{1,5},{2,6},{3,7},{4,0},{5,1},{6,2},{7,3},{8,12},{9,13},{10,... | collective-permute-start | bytes 245768 | tf_op jit(solution)/shard_map/ppermute | solution.py:562
  84.5 1.4 %collective-permute-start.24 = (bf16[80,512]{1,0:T(8,128)(2,1)S(1)}, bf16[80,512]{1,0:T(8,128)(2,1)S(1)}, u32[]{:S(2)}, u32[]{:S(2)}) collective-permute-start(bf16[80,512]{1,0:T(8,128)(2,1)S(1)} %shard_map.109), channel_id=1, source_target_pairs={{0,2},{1,3},{2,0},{3,1},{4,6},{5,7},{6,4},{7,5},{8,10},{9,11},{10,... | collective-permute-start | bytes 245768 | tf_op jit(solution)/shard_map/ppermute | solution.py:562
  86.0 2.3 %collective-permute-done.26 = bf16[80,512]{1,0:T(8,128)(2,1)S(1)} collective-permute-done((bf16[80,512]{1,0:T(8,128)(2,1)S(1)}, bf16[80,512]{1,0:T(8,128)(2,1)S(1)}, u32[]{:S(2)}, u32[]{:S(2)}) %collective-permute-start.26) | collective-permute-done | bytes 81952 | tf_op jit(solution)/shard_map/ppermute | solution.py:562
  88.3 2.2 %collective-permute-done.25 = bf16[80,512]{1,0:T(8,128)(2,1)S(1)} collective-permute-done((bf16[80,512]{1,0:T(8,128)(2,1)S(1)}, bf16[80,512]{1,0:T(8,128)(2,1)S(1)}, u32[]{:S(2)}, u32[]{:S(2)}) %collective-permute-start.25) | collective-permute-done | bytes 81952 | tf_op jit(solution)/shard_map/ppermute | solution.py:562
  90.5 2.4 %collective-permute-start.29 = (bf16[320,512]{1,0:T(8,128)(2,1)S(1)}, bf16[320,512]{1,0:T(8,128)(2,1)S(1)}, u32[]{:S(2)}, u32[]{:S(2)}) collective-permute-start(bf16[320,512]{1,0:T(8,128)(2,1)S(1)} %pad_maximum_fusion.refs_0_), channel_id=1, source_target_pairs={{0,24},{8,16},{16,8},{24,0},{1,25},{9,17},{17,9},{25,1},{2,26},{10... | collective-permute-start | bytes 983048 | tf_op jit(solution)/shard_map/ppermute | solution.py:562
  94.1 8.0 %collective-permute-done.29.refs_3_ = bf16[320,512]{1,0:T(8,128)(2,1)S(1)} collective-permute-done((bf16[320,512]{1,0:T(8,128)(2,1)S(1)}, bf16[320,512]{1,0:T(8,128)(2,1)S(1)}, u32[]{:S(2)}, u32[]{:S(2)}) %collective-permute-start.29) | collective-permute-done | bytes 327712 | tf_op jit(solution)/shard_map/ppermute | solution.py:562
  102.1 4.5 %collective-permute-done.28.refs_2_ = bf16[320,512]{1,0:T(8,128)(2,1)S(1)} collective-permute-done((bf16[320,512]{1,0:T(8,128)(2,1)S(1)}, bf16[320,512]{1,0:T(8,128)(2,1)S(1)}, u32[]{:S(2)}, u32[]{:S(2)}) %collective-permute-start.28) | collective-permute-done | bytes 327712 | tf_op jit(solution)/shard_map/ppermute | solution.py:562
  107.1 1.1 collective-permute-done.32.refs_6_
  108.7 3.0 %shard_map.110 = (f32[256,128]{1,0:T(8,128)}, f32[2048,512]{1,0:T(8,128)}, f32[512,128]{1,0:T(8,128)}) custom-call(bf16[320,512]{1,0:T(8,128)(2,1)S(1)} %pad_maximum_fusion.refs_0_, bf16[320,512]{1,0:T(8,128)(2,1)S(1)} %collective-permute-done.27.refs_1_, bf16[320,512]{1,0:T(8,128)(2,1)S(1)} %collective-permute-done.28.refs_2_, ...), custom_call_target="tpu_custom_call" | custom-call | flops 1000000 | bytes 8000000 | tf_op jit(solution)/shard_map/pallas_call | solution.py:546
  (72 shorter events, 13.7 us)
Async XLA Ops:
  11.7 8.9 %collective-permute-start.5 = (bf16[128,128]{1,0:T(8,128)(2,1)}, bf16[128,128]{1,0:T(8,128)(2,1)S(1)}, u32[]{:S(2)}, u32[]{:S(2)}) collective-permute-start(bf16[128,128]{1,0:T(8,128)(2,1)} %get-tuple-element.40.refs_0_), channel_id=1, source_target_pairs={{0,6},{1,7},{2,4},{3,5},{4,2},{5,3},{6,0},{7,1},{8,14},{9,15},{10,... | collective-permute-start | bytes 98312 | tf_op jit(solution)/shard_map/ppermute | solution.py:562
  16.8 5.0 %collective-permute-start.4 = (bf16[128,128]{1,0:T(8,128)(2,1)}, bf16[128,128]{1,0:T(8,128)(2,1)S(1)}, u32[]{:S(2)}, u32[]{:S(2)}) collective-permute-start(bf16[128,128]{1,0:T(8,128)(2,1)} %get-tuple-element.40.refs_0_), channel_id=1, source_target_pairs={{0,4},{1,5},{2,6},{3,7},{4,0},{5,1},{6,2},{7,3},{8,12},{9,13},{10,... | collective-permute-start | bytes 98312 | tf_op jit(solution)/shard_map/ppermute | solution.py:562
  16.8 5.0 %collective-permute-start.3 = (bf16[128,128]{1,0:T(8,128)(2,1)}, bf16[128,128]{1,0:T(8,128)(2,1)S(1)}, u32[]{:S(2)}, u32[]{:S(2)}) collective-permute-start(bf16[128,128]{1,0:T(8,128)(2,1)} %get-tuple-element.40.refs_0_), channel_id=1, source_target_pairs={{0,2},{1,3},{2,0},{3,1},{4,6},{5,7},{6,4},{7,5},{8,10},{9,11},{10,... | collective-permute-start | bytes 98312 | tf_op jit(solution)/shard_map/ppermute | solution.py:562
  17.5 5.0 %collective-permute-start.2 = (bf16[128,128]{1,0:T(8,128)(2,1)}, bf16[128,128]{1,0:T(8,128)(2,1)S(1)}, u32[]{:S(2)}, u32[]{:S(2)}) collective-permute-start(bf16[128,128]{1,0:T(8,128)(2,1)} %get-tuple-element.40.refs_0_), channel_id=1, source_target_pairs={{0,24},{8,16},{16,8},{24,0},{1,25},{9,17},{17,9},{25,1},{2,26},{10... | collective-permute-start | bytes 98312 | tf_op jit(solution)/shard_map/ppermute | solution.py:562
  20.1 4.1 %collective-permute-start.1 = (bf16[128,128]{1,0:T(8,128)(2,1)}, bf16[128,128]{1,0:T(8,128)(2,1)S(1)}, u32[]{:S(2)}, u32[]{:S(2)}) collective-permute-start(bf16[128,128]{1,0:T(8,128)(2,1)} %get-tuple-element.40.refs_0_), channel_id=1, source_target_pairs={{0,16},{8,24},{16,0},{24,8},{1,17},{9,25},{17,1},{25,9},{2,18},{10... | collective-permute-start | bytes 98312 | tf_op jit(solution)/shard_map/ppermute | solution.py:562
  20.6 4.1 %collective-permute-start = (bf16[128,128]{1,0:T(8,128)(2,1)}, bf16[128,128]{1,0:T(8,128)(2,1)S(1)}, u32[]{:S(2)}, u32[]{:S(2)}) collective-permute-start(bf16[128,128]{1,0:T(8,128)(2,1)} %get-tuple-element.40.refs_0_), channel_id=1, source_target_pairs={{0,8},{8,0},{16,24},{24,16},{1,9},{9,1},{17,25},{25,17},{2,10},{10... | collective-permute-start | bytes 98312 | tf_op jit(solution)/shard_map/ppermute | solution.py:562
  25.8 3.6 %collective-permute-start.6 = (bf16[512,128]{1,0:T(8,128)(2,1)S(1)}, bf16[512,128]{1,0:T(8,128)(2,1)S(1)}, u32[]{:S(2)}, u32[]{:S(2)}) collective-permute-start(bf16[512,128]{1,0:T(8,128)(2,1)S(1)} %get-tuple-element.47.even_ref.refs_8_), channel_id=1, source_target_pairs={{0,1},{1,0},{2,3},{3,2},{4,5},{5,4},{6,7},{7,6},{8,9},{9,8},{10,11... | collective-permute-start | bytes 393224 | tf_op jit(solution)/shard_map/ppermute | solution.py:562
  25.9 40.7 %collective-permute-start.7 = (bf16[128,1152]{1,0:T(8,128)(2,1)}, bf16[128,1152]{1,0:T(8,128)(2,1)S(1)}, u32[]{:S(2)}, u32[]{:S(2)}) collective-permute-start(bf16[128,1152]{1,0:T(8,128)(2,1)} %get-tuple-element.56), channel_id=1, source_target_pairs={{0,8},{8,0},{16,24},{24,16},{1,9},{9,1},{17,25},{25,17},{2,10},{10... | collective-permute-start | bytes 884744 | tf_op jit(solution)/shard_map/ppermute | solution.py:562
  26.4 40.2 %collective-permute-start.8 = (bf16[128,1152]{1,0:T(8,128)(2,1)}, bf16[128,1152]{1,0:T(8,128)(2,1)S(1)}, u32[]{:S(2)}, u32[]{:S(2)}) collective-permute-start(bf16[128,1152]{1,0:T(8,128)(2,1)} %get-tuple-element.57), channel_id=1, source_target_pairs={{0,16},{8,24},{16,0},{24,8},{1,17},{9,25},{17,1},{25,9},{2,18},{10... | collective-permute-start | bytes 884744 | tf_op jit(solution)/shard_map/ppermute | solution.py:562
  28.1 38.6 %collective-permute-start.9 = (bf16[128,1152]{1,0:T(8,128)(2,1)}, bf16[128,1152]{1,0:T(8,128)(2,1)S(1)}, u32[]{:S(2)}, u32[]{:S(2)}) collective-permute-start(bf16[128,1152]{1,0:T(8,128)(2,1)} %get-tuple-element.58), channel_id=1, source_target_pairs={{0,24},{8,16},{16,8},{24,0},{1,25},{9,17},{17,9},{25,1},{2,26},{10... | collective-permute-start | bytes 884744 | tf_op jit(solution)/shard_map/ppermute | solution.py:562
  30.6 11.7 %collective-permute-start.15 = (f32[8,128]{1,0:T(8,128)S(1)}, f32[8,128]{1,0:T(8,128)S(1)}, u32[]{:S(2)}, u32[]{:S(2)}) collective-permute-start(f32[8,128]{1,0:T(8,128)S(1)} %get-tuple-element.59.refs_4_), channel_id=1, source_target_pairs={{0,6},{1,7},{2,4},{3,5},{4,2},{5,3},{6,0},{7,1},{8,14},{9,15},{10,... | collective-permute-start | bytes 12296 | tf_op jit(solution)/shard_map/ppermute | solution.py:562
  34.2 3.6 %collective-permute-start.13 = (f32[8,128]{1,0:T(8,128)S(1)}, f32[8,128]{1,0:T(8,128)S(1)}, u32[]{:S(2)}, u32[]{:S(2)}) collective-permute-start(f32[8,128]{1,0:T(8,128)S(1)} %get-tuple-element.59.refs_4_), channel_id=1, source_target_pairs={{0,2},{1,3},{2,0},{3,1},{4,6},{5,7},{6,4},{7,5},{8,10},{9,11},{10,... | collective-permute-start | bytes 12296 | tf_op jit(solution)/shard_map/ppermute | solution.py:562
  37.8 4.5 %collective-permute-start.14 = (f32[8,128]{1,0:T(8,128)S(1)}, f32[8,128]{1,0:T(8,128)S(1)}, u32[]{:S(2)}, u32[]{:S(2)}) collective-permute-start(f32[8,128]{1,0:T(8,128)S(1)} %get-tuple-element.59.refs_4_), channel_id=1, source_target_pairs={{0,4},{1,5},{2,6},{3,7},{4,0},{5,1},{6,2},{7,3},{8,12},{9,13},{10,... | collective-permute-start | bytes 12296 | tf_op jit(solution)/shard_map/ppermute | solution.py:562
  42.3 11.9 %collective-permute-start.16 = (f32[32,128]{1,0:T(8,128)S(1)}, f32[32,128]{1,0:T(8,128)S(1)}, u32[]{:S(2)}, u32[]{:S(2)}) collective-permute-start(f32[32,128]{1,0:T(8,128)S(1)} %constant_dynamic-update-slice_fusion.refs_10_), channel_id=1, source_target_pairs={{0,1},{1,0},{2,3},{3,2},{4,5},{5,4},{6,7},{7,6},{8,9},{9,8},{10,11... | collective-permute-start | bytes 49160 | tf_op jit(solution)/shard_map/ppermute | solution.py:562
  42.4 4.6 %collective-permute-start.12 = (f32[8,128]{1,0:T(8,128)S(1)}, f32[8,128]{1,0:T(8,128)S(1)}, u32[]{:S(2)}, u32[]{:S(2)}) collective-permute-start(f32[8,128]{1,0:T(8,128)S(1)} %get-tuple-element.59.refs_4_), channel_id=1, source_target_pairs={{0,24},{8,16},{16,8},{24,0},{1,25},{9,17},{17,9},{25,1},{2,26},{10... | collective-permute-start | bytes 12296 | tf_op jit(solution)/shard_map/ppermute | solution.py:562
  47.0 3.6 %collective-permute-start.11 = (f32[8,128]{1,0:T(8,128)S(1)}, f32[8,128]{1,0:T(8,128)S(1)}, u32[]{:S(2)}, u32[]{:S(2)}) collective-permute-start(f32[8,128]{1,0:T(8,128)S(1)} %get-tuple-element.59.refs_4_), channel_id=1, source_target_pairs={{0,16},{8,24},{16,0},{24,8},{1,17},{9,25},{17,1},{25,9},{2,18},{10... | collective-permute-start | bytes 12296 | tf_op jit(solution)/shard_map/ppermute | solution.py:562
  50.6 3.6 %collective-permute-start.10 = (f32[8,128]{1,0:T(8,128)S(1)}, f32[8,128]{1,0:T(8,128)S(1)}, u32[]{:S(2)}, u32[]{:S(2)}) collective-permute-start(f32[8,128]{1,0:T(8,128)S(1)} %get-tuple-element.59.refs_4_), channel_id=1, source_target_pairs={{0,8},{8,0},{16,24},{24,16},{1,9},{9,1},{17,25},{25,17},{2,10},{10... | collective-permute-start | bytes 12296 | tf_op jit(solution)/shard_map/ppermute | solution.py:562
  55.0 5.0 %collective-permute-start.19 = (bf16[128,128]{1,0:T(8,128)(2,1)S(1)}, bf16[128,128]{1,0:T(8,128)(2,1)S(1)}, u32[]{:S(2)}, u32[]{:S(2)}) collective-permute-start(bf16[128,128]{1,0:T(8,128)(2,1)S(1)} %shard_map.105.raw_ref.refs_4_), channel_id=1, source_target_pairs={{0,24},{8,16},{16,8},{24,0},{1,25},{9,17},{17,9},{25,1},{2,26},{10... | collective-permute-start | bytes 98312 | tf_op jit(solution)/shard_map/ppermute | solution.py:562
  56.6 10.0 %collective-permute-start.18 = (bf16[128,128]{1,0:T(8,128)(2,1)S(1)}, bf16[128,128]{1,0:T(8,128)(2,1)S(1)}, u32[]{:S(2)}, u32[]{:S(2)}) collective-permute-start(bf16[128,128]{1,0:T(8,128)(2,1)S(1)} %shard_map.105.raw_ref.refs_4_), channel_id=1, source_target_pairs={{0,16},{8,24},{16,0},{24,8},{1,17},{9,25},{17,1},{25,9},{2,18},{10... | collective-permute-start | bytes 98312 | tf_op jit(solution)/shard_map/ppermute | solution.py:562
  60.0 6.6 %collective-permute-start.17 = (bf16[128,128]{1,0:T(8,128)(2,1)S(1)}, bf16[128,128]{1,0:T(8,128)(2,1)S(1)}, u32[]{:S(2)}, u32[]{:S(2)}) collective-permute-start(bf16[128,128]{1,0:T(8,128)(2,1)S(1)} %shard_map.105.raw_ref.refs_4_), channel_id=1, source_target_pairs={{0,8},{8,0},{16,24},{24,16},{1,9},{9,1},{17,25},{25,17},{2,10},{10... | collective-permute-start | bytes 98312 | tf_op jit(solution)/shard_map/ppermute | solution.py:562
  71.6 5.6 %collective-permute-start.21 = (bf16[80,512]{1,0:T(8,128)(2,1)S(1)}, bf16[80,512]{1,0:T(8,128)(2,1)S(1)}, u32[]{:S(2)}, u32[]{:S(2)}) collective-permute-start(bf16[80,512]{1,0:T(8,128)(2,1)S(1)} %get-tuple-element.70), channel_id=1, source_target_pairs={{0,2},{1,3},{2,0},{3,1},{4,6},{5,7},{6,4},{7,5},{8,10},{9,11},{10,... | collective-permute-start | bytes 245768 | tf_op jit(solution)/shard_map/ppermute | solution.py:562
  71.7 9.8 %collective-permute-start.22 = (bf16[80,512]{1,0:T(8,128)(2,1)S(1)}, bf16[80,512]{1,0:T(8,128)(2,1)S(1)}, u32[]{:S(2)}, u32[]{:S(2)}) collective-permute-start(bf16[80,512]{1,0:T(8,128)(2,1)S(1)} %get-tuple-element.71), channel_id=1, source_target_pairs={{0,4},{1,5},{2,6},{3,7},{4,0},{5,1},{6,2},{7,3},{8,12},{9,13},{10,... | collective-permute-start | bytes 245768 | tf_op jit(solution)/shard_map/ppermute | solution.py:562
  72.5 8.9 %collective-permute-start.23 = (bf16[80,512]{1,0:T(8,128)(2,1)S(1)}, bf16[80,512]{1,0:T(8,128)(2,1)S(1)}, u32[]{:S(2)}, u32[]{:S(2)}) collective-permute-start(bf16[80,512]{1,0:T(8,128)(2,1)S(1)} %get-tuple-element.72), channel_id=1, source_target_pairs={{0,6},{1,7},{2,4},{3,5},{4,2},{5,3},{6,0},{7,1},{8,14},{9,15},{10,... | collective-permute-start | bytes 245768 | tf_op jit(solution)/shard_map/ppermute | solution.py:562
  81.5 6.8 %collective-permute-start.26 = (bf16[80,512]{1,0:T(8,128)(2,1)S(1)}, bf16[80,512]{1,0:T(8,128)(2,1)S(1)}, u32[]{:S(2)}, u32[]{:S(2)}) collective-permute-start(bf16[80,512]{1,0:T(8,128)(2,1)S(1)} %shard_map.109), channel_id=1, source_target_pairs={{0,6},{1,7},{2,4},{3,5},{4,2},{5,3},{6,0},{7,1},{8,14},{9,15},{10,... | collective-permute-start | bytes 245768 | tf_op jit(solution)/shard_map/ppermute | solution.py:562
  82.8 7.7 %collective-permute-start.25 = (bf16[80,512]{1,0:T(8,128)(2,1)S(1)}, bf16[80,512]{1,0:T(8,128)(2,1)S(1)}, u32[]{:S(2)}, u32[]{:S(2)}) collective-permute-start(bf16[80,512]{1,0:T(8,128)(2,1)S(1)} %shard_map.109), channel_id=1, source_target_pairs={{0,4},{1,5},{2,6},{3,7},{4,0},{5,1},{6,2},{7,3},{8,12},{9,13},{10,... | collective-permute-start | bytes 245768 | tf_op jit(solution)/shard_map/ppermute | solution.py:562
  84.5 6.0 %collective-permute-start.24 = (bf16[80,512]{1,0:T(8,128)(2,1)S(1)}, bf16[80,512]{1,0:T(8,128)(2,1)S(1)}, u32[]{:S(2)}, u32[]{:S(2)}) collective-permute-start(bf16[80,512]{1,0:T(8,128)(2,1)S(1)} %shard_map.109), channel_id=1, source_target_pairs={{0,2},{1,3},{2,0},{3,1},{4,6},{5,7},{6,4},{7,5},{8,10},{9,11},{10,... | collective-permute-start | bytes 245768 | tf_op jit(solution)/shard_map/ppermute | solution.py:562
  90.5 11.6 %collective-permute-start.29 = (bf16[320,512]{1,0:T(8,128)(2,1)S(1)}, bf16[320,512]{1,0:T(8,128)(2,1)S(1)}, u32[]{:S(2)}, u32[]{:S(2)}) collective-permute-start(bf16[320,512]{1,0:T(8,128)(2,1)S(1)} %pad_maximum_fusion.refs_0_), channel_id=1, source_target_pairs={{0,24},{8,16},{16,8},{24,0},{1,25},{9,17},{17,9},{25,1},{2,26},{10... | collective-permute-start | bytes 983048 | tf_op jit(solution)/shard_map/ppermute | solution.py:562
  93.0 13.7 %collective-permute-start.28 = (bf16[320,512]{1,0:T(8,128)(2,1)S(1)}, bf16[320,512]{1,0:T(8,128)(2,1)S(1)}, u32[]{:S(2)}, u32[]{:S(2)}) collective-permute-start(bf16[320,512]{1,0:T(8,128)(2,1)S(1)} %pad_maximum_fusion.refs_0_), channel_id=1, source_target_pairs={{0,16},{8,24},{16,0},{24,8},{1,17},{9,25},{17,1},{25,9},{2,18},{10... | collective-permute-start | bytes 983048 | tf_op jit(solution)/shard_map/ppermute | solution.py:562
  93.5 13.1 %collective-permute-start.27 = (bf16[320,512]{1,0:T(8,128)(2,1)S(1)}, bf16[320,512]{1,0:T(8,128)(2,1)S(1)}, u32[]{:S(2)}, u32[]{:S(2)}) collective-permute-start(bf16[320,512]{1,0:T(8,128)(2,1)S(1)} %pad_maximum_fusion.refs_0_), channel_id=1, source_target_pairs={{0,8},{8,0},{16,24},{24,16},{1,9},{9,1},{17,25},{25,17},{2,10},{10... | collective-permute-start | bytes 983048 | tf_op jit(solution)/shard_map/ppermute | solution.py:562
  94.1 13.0 %collective-permute-start.30 = (bf16[320,512]{1,0:T(8,128)(2,1)S(1)}, bf16[320,512]{1,0:T(8,128)(2,1)S(1)}, u32[]{:S(2)}, u32[]{:S(2)}) collective-permute-start(bf16[320,512]{1,0:T(8,128)(2,1)S(1)} %pad_maximum_fusion.refs_0_), channel_id=1, source_target_pairs={{0,1},{1,0},{2,3},{3,2},{4,5},{5,4},{6,7},{7,6},{8,9},{9,8},{10,11... | collective-permute-start | bytes 983048 | tf_op jit(solution)/shard_map/ppermute | solution.py:562
  102.1 5.0 %collective-permute-start.33 = (bf16[320,512]{1,0:T(8,128)(2,1)S(1)}, bf16[320,512]{1,0:T(8,128)(2,1)S(1)}, u32[]{:S(2)}, u32[]{:S(2)}) collective-permute-start(bf16[320,512]{1,0:T(8,128)(2,1)S(1)} %collective-permute-done.29.refs_3_), channel_id=1, source_target_pairs={{0,1},{1,0},{2,3},{3,2},{4,5},{5,4},{6,7},{7,6},{8,9},{9,8},{10,11... | collective-permute-start | bytes 983048 | tf_op jit(solution)/shard_map/ppermute | solution.py:562
  106.6 2.1 %collective-permute-start.31 = (bf16[320,512]{1,0:T(8,128)(2,1)S(1)}, bf16[320,512]{1,0:T(8,128)(2,1)S(1)}, u32[]{:S(2)}, u32[]{:S(2)}) collective-permute-start(bf16[320,512]{1,0:T(8,128)(2,1)S(1)} %collective-permute-done.27.refs_1_), channel_id=1, source_target_pairs={{0,1},{1,0},{2,3},{3,2},{4,5},{5,4},{6,7},{7,6},{8,9},{9,8},{10,11... | collective-permute-start | bytes 983048 | tf_op jit(solution)/shard_map/ppermute | solution.py:562
  (13 other events, 167.3 us)

commit v4 on v3

--- a/solution.py
+++ b/solution.py
@@ -9,12 +9,14 @@
 from jax.experimental.pallas import tpu as pltpu
 from jax.sharding import PartitionSpec as P
 
+
 SCALE = 10.0
 SUB = 8
 BF16 = jnp.bfloat16
 F32 = jnp.float32
 VMEM = pl.BlockSpec(memory_space=pltpu.VMEM)
 ANY = pl.BlockSpec(memory_space=pl.ANY)
+HBM = pl.BlockSpec(memory_space=pltpu.MemorySpace.HBM)
 
 
 def shape(dims, dtype):
@@ -273,7 +275,7 @@
     pieces, rest = refs[:size], refs[size:]
     stats, rest = rest[:size], rest[size:]
     (even_ref, odd_ref, even_stats, odd_stats, local_ref, unit32_ref, norm_ref, out_ref) = rest
-    count, embed = local_ref.shape
+    count, _ = local_ref.shape
     coef = SCALE / count
     units = pieces[0][...]
     keyterm = None
@@ -324,37 +326,55 @@
     freqs,
     columns,
     raw_ref,
-    out_w_ref,
-    piece_ref,
-    normed_ref,
-    rscale_ref,
+    out_w_hbm,
+    piece_hbm,
+    normed_hbm,
+    rscale_hbm,
     in_hbm,
     mixed_hbm,
     spec_hbm,
     g_mix_ref,
+    out_w,
+    slope,
     in_w,
+    normed,
+    rscale,
     mixed,
     spec,
     grad_feat,
     sems,
 ):
+    deep, width, _ = columns
+    sources = [
+        out_w_hbm,
+        piece_hbm.at[:, deep : deep + width],
+        in_hbm,
+        normed_hbm,
+        rscale_hbm,
+        mixed_hbm,
+        spec_hbm,
+    ]
+    targets = [out_w, slope, in_w, normed, rscale, mixed, spec]
     loads = [
         pltpu.make_async_copy(source, target, sems.at[i])
-        for i, (source, target) in enumerate([(in_hbm, in_w), (mixed_hbm, mixed), (spec_hbm, spec)])
+        for i, (source, target) in enumerate(zip(sources, targets))
     ]
     for each in loads:
         each.start()
-    deep, width, _ = columns
-    grad_pre = pre_grads(raw_ref[...], out_w_ref[...], piece_ref[:, deep : deep + width])
     loads[0].wait()
+    loads[1].wait()
+    grad_pre = pre_grads(raw_ref[...], out_w[...], slope[...])
+    loads[2].wait()
     grad_norm = mm_nt(grad_pre, in_w[...])
-    xhat = normed_ref[...].astype(F32)
+    loads[3].wait()
+    loads[4].wait()
+    xhat = normed[...].astype(F32)
     mean = jnp.mean(grad_norm, axis=1, keepdims=True)
-    slope = jnp.mean(grad_norm * xhat, axis=1, keepdims=True)
-    grad_feat[...] = rscale_ref[:, :1] * (grad_norm - mean - xhat * slope)
-    loads[1].wait()
-    loads[2].wait()
-    groups, rows, filters = mixed.shape
+    tilt = jnp.mean(grad_norm * xhat, axis=1, keepdims=True)
+    grad_feat[...] = rscale[:, :1] * (grad_norm - mean - xhat * tilt)
+    loads[5].wait()
+    loads[6].wait()
+    groups, _, filters = mixed.shape
     half = freqs * SUB
 
     def one(g, total):
@@ -375,21 +395,25 @@
 
 def lower(grad_raw, w_out, piece, normed, rscale, w_in, mixed, spec, freqs, columns):
     count, feats = normed.shape
-    groups, rows, filters = mixed.shape
+    _, _, filters = mixed.shape
     lanes = spec.shape[2]
     return pl.pallas_call(
         functools.partial(lower_kernel, freqs, columns),
-        in_specs=[VMEM] * 5 + [ANY] * 3,
+        in_specs=[VMEM] + [HBM] * 7,
         out_shape=shape((lanes, filters), F32),
         out_specs=VMEM,
         scratch_shapes=[
+            pltpu.VMEM(w_out.shape, BF16),
+            pltpu.VMEM((count, columns[1]), BF16),
             pltpu.VMEM(w_in.shape, BF16),
+            pltpu.VMEM((count, feats), BF16),
+            pltpu.VMEM(rscale.shape, F32),
             pltpu.VMEM(mixed.shape, F32),
             pltpu.VMEM(spec.shape, BF16),
             pltpu.VMEM((count, feats), F32),
-            pltpu.SemaphoreType.DMA((3,)),
+            pltpu.SemaphoreType.DMA((7,)),
         ],
-        compiler_params=params(60),
+        compiler_params=params(20),
         cost_estimate=cost(1e9, 7e6),
     )(grad_raw, w_out, piece, normed, rscale, w_in, mixed, spec)
 
@@ -581,23 +605,24 @@
     spec, mixed, units, unit32, norms, rscale, normed, *early = encode(
         patches, w_mix, w_in, w_out, size
     )
+    stacked = spread(units, "dp", along)
     pieces = spread(units, "blk", across)
-    stacked = spread(units, "dp", along)
     pieces[1:], stacked[1:] = lax.optimization_barrier((pieces[1:], stacked[1:]))
-    early = lax.optimization_barrier((early, pieces[1:]))[0]
     zneg, numer, even = negatives(pieces, stacked[1:])
     odd = swap(even, "dp", 1)
+    local, stats, loss = positives(partner_dev, partner_row, even, odd, zneg, numer)
+    dp_stats = spread(stats, "dp", along)
+    group_stats = spread(stats, "blk", across)
+    dp_stats[1:], group_stats[1:] = lax.optimization_barrier((dp_stats[1:], group_stats[1:]))
     factors = [early[0]] + [swap(early[hop], "blk", hop) for hop in across]
-    local, stats, loss = positives(partner_dev, partner_row, even, odd, zneg, numer)
-    group_stats = spread(stats, "blk", across)
-    even_stats = jnp.concatenate(spread(stats, "dp", along), axis=0)
+    even_stats = jnp.concatenate(dp_stats, axis=0)
     odd_stats = swap(even_stats, "dp", 1)
     grad_raw = upper(pieces, group_stats, even, odd, even_stats, odd_stats, local, unit32, norms)
     raws = spread(grad_raw, "blk", across)
     g_mix = lower(grad_raw, w_out, early[0], normed, rscale, w_in, mixed, spec, freqs, columns)
-
     keep, away = weight_grads(lay, columns, factors, raws, w_out, g_mix)
-    own, *sends = pair_sum(keep, swap(away, "dp", 1))
+    got = swap(away, "dp", 1)
+    own, *sends = pair_sum(keep, got)
     got = [swap(block, "dp", hop) for block, hop in zip(sends, along)]
     share = total_sum(own, got)
     plane = jnp.concatenate(spread(share, "dp", along), axis=0)

time: 112 us -> 105 us (0.938)
  waiting for transfers between devices: 48.6 us -> 39.3 us
  local copies, waits for them, and re-layouts: 2.45 us -> 6.69 us
  Pallas kernels: 23.9 us -> 21.3 us
    ppermute x34, waiting for transfers between devices: 48.6 us -> 39.3 us  [swap(): return lax.ppermute(block, axis, [(src, src ^ bit) for src in range(size)])]
    unnamed x25 -> x29, local copies, waits for them, and re-layouts: 2.45 us -> 6.69 us
    pallas_call x1, Pallas kernels: 6.04 us -> 3.41 us  [lower(): pl.pallas_call(functools.partial(lower_kernel, freqs, columns), in_specs=...]
  transfers between devices with their start and end apart: 34 -> 34, of which waited for: 19 -> 17; matrix products, arithmetic and copies ran while one was open for 0% -> 0% of each run, Pallas kernels for 7% -> 4%
where the time goes in v4:
time: 105 us
  waiting for transfers between devices  39.3 us (37%)
  starting transfers between devices  36.4 us (35%)
  Pallas kernels  21.3 us (20%)
  local copies, waits for them, and re-layouts  6.69 us (6%)
    ppermute x34, waiting for transfers between devices, swap(): return lax.ppermute(block, axis, [(src, src ^ bit) for src in range(size)])  39.3 us
    ppermute x34, starting transfers between devices, swap(): return lax.ppermute(block, axis, [(src, src ^ bit) for src in range(size)])  36.4 us
    pallas_call x1, Pallas kernels, encode(): pl.pallas_call(functools.partial(encode_kernel, freqs, size), grid=(count...  11.1 us
    unnamed x29, local copies, waits for them, and re-layouts  6.69 us
    pallas_call x1, Pallas kernels, lower(): pl.pallas_call(functools.partial(lower_kernel, freqs, columns), in_specs=...  3.41 us
    pallas_call x1, Pallas kernels, finish(): pl.pallas_call(functools.partial(finish_kernel, lay), in_specs=[VMEM] * (...  3.02 us
  transfers between devices with their start and end apart: 34, of which 17 were waited for; matrix products, arithmetic and copies ran while one was open for 0% of the time, Pallas kernels for 4%

profile of v4, /device:TPU:0, one launch (start us, length us, event | category | flops | bytes accessed | tf_op | source)
XLA Modules:
  0.0 104.6 jit_solution(11404689347155577505)
XLA Ops:
  0.7 11.1 %shard_map.102 = (bf16[16,256,256]{2,1,0:T(8,128)(2,1)}, f32[16,256,128]{2,1,0:T(8,128)}, bf16[128,128]{1,0:T(8,128)(2,1)}, f32[128,128]{1,0:T(8,128)}, f32[128,...) custom-call(bf16[128,64,256]{2,1,0:T(8,128)(2,1)} %patch_ref.1, ...), custom_call_target="tpu_custom_call" | custom-call | flops 3000000000 | bytes 14000000 | tf_op jit(solution)/shard_map/pallas_call | solution.py:159
  11.8 5.1 %collective-permute-start.5 = (bf16[128,128]{1,0:T(8,128)(2,1)}, bf16[128,128]{1,0:T(8,128)(2,1)S(1)}, u32[]{:S(2)}, u32[]{:S(2)}) collective-permute-start(bf16[128,128]{1,0:T(8,128)(2,1)} %get-tuple-element.42.refs_0_), channel_id=1, source_target_pairs={{0,6},{1,7},{2,4},{3,5},{4,2},{5,3},{6,0},{7,1},{8,14},{9,15},{10,... | collective-permute-start | bytes 98312 | tf_op jit(solution)/shard_map/ppermute | solution.py:586
  17.6 2.6 %collective-permute-start.2 = (bf16[128,128]{1,0:T(8,128)(2,1)}, bf16[128,128]{1,0:T(8,128)(2,1)S(1)}, u32[]{:S(2)}, u32[]{:S(2)}) collective-permute-start(bf16[128,128]{1,0:T(8,128)(2,1)} %get-tuple-element.42.refs_0_), channel_id=1, source_target_pairs={{0,24},{8,16},{16,8},{24,0},{1,25},{9,17},{17,9},{25,1},{2,26},{10... | collective-permute-start | bytes 98312 | tf_op jit(solution)/shard_map/ppermute | solution.py:586
  22.6 1.7 %collective-permute-done.1.refs_2_ = bf16[128,128]{1,0:T(8,128)(2,1)S(1)} collective-permute-done((bf16[128,128]{1,0:T(8,128)(2,1)}, bf16[128,128]{1,0:T(8,128)(2,1)S(1)}, u32[]{:S(2)}, u32[]{:S(2)}) %collective-permute-start.1) | collective-permute-done | bytes 32800 | tf_op jit(solution)/shard_map/ppermute | solution.py:586
  26.0 1.3 %collective-permute-done.6.odd_ref.refs_9_ = bf16[512,128]{1,0:T(8,128)(2,1)S(1)} collective-permute-done((bf16[512,128]{1,0:T(8,128)(2,1)S(1)}, bf16[512,128]{1,0:T(8,128)(2,1)S(1)}, u32[]{:S(2)}, u32[]{:S(2)}) %collective-permute-start.6) | collective-permute-done | bytes 131104 | tf_op jit(solution)/shard_map/ppermute | solution.py:586
  27.3 1.1 %shard_map.104 = (f32[128,128]{1,0:T(8,128)S(1)}, f32[8,128]{1,0:T(8,128)S(1)}, f32[1,128]{1,0:T(1,128)}) custom-call(s32[1,128]{1,0:T(1,128)S(1)} %bitcast.3, s32[1,128]{1,0:T(1,128)S(1)} %bitcast.4, bf16[512,128]{1,0:T(8,128)(2,1)S(1)} %get-tuple-element.49.even_ref.refs_8_, bf16[512,128]{1,0:T(8,128)(2,1)S(1)} %collective-permute-done.6.odd_ref.refs_9_, ...), custom_call_target="tpu_custom_call" | custom-call | flops 400000000 | bytes 1000000 | tf_op jit(solution)/shard_map/pallas_call | solution.py:264
  28.4 1.5 %collective-permute-start.15 = (f32[8,128]{1,0:T(8,128)S(1)}, f32[8,128]{1,0:T(8,128)S(1)}, u32[]{:S(2)}, u32[]{:S(2)}) collective-permute-start(f32[8,128]{1,0:T(8,128)S(1)} %get-tuple-element.57.refs_4_), channel_id=1, source_target_pairs={{0,24},{8,16},{16,8},{24,0},{1,25},{9,17},{17,9},{25,1},{2,26},{10... | collective-permute-start | bytes 12296 | tf_op jit(solution)/shard_map/ppermute | solution.py:586
  30.3 1.6 %collective-permute-start.13 = (f32[8,128]{1,0:T(8,128)S(1)}, f32[8,128]{1,0:T(8,128)S(1)}, u32[]{:S(2)}, u32[]{:S(2)}) collective-permute-start(f32[8,128]{1,0:T(8,128)S(1)} %get-tuple-element.57.refs_4_), channel_id=1, source_target_pairs={{0,8},{8,0},{16,24},{24,16},{1,9},{9,1},{17,25},{25,17},{2,10},{10... | collective-permute-start | bytes 12296 | tf_op jit(solution)/shard_map/ppermute | solution.py:586
  31.9 3.6 %collective-permute-start.12 = (f32[8,128]{1,0:T(8,128)S(1)}, f32[8,128]{1,0:T(8,128)S(1)}, u32[]{:S(2)}, u32[]{:S(2)}) collective-permute-start(f32[8,128]{1,0:T(8,128)S(1)} %get-tuple-element.57.refs_4_), channel_id=1, source_target_pairs={{0,6},{1,7},{2,4},{3,5},{4,2},{5,3},{6,0},{7,1},{8,14},{9,15},{10,... | collective-permute-start | bytes 12296 | tf_op jit(solution)/shard_map/ppermute | solution.py:586
  36.7 1.7 %collective-permute-start.8 = (bf16[128,1152]{1,0:T(8,128)(2,1)}, bf16[128,1152]{1,0:T(8,128)(2,1)S(1)}, u32[]{:S(2)}, u32[]{:S(2)}) collective-permute-start(bf16[128,1152]{1,0:T(8,128)(2,1)} %get-tuple-element.55), channel_id=1, source_target_pairs={{0,16},{8,24},{16,0},{24,8},{1,17},{9,25},{17,1},{25,9},{2,18},{10... | collective-permute-start | bytes 884744 | tf_op jit(solution)/shard_map/ppermute | solution.py:586
  38.4 1.4 %collective-permute-start.9 = (bf16[128,1152]{1,0:T(8,128)(2,1)}, bf16[128,1152]{1,0:T(8,128)(2,1)S(1)}, u32[]{:S(2)}, u32[]{:S(2)}) collective-permute-start(bf16[128,1152]{1,0:T(8,128)(2,1)} %get-tuple-element.56), channel_id=1, source_target_pairs={{0,24},{8,16},{16,8},{24,0},{1,25},{9,17},{17,9},{25,1},{2,26},{10... | collective-permute-start | bytes 884744 | tf_op jit(solution)/shard_map/ppermute | solution.py:586
  40.1 1.2 %collective-permute-done.16.refs_11_ = f32[32,128]{1,0:T(8,128)S(1)} collective-permute-done((f32[32,128]{1,0:T(8,128)S(1)}, f32[32,128]{1,0:T(8,128)S(1)}, u32[]{:S(2)}, u32[]{:S(2)}) %collective-permute-start.16) | collective-permute-done | bytes 16416 | tf_op jit(solution)/shard_map/ppermute | solution.py:586
  44.5 1.6 %collective-permute-start.19 = (bf16[128,128]{1,0:T(8,128)(2,1)S(1)}, bf16[128,128]{1,0:T(8,128)(2,1)S(1)}, u32[]{:S(2)}, u32[]{:S(2)}) collective-permute-start(bf16[128,128]{1,0:T(8,128)(2,1)S(1)} %shard_map.105.raw_ref.refs_4_), channel_id=1, source_target_pairs={{0,24},{8,16},{16,8},{24,0},{1,25},{9,17},{17,9},{25,1},{2,26},{10... | collective-permute-start | bytes 98312 | tf_op jit(solution)/shard_map/ppermute | solution.py:586
  46.6 5.5 %collective-permute-done.19.refs_7_ = bf16[128,128]{1,0:T(8,128)(2,1)S(1)} collective-permute-done((bf16[128,128]{1,0:T(8,128)(2,1)S(1)}, bf16[128,128]{1,0:T(8,128)(2,1)S(1)}, u32[]{:S(2)}, u32[]{:S(2)}) %collective-permute-start.19) | collective-permute-done | bytes 32800 | tf_op jit(solution)/shard_map/ppermute | solution.py:586
  52.6 1.6 %copy-done.2 = f32[16,256,128]{2,1,0:T(8,128)S(1)} copy-done((f32[16,256,128]{2,1,0:T(8,128)S(1)}, f32[16,256,128]{2,1,0:T(8,128)}, u32[]{:S(2)}) %copy-start.2) | copy-done | bytes 2097176
  54.2 1.0 copy-done.3
  56.1 3.4 %shard_map.106.refs_9_ = f32[256,128]{1,0:T(8,128)S(1)} custom-call(bf16[128,128]{1,0:T(8,128)(2,1)S(1)} %shard_map.105.raw_ref.refs_4_, bf16[512,128]{1,0:T(8,128)(2,1)S(1)} %copy-done.5, bf16[128,1152]{1,0:T(8,128)(2,1)S(1)} %copy-done.4, bf16[128,2048]{1,0:T(8,128)(2,1)S(1)} %copy-done.3, f32[128,128]{1,0:T(8,128)S(1)} %copy-done.6, ...), custom_call_target="tpu_custom_call" | custom-call | flops 1000000000 | bytes 7000000 | tf_op jit(solution)/shard_map/pallas_call | solution.py:400
  59.6 1.5 %shard_map.107 = (f32[4,80,512]{2,1,0:T(8,128)S(1)}, bf16[4,80,512]{2,1,0:T(8,128)(2,1)S(1)}) custom-call(bf16[128,1152]{1,0:T(8,128)(2,1)S(1)} %copy-done.4, bf16[128,1152]{1,0:T(8,128)(2,1)S(1)} %collective-permute-done.7.refs_1_, bf16[128,1152]{1,0:T(8,128)(2,1)S(1)} %collective-permute-done.8.refs_2_, ...), custom_call_target="tpu_custom_call" | custom-call | flops 600000000 | bytes 4000000 | tf_op jit(solution)/shard_map/pallas_call | solution.py:483
  61.1 1.6 %collective-permute-done.20.got_ref = bf16[4,80,512]{2,1,0:T(8,128)(2,1)S(1)} collective-permute-done((bf16[4,80,512]{2,1,0:T(8,128)(2,1)S(1)}, bf16[4,80,512]{2,1,0:T(8,128)(2,1)S(1)}, u32[]{:S(2)}, u32[]{:S(2)}) %collective-permute-start.20) | collective-permute-done | bytes 327712 | tf_op jit(solution)/shard_map/ppermute | solution.py:586
  62.8 1.5 %collective-permute-start.21 = (bf16[80,512]{1,0:T(8,128)(2,1)S(1)}, bf16[80,512]{1,0:T(8,128)(2,1)S(1)}, u32[]{:S(2)}, u32[]{:S(2)}) collective-permute-start(bf16[80,512]{1,0:T(8,128)(2,1)S(1)} %get-tuple-element.74), channel_id=1, source_target_pairs={{0,2},{1,3},{2,0},{3,1},{4,6},{5,7},{6,4},{7,5},{8,10},{9,11},{10,... | collective-permute-start | bytes 245768 | tf_op jit(solution)/shard_map/ppermute | solution.py:586
  64.3 2.6 %collective-permute-start.22 = (bf16[80,512]{1,0:T(8,128)(2,1)S(1)}, bf16[80,512]{1,0:T(8,128)(2,1)S(1)}, u32[]{:S(2)}, u32[]{:S(2)}) collective-permute-start(bf16[80,512]{1,0:T(8,128)(2,1)S(1)} %get-tuple-element.75), channel_id=1, source_target_pairs={{0,4},{1,5},{2,6},{3,7},{4,0},{5,1},{6,2},{7,3},{8,12},{9,13},{10,... | collective-permute-start | bytes 245768 | tf_op jit(solution)/shard_map/ppermute | solution.py:586
  67.4 6.4 %collective-permute-done.22.refs_1_ = bf16[80,512]{1,0:T(8,128)(2,1)S(1)} collective-permute-done((bf16[80,512]{1,0:T(8,128)(2,1)S(1)}, bf16[80,512]{1,0:T(8,128)(2,1)S(1)}, u32[]{:S(2)}, u32[]{:S(2)}) %collective-permute-start.22) | collective-permute-done | bytes 81952 | tf_op jit(solution)/shard_map/ppermute | solution.py:586
  73.8 2.5 %collective-permute-start.26 = (bf16[80,512]{1,0:T(8,128)(2,1)S(1)}, bf16[80,512]{1,0:T(8,128)(2,1)S(1)}, u32[]{:S(2)}, u32[]{:S(2)}) collective-permute-start(bf16[80,512]{1,0:T(8,128)(2,1)S(1)} %shard_map.109), channel_id=1, source_target_pairs={{0,6},{1,7},{2,4},{3,5},{4,2},{5,3},{6,0},{7,1},{8,14},{9,15},{10,... | collective-permute-start | bytes 245768 | tf_op jit(solution)/shard_map/ppermute | solution.py:586
  76.9 1.4 %collective-permute-start.24 = (bf16[80,512]{1,0:T(8,128)(2,1)S(1)}, bf16[80,512]{1,0:T(8,128)(2,1)S(1)}, u32[]{:S(2)}, u32[]{:S(2)}) collective-permute-start(bf16[80,512]{1,0:T(8,128)(2,1)S(1)} %shard_map.109), channel_id=1, source_target_pairs={{0,2},{1,3},{2,0},{3,1},{4,6},{5,7},{6,4},{7,5},{8,10},{9,11},{10,... | collective-permute-start | bytes 245768 | tf_op jit(solution)/shard_map/ppermute | solution.py:586
  78.3 2.6 %collective-permute-done.26 = bf16[80,512]{1,0:T(8,128)(2,1)S(1)} collective-permute-done((bf16[80,512]{1,0:T(8,128)(2,1)S(1)}, bf16[80,512]{1,0:T(8,128)(2,1)S(1)}, u32[]{:S(2)}, u32[]{:S(2)}) %collective-permute-start.26) | collective-permute-done | bytes 81952 | tf_op jit(solution)/shard_map/ppermute | solution.py:586
  80.9 2.4 %collective-permute-done.25 = bf16[80,512]{1,0:T(8,128)(2,1)S(1)} collective-permute-done((bf16[80,512]{1,0:T(8,128)(2,1)S(1)}, bf16[80,512]{1,0:T(8,128)(2,1)S(1)}, u32[]{:S(2)}, u32[]{:S(2)}) %collective-permute-start.25) | collective-permute-done | bytes 81952 | tf_op jit(solution)/shard_map/ppermute | solution.py:586
  83.3 1.5 %collective-permute-start.29 = (bf16[320,512]{1,0:T(8,128)(2,1)S(1)}, bf16[320,512]{1,0:T(8,128)(2,1)S(1)}, u32[]{:S(2)}, u32[]{:S(2)}) collective-permute-start(bf16[320,512]{1,0:T(8,128)(2,1)S(1)} %pad_maximum_fusion.refs_0_), channel_id=1, source_target_pairs={{0,24},{8,16},{16,8},{24,0},{1,25},{9,17},{17,9},{25,1},{2,26},{10... | collective-permute-start | bytes 983048 | tf_op jit(solution)/shard_map/ppermute | solution.py:586
  84.8 1.5 %collective-permute-start.28 = (bf16[320,512]{1,0:T(8,128)(2,1)S(1)}, bf16[320,512]{1,0:T(8,128)(2,1)S(1)}, u32[]{:S(2)}, u32[]{:S(2)}) collective-permute-start(bf16[320,512]{1,0:T(8,128)(2,1)S(1)} %pad_maximum_fusion.refs_0_), channel_id=1, source_target_pairs={{0,16},{8,24},{16,0},{24,8},{1,17},{9,25},{17,1},{25,9},{2,18},{10... | collective-permute-start | bytes 983048 | tf_op jit(solution)/shard_map/ppermute | solution.py:586
  86.9 8.0 %collective-permute-done.29.refs_3_ = bf16[320,512]{1,0:T(8,128)(2,1)S(1)} collective-permute-done((bf16[320,512]{1,0:T(8,128)(2,1)S(1)}, bf16[320,512]{1,0:T(8,128)(2,1)S(1)}, u32[]{:S(2)}, u32[]{:S(2)}) %collective-permute-start.29) | collective-permute-done | bytes 327712 | tf_op jit(solution)/shard_map/ppermute | solution.py:586
  94.9 4.7 %collective-permute-done.28.refs_2_ = bf16[320,512]{1,0:T(8,128)(2,1)S(1)} collective-permute-done((bf16[320,512]{1,0:T(8,128)(2,1)S(1)}, bf16[320,512]{1,0:T(8,128)(2,1)S(1)}, u32[]{:S(2)}, u32[]{:S(2)}) %collective-permute-start.28) | collective-permute-done | bytes 327712 | tf_op jit(solution)/shard_map/ppermute | solution.py:586
  100.0 1.1 %collective-permute-done.32.refs_6_ = bf16[320,512]{1,0:T(8,128)(2,1)S(1)} collective-permute-done((bf16[320,512]{1,0:T(8,128)(2,1)S(1)}, bf16[320,512]{1,0:T(8,128)(2,1)S(1)}, u32[]{:S(2)}, u32[]{:S(2)}) %collective-permute-start.32) | collective-permute-done | bytes 327712 | tf_op jit(solution)/shard_map/ppermute | solution.py:586
  101.6 3.0 %shard_map.110 = (f32[256,128]{1,0:T(8,128)}, f32[2048,512]{1,0:T(8,128)}, f32[512,128]{1,0:T(8,128)}) custom-call(bf16[320,512]{1,0:T(8,128)(2,1)S(1)} %pad_maximum_fusion.refs_0_, bf16[320,512]{1,0:T(8,128)(2,1)S(1)} %collective-permute-done.27.refs_1_, bf16[320,512]{1,0:T(8,128)(2,1)S(1)} %collective-permute-done.28.refs_2_, ...), custom_call_target="tpu_custom_call" | custom-call | flops 1000000 | bytes 8000000 | tf_op jit(solution)/shard_map/pallas_call | solution.py:570
  (76 shorter events, 14.3 us)
Async XLA Ops:
  11.8 8.9 %collective-permute-start.5 = (bf16[128,128]{1,0:T(8,128)(2,1)}, bf16[128,128]{1,0:T(8,128)(2,1)S(1)}, u32[]{:S(2)}, u32[]{:S(2)}) collective-permute-start(bf16[128,128]{1,0:T(8,128)(2,1)} %get-tuple-element.42.refs_0_), channel_id=1, source_target_pairs={{0,6},{1,7},{2,4},{3,5},{4,2},{5,3},{6,0},{7,1},{8,14},{9,15},{10,... | collective-permute-start | bytes 98312 | tf_op jit(solution)/shard_map/ppermute | solution.py:586
  16.9 5.0 %collective-permute-start.4 = (bf16[128,128]{1,0:T(8,128)(2,1)}, bf16[128,128]{1,0:T(8,128)(2,1)S(1)}, u32[]{:S(2)}, u32[]{:S(2)}) collective-permute-start(bf16[128,128]{1,0:T(8,128)(2,1)} %get-tuple-element.42.refs_0_), channel_id=1, source_target_pairs={{0,4},{1,5},{2,6},{3,7},{4,0},{5,1},{6,2},{7,3},{8,12},{9,13},{10,... | collective-permute-start | bytes 98312 | tf_op jit(solution)/shard_map/ppermute | solution.py:586
  16.9 5.0 %collective-permute-start.3 = (bf16[128,128]{1,0:T(8,128)(2,1)}, bf16[128,128]{1,0:T(8,128)(2,1)S(1)}, u32[]{:S(2)}, u32[]{:S(2)}) collective-permute-start(bf16[128,128]{1,0:T(8,128)(2,1)} %get-tuple-element.42.refs_0_), channel_id=1, source_target_pairs={{0,2},{1,3},{2,0},{3,1},{4,6},{5,7},{6,4},{7,5},{8,10},{9,11},{10,... | collective-permute-start | bytes 98312 | tf_op jit(solution)/shard_map/ppermute | solution.py:586
  17.6 5.0 %collective-permute-start.2 = (bf16[128,128]{1,0:T(8,128)(2,1)}, bf16[128,128]{1,0:T(8,128)(2,1)S(1)}, u32[]{:S(2)}, u32[]{:S(2)}) collective-permute-start(bf16[128,128]{1,0:T(8,128)(2,1)} %get-tuple-element.42.refs_0_), channel_id=1, source_target_pairs={{0,24},{8,16},{16,8},{24,0},{1,25},{9,17},{17,9},{25,1},{2,26},{10... | collective-permute-start | bytes 98312 | tf_op jit(solution)/shard_map/ppermute | solution.py:586
  20.2 4.1 %collective-permute-start.1 = (bf16[128,128]{1,0:T(8,128)(2,1)}, bf16[128,128]{1,0:T(8,128)(2,1)S(1)}, u32[]{:S(2)}, u32[]{:S(2)}) collective-permute-start(bf16[128,128]{1,0:T(8,128)(2,1)} %get-tuple-element.42.refs_0_), channel_id=1, source_target_pairs={{0,16},{8,24},{16,0},{24,8},{1,17},{9,25},{17,1},{25,9},{2,18},{10... | collective-permute-start | bytes 98312 | tf_op jit(solution)/shard_map/ppermute | solution.py:586
  20.7 4.1 %collective-permute-start = (bf16[128,128]{1,0:T(8,128)(2,1)}, bf16[128,128]{1,0:T(8,128)(2,1)S(1)}, u32[]{:S(2)}, u32[]{:S(2)}) collective-permute-start(bf16[128,128]{1,0:T(8,128)(2,1)} %get-tuple-element.42.refs_0_), channel_id=1, source_target_pairs={{0,8},{8,0},{16,24},{24,16},{1,9},{9,1},{17,25},{25,17},{2,10},{10... | collective-permute-start | bytes 98312 | tf_op jit(solution)/shard_map/ppermute | solution.py:586
  28.4 7.1 %collective-permute-start.15 = (f32[8,128]{1,0:T(8,128)S(1)}, f32[8,128]{1,0:T(8,128)S(1)}, u32[]{:S(2)}, u32[]{:S(2)}) collective-permute-start(f32[8,128]{1,0:T(8,128)S(1)} %get-tuple-element.57.refs_4_), channel_id=1, source_target_pairs={{0,24},{8,16},{16,8},{24,0},{1,25},{9,17},{17,9},{25,1},{2,26},{10... | collective-permute-start | bytes 12296 | tf_op jit(solution)/shard_map/ppermute | solution.py:586
  29.9 6.4 %collective-permute-start.14 = (f32[8,128]{1,0:T(8,128)S(1)}, f32[8,128]{1,0:T(8,128)S(1)}, u32[]{:S(2)}, u32[]{:S(2)}) collective-permute-start(f32[8,128]{1,0:T(8,128)S(1)} %get-tuple-element.57.refs_4_), channel_id=1, source_target_pairs={{0,16},{8,24},{16,0},{24,8},{1,17},{9,25},{17,1},{25,9},{2,18},{10... | collective-permute-start | bytes 12296 | tf_op jit(solution)/shard_map/ppermute | solution.py:586
  30.3 6.4 %collective-permute-start.13 = (f32[8,128]{1,0:T(8,128)S(1)}, f32[8,128]{1,0:T(8,128)S(1)}, u32[]{:S(2)}, u32[]{:S(2)}) collective-permute-start(f32[8,128]{1,0:T(8,128)S(1)} %get-tuple-element.57.refs_4_), channel_id=1, source_target_pairs={{0,8},{8,0},{16,24},{24,16},{1,9},{9,1},{17,25},{25,17},{2,10},{10... | collective-permute-start | bytes 12296 | tf_op jit(solution)/shard_map/ppermute | solution.py:586
  31.9 6.5 %collective-permute-start.12 = (f32[8,128]{1,0:T(8,128)S(1)}, f32[8,128]{1,0:T(8,128)S(1)}, u32[]{:S(2)}, u32[]{:S(2)}) collective-permute-start(f32[8,128]{1,0:T(8,128)S(1)} %get-tuple-element.57.refs_4_), channel_id=1, source_target_pairs={{0,6},{1,7},{2,4},{3,5},{4,2},{5,3},{6,0},{7,1},{8,14},{9,15},{10,... | collective-permute-start | bytes 12296 | tf_op jit(solution)/shard_map/ppermute | solution.py:586
  35.5 4.5 %collective-permute-start.11 = (f32[8,128]{1,0:T(8,128)S(1)}, f32[8,128]{1,0:T(8,128)S(1)}, u32[]{:S(2)}, u32[]{:S(2)}) collective-permute-start(f32[8,128]{1,0:T(8,128)S(1)} %get-tuple-element.57.refs_4_), channel_id=1, source_target_pairs={{0,4},{1,5},{2,6},{3,7},{4,0},{5,1},{6,2},{7,3},{8,12},{9,13},{10,... | collective-permute-start | bytes 12296 | tf_op jit(solution)/shard_map/ppermute | solution.py:586
  35.5 4.5 %collective-permute-start.10 = (f32[8,128]{1,0:T(8,128)S(1)}, f32[8,128]{1,0:T(8,128)S(1)}, u32[]{:S(2)}, u32[]{:S(2)}) collective-permute-start(f32[8,128]{1,0:T(8,128)S(1)} %get-tuple-element.57.refs_4_), channel_id=1, source_target_pairs={{0,2},{1,3},{2,0},{3,1},{4,6},{5,7},{6,4},{7,5},{8,10},{9,11},{10,... | collective-permute-start | bytes 12296 | tf_op jit(solution)/shard_map/ppermute | solution.py:586
  36.3 23.2 %collective-permute-start.7 = (bf16[128,1152]{1,0:T(8,128)(2,1)}, bf16[128,1152]{1,0:T(8,128)(2,1)S(1)}, u32[]{:S(2)}, u32[]{:S(2)}) collective-permute-start(bf16[128,1152]{1,0:T(8,128)(2,1)} %get-tuple-element.54), channel_id=1, source_target_pairs={{0,8},{8,0},{16,24},{24,16},{1,9},{9,1},{17,25},{25,17},{2,10},{10... | collective-permute-start | bytes 884744 | tf_op jit(solution)/shard_map/ppermute | solution.py:586
  36.7 22.8 %collective-permute-start.8 = (bf16[128,1152]{1,0:T(8,128)(2,1)}, bf16[128,1152]{1,0:T(8,128)(2,1)S(1)}, u32[]{:S(2)}, u32[]{:S(2)}) collective-permute-start(bf16[128,1152]{1,0:T(8,128)(2,1)} %get-tuple-element.55), channel_id=1, source_target_pairs={{0,16},{8,24},{16,0},{24,8},{1,17},{9,25},{17,1},{25,9},{2,18},{10... | collective-permute-start | bytes 884744 | tf_op jit(solution)/shard_map/ppermute | solution.py:586
  38.4 21.1 %collective-permute-start.9 = (bf16[128,1152]{1,0:T(8,128)(2,1)}, bf16[128,1152]{1,0:T(8,128)(2,1)S(1)}, u32[]{:S(2)}, u32[]{:S(2)}) collective-permute-start(bf16[128,1152]{1,0:T(8,128)(2,1)} %get-tuple-element.56), channel_id=1, source_target_pairs={{0,24},{8,16},{16,8},{24,0},{1,25},{9,17},{17,9},{25,1},{2,26},{10... | collective-permute-start | bytes 884744 | tf_op jit(solution)/shard_map/ppermute | solution.py:586
  44.5 7.5 %collective-permute-start.19 = (bf16[128,128]{1,0:T(8,128)(2,1)S(1)}, bf16[128,128]{1,0:T(8,128)(2,1)S(1)}, u32[]{:S(2)}, u32[]{:S(2)}) collective-permute-start(bf16[128,128]{1,0:T(8,128)(2,1)S(1)} %shard_map.105.raw_ref.refs_4_), channel_id=1, source_target_pairs={{0,24},{8,16},{16,8},{24,0},{1,25},{9,17},{17,9},{25,1},{2,26},{10... | collective-permute-start | bytes 98312 | tf_op jit(solution)/shard_map/ppermute | solution.py:586
  46.1 13.4 %collective-permute-start.18 = (bf16[128,128]{1,0:T(8,128)(2,1)S(1)}, bf16[128,128]{1,0:T(8,128)(2,1)S(1)}, u32[]{:S(2)}, u32[]{:S(2)}) collective-permute-start(bf16[128,128]{1,0:T(8,128)(2,1)S(1)} %shard_map.105.raw_ref.refs_4_), channel_id=1, source_target_pairs={{0,16},{8,24},{16,0},{24,8},{1,17},{9,25},{17,1},{25,9},{2,18},{10... | collective-permute-start | bytes 98312 | tf_op jit(solution)/shard_map/ppermute | solution.py:586
  52.1 7.4 %collective-permute-start.17 = (bf16[128,128]{1,0:T(8,128)(2,1)S(1)}, bf16[128,128]{1,0:T(8,128)(2,1)S(1)}, u32[]{:S(2)}, u32[]{:S(2)}) collective-permute-start(bf16[128,128]{1,0:T(8,128)(2,1)S(1)} %shard_map.105.raw_ref.refs_4_), channel_id=1, source_target_pairs={{0,8},{8,0},{16,24},{24,16},{1,9},{9,1},{17,25},{25,17},{2,10},{10... | collective-permute-start | bytes 98312 | tf_op jit(solution)/shard_map/ppermute | solution.py:586
  61.0 1.7 %collective-permute-start.20 = (bf16[4,80,512]{2,1,0:T(8,128)(2,1)S(1)}, bf16[4,80,512]{2,1,0:T(8,128)(2,1)S(1)}, u32[]{:S(2)}, u32[]{:S(2)}) collective-permute-start(bf16[4,80,512]{2,1,0:T(8,128)(2,1)S(1)} %get-tuple-element.72), channel_id=1, source_target_pairs={{0,1},{1,0},{2,3},{3,2},{4,5},{5,4},{6,7},{7,6},{8,9},{9,8},{10,11... | collective-permute-start | bytes 983048 | tf_op jit(solution)/shard_map/ppermute | solution.py:586
  62.8 4.6 %collective-permute-start.21 = (bf16[80,512]{1,0:T(8,128)(2,1)S(1)}, bf16[80,512]{1,0:T(8,128)(2,1)S(1)}, u32[]{:S(2)}, u32[]{:S(2)}) collective-permute-start(bf16[80,512]{1,0:T(8,128)(2,1)S(1)} %get-tuple-element.74), channel_id=1, source_target_pairs={{0,2},{1,3},{2,0},{3,1},{4,6},{5,7},{6,4},{7,5},{8,10},{9,11},{10,... | collective-permute-start | bytes 245768 | tf_op jit(solution)/shard_map/ppermute | solution.py:586
  64.3 9.5 %collective-permute-start.22 = (bf16[80,512]{1,0:T(8,128)(2,1)S(1)}, bf16[80,512]{1,0:T(8,128)(2,1)S(1)}, u32[]{:S(2)}, u32[]{:S(2)}) collective-permute-start(bf16[80,512]{1,0:T(8,128)(2,1)S(1)} %get-tuple-element.75), channel_id=1, source_target_pairs={{0,4},{1,5},{2,6},{3,7},{4,0},{5,1},{6,2},{7,3},{8,12},{9,13},{10,... | collective-permute-start | bytes 245768 | tf_op jit(solution)/shard_map/ppermute | solution.py:586
  67.0 6.8 %collective-permute-start.23 = (bf16[80,512]{1,0:T(8,128)(2,1)S(1)}, bf16[80,512]{1,0:T(8,128)(2,1)S(1)}, u32[]{:S(2)}, u32[]{:S(2)}) collective-permute-start(bf16[80,512]{1,0:T(8,128)(2,1)S(1)} %get-tuple-element.76), channel_id=1, source_target_pairs={{0,6},{1,7},{2,4},{3,5},{4,2},{5,3},{6,0},{7,1},{8,14},{9,15},{10,... | collective-permute-start | bytes 245768 | tf_op jit(solution)/shard_map/ppermute | solution.py:586
  73.8 7.1 %collective-permute-start.26 = (bf16[80,512]{1,0:T(8,128)(2,1)S(1)}, bf16[80,512]{1,0:T(8,128)(2,1)S(1)}, u32[]{:S(2)}, u32[]{:S(2)}) collective-permute-start(bf16[80,512]{1,0:T(8,128)(2,1)S(1)} %shard_map.109), channel_id=1, source_target_pairs={{0,6},{1,7},{2,4},{3,5},{4,2},{5,3},{6,0},{7,1},{8,14},{9,15},{10,... | collective-permute-start | bytes 245768 | tf_op jit(solution)/shard_map/ppermute | solution.py:586
  76.4 6.9 %collective-permute-start.25 = (bf16[80,512]{1,0:T(8,128)(2,1)S(1)}, bf16[80,512]{1,0:T(8,128)(2,1)S(1)}, u32[]{:S(2)}, u32[]{:S(2)}) collective-permute-start(bf16[80,512]{1,0:T(8,128)(2,1)S(1)} %shard_map.109), channel_id=1, source_target_pairs={{0,4},{1,5},{2,6},{3,7},{4,0},{5,1},{6,2},{7,3},{8,12},{9,13},{10,... | collective-permute-start | bytes 245768 | tf_op jit(solution)/shard_map/ppermute | solution.py:586
  76.9 6.4 %collective-permute-start.24 = (bf16[80,512]{1,0:T(8,128)(2,1)S(1)}, bf16[80,512]{1,0:T(8,128)(2,1)S(1)}, u32[]{:S(2)}, u32[]{:S(2)}) collective-permute-start(bf16[80,512]{1,0:T(8,128)(2,1)S(1)} %shard_map.109), channel_id=1, source_target_pairs={{0,2},{1,3},{2,0},{3,1},{4,6},{5,7},{6,4},{7,5},{8,10},{9,11},{10,... | collective-permute-start | bytes 245768 | tf_op jit(solution)/shard_map/ppermute | solution.py:586
  83.3 11.5 %collective-permute-start.29 = (bf16[320,512]{1,0:T(8,128)(2,1)S(1)}, bf16[320,512]{1,0:T(8,128)(2,1)S(1)}, u32[]{:S(2)}, u32[]{:S(2)}) collective-permute-start(bf16[320,512]{1,0:T(8,128)(2,1)S(1)} %pad_maximum_fusion.refs_0_), channel_id=1, source_target_pairs={{0,24},{8,16},{16,8},{24,0},{1,25},{9,17},{17,9},{25,1},{2,26},{10... | collective-permute-start | bytes 983048 | tf_op jit(solution)/shard_map/ppermute | solution.py:586
  84.8 14.7 %collective-permute-start.28 = (bf16[320,512]{1,0:T(8,128)(2,1)S(1)}, bf16[320,512]{1,0:T(8,128)(2,1)S(1)}, u32[]{:S(2)}, u32[]{:S(2)}) collective-permute-start(bf16[320,512]{1,0:T(8,128)(2,1)S(1)} %pad_maximum_fusion.refs_0_), channel_id=1, source_target_pairs={{0,16},{8,24},{16,0},{24,8},{1,17},{9,25},{17,1},{25,9},{2,18},{10... | collective-permute-start | bytes 983048 | tf_op jit(solution)/shard_map/ppermute | solution.py:586
  86.3 13.2 %collective-permute-start.27 = (bf16[320,512]{1,0:T(8,128)(2,1)S(1)}, bf16[320,512]{1,0:T(8,128)(2,1)S(1)}, u32[]{:S(2)}, u32[]{:S(2)}) collective-permute-start(bf16[320,512]{1,0:T(8,128)(2,1)S(1)} %pad_maximum_fusion.refs_0_), channel_id=1, source_target_pairs={{0,8},{8,0},{16,24},{24,16},{1,9},{9,1},{17,25},{25,17},{2,10},{10... | collective-permute-start | bytes 983048 | tf_op jit(solution)/shard_map/ppermute | solution.py:586
  86.9 13.2 %collective-permute-start.30 = (bf16[320,512]{1,0:T(8,128)(2,1)S(1)}, bf16[320,512]{1,0:T(8,128)(2,1)S(1)}, u32[]{:S(2)}, u32[]{:S(2)}) collective-permute-start(bf16[320,512]{1,0:T(8,128)(2,1)S(1)} %pad_maximum_fusion.refs_0_), channel_id=1, source_target_pairs={{0,1},{1,0},{2,3},{3,2},{4,5},{5,4},{6,7},{7,6},{8,9},{9,8},{10,11... | collective-permute-start | bytes 983048 | tf_op jit(solution)/shard_map/ppermute | solution.py:586
  94.9 5.2 %collective-permute-start.33 = (bf16[320,512]{1,0:T(8,128)(2,1)S(1)}, bf16[320,512]{1,0:T(8,128)(2,1)S(1)}, u32[]{:S(2)}, u32[]{:S(2)}) collective-permute-start(bf16[320,512]{1,0:T(8,128)(2,1)S(1)} %collective-permute-done.29.refs_3_), channel_id=1, source_target_pairs={{0,1},{1,0},{2,3},{3,2},{4,5},{5,4},{6,7},{7,6},{8,9},{9,8},{10,11... | collective-permute-start | bytes 983048 | tf_op jit(solution)/shard_map/ppermute | solution.py:586
  99.5 1.6 %collective-permute-start.32 = (bf16[320,512]{1,0:T(8,128)(2,1)S(1)}, bf16[320,512]{1,0:T(8,128)(2,1)S(1)}, u32[]{:S(2)}, u32[]{:S(2)}) collective-permute-start(bf16[320,512]{1,0:T(8,128)(2,1)S(1)} %collective-permute-done.28.refs_2_), channel_id=1, source_target_pairs={{0,1},{1,0},{2,3},{3,2},{4,5},{5,4},{6,7},{7,6},{8,9},{9,8},{10,11... | collective-permute-start | bytes 983048 | tf_op jit(solution)/shard_map/ppermute | solution.py:586
  99.5 2.1 %collective-permute-start.31 = (bf16[320,512]{1,0:T(8,128)(2,1)S(1)}, bf16[320,512]{1,0:T(8,128)(2,1)S(1)}, u32[]{:S(2)}, u32[]{:S(2)}) collective-permute-start(bf16[320,512]{1,0:T(8,128)(2,1)S(1)} %collective-permute-done.27.refs_1_), channel_id=1, source_target_pairs={{0,1},{1,0},{2,3},{3,2},{4,5},{5,4},{6,7},{7,6},{8,9},{9,8},{10,11... | collective-permute-start | bytes 983048 | tf_op jit(solution)/shard_map/ppermute | solution.py:586
  (15 other events, 237.2 us)
